TPU v7x, 32 devices: a whole 2x2x4 slice. The times are simulated.
32 devices in a mesh: dp: 8 (over z, y), tensor: 4 (over x, core).
Axes of the slice: x: 2, y: 2, z: 4, core: 2. Of those that a mesh axis runs over, the one named last changes fastest.
Arguments:
- patches: bfloat16 [64, 196, 768], P('dp'), may hold values from -6 to 6
- cotangent: bfloat16 [64, 196, 768], P('dp'), may hold values from -6 to 6
- mask_rank: int32 [64, 196], P('dp'), may hold values from 0 to 195, each once within a row
- mask_count: int32 [64], P('dp'), may hold values from 78 to 156
- image_count: int32 [8], P('dp'), may hold values from 1 to 8, as said below
- entry_weight: float32 [3, 768, 768], P(None, 'dp', 'tensor'), may hold values from -0.21875 to 0.21875
- entry_moment: float32 [3, 768, 768], P(None, 'dp', 'tensor'), may hold values from -20 to 20
- entry_second: float32 [3, 768, 768], P(None, 'dp', 'tensor'), may hold values from 0.426496 to 6.77376
- entry_bias: float32 [2, 4, 192], P(None, 'tensor', 'dp'), may hold values from -4 to 4
- entry_bias_moment: float32 [2, 4, 192], P(None, 'tensor', 'dp'), may hold values from -20 to 20
- entry_bias_second: float32 [2, 4, 192], P(None, 'tensor', 'dp'), may hold values from 0.426496 to 6.77376
- exit_weight: float32 [768, 768], P('tensor', 'dp'), may hold values from -0.625 to 0.625
- exit_moment: float32 [768, 768], P('tensor', 'dp'), may hold values from -20 to 20
- exit_second: float32 [768, 768], P('tensor', 'dp'), may hold values from 0.426496 to 6.77376
- expand_weight: float32 [768, 3072], P('dp', 'tensor'), may hold values from -0.21875 to 0.21875
- expand_moment: float32 [768, 3072], P('dp', 'tensor'), may hold values from -20 to 20
- expand_second: float32 [768, 3072], P('dp', 'tensor'), may hold values from 0.426496 to 6.77376
- expand_bias: float32 [4, 768], P('tensor', 'dp'), may hold values from -4 to 4
- expand_bias_moment: float32 [4, 768], P('tensor', 'dp'), may hold values from -20 to 20
- expand_bias_second: float32 [4, 768], P('tensor', 'dp'), may hold values from 0.426496 to 6.77376
- reduce_weight: float32 [3072, 768], P('tensor', 'dp'), may hold values from -0.109375 to 0.109375
- reduce_moment: float32 [3072, 768], P('tensor', 'dp'), may hold values from -20 to 20
- reduce_second: float32 [3072, 768], P('tensor', 'dp'), may hold values from 0.426496 to 6.77376
- vectors: float32 [7, 768], P(None, 'dp'), may hold values from -6 to 6, as said below
- vectors_moment: float32 [7, 768], P(None, 'dp'), may hold values from -64 to 64
- vectors_second: float32 [7, 768], P(None, 'dp'), may hold values from 4.704 to 75.264
- position: float32 [196, 768], P(None, 'dp'), may hold values from -4 to 4
- position_moment: float32 [196, 768], P(None, 'dp'), may hold values from -4 to 4
- position_second: float32 [196, 768], P(None, 'dp'), may hold values from 0.064 to 0.512
Outputs:
- block_out: bfloat16 [64, 196, 768], P('dp')
- patch_grad: bfloat16 [64, 196, 768], P('dp')
- entry_new: float32 [3, 768, 768], P(None, 'dp', 'tensor')
- entry_moment_new: float32 [3, 768, 768], P(None, 'dp', 'tensor')
- entry_second_new: float32 [3, 768, 768], P(None, 'dp', 'tensor')
- entry_copy: bfloat16 [3, 768, 768], P(None, 'dp', 'tensor')
- entry_bias_new: float32 [2, 4, 192], P(None, 'tensor', 'dp')
- entry_bias_moment_new: float32 [2, 4, 192], P(None, 'tensor', 'dp')
- entry_bias_second_new: float32 [2, 4, 192], P(None, 'tensor', 'dp')
- entry_bias_copy: bfloat16 [2, 4, 192], P(None, 'tensor', 'dp')
- exit_new: float32 [768, 768], P('tensor', 'dp')
- exit_moment_new: float32 [768, 768], P('tensor', 'dp')
- exit_second_new: float32 [768, 768], P('tensor', 'dp')
- exit_copy: bfloat16 [768, 768], P('tensor', 'dp')
- expand_new: float32 [768, 3072], P('dp', 'tensor')
- expand_moment_new: float32 [768, 3072], P('dp', 'tensor')
- expand_second_new: float32 [768, 3072], P('dp', 'tensor')
- expand_copy: bfloat16 [768, 3072], P('dp', 'tensor')
- expand_bias_new: float32 [4, 768], P('tensor', 'dp')
- expand_bias_moment_new: float32 [4, 768], P('tensor', 'dp')
- expand_bias_second_new: float32 [4, 768], P('tensor', 'dp')
- expand_bias_copy: bfloat16 [4, 768], P('tensor', 'dp')
- reduce_new: float32 [3072, 768], P('tensor', 'dp')
- reduce_moment_new: float32 [3072, 768], P('tensor', 'dp')
- reduce_second_new: float32 [3072, 768], P('tensor', 'dp')
- reduce_copy: bfloat16 [3072, 768], P('tensor', 'dp')
- vectors_new: float32 [7, 768], P(None, 'dp')
- vectors_moment_new: float32 [7, 768], P(None, 'dp')
- vectors_second_new: float32 [7, 768], P(None, 'dp')
- vectors_copy: bfloat16 [7, 768], P(None, 'dp')
- position_new: float32 [196, 768], P(None, 'dp')
- position_moment_new: float32 [196, 768], P(None, 'dp')
- position_second_new: float32 [196, 768], P(None, 'dp')
- position_copy: bfloat16 [196, 768], P(None, 'dp')
Inputs may be any that keep to these rules, and one draw needn't show every extreme that they name: `mask_rank`: each image's row is a permutation of the patch indices. `image_count`: some index of dp holds 8 live images in every draw. `vectors`: rows 0 and 2 (gains) lie in 0.4 to 1.6; rows 1, 3, 4 and 5 in -1.8 to 1.8; row 6 (the mask token) in -6 to 6.
All inputs are finite; a program needn't handle non-finite values.
Results may differ from a plain program's by a relative error of at most 0.015.
Values may be sent and summed in bfloat16 or wider, within the bound.
No kernel may reach another device: no remote copies, remote signals or barrier semaphores. Data moves between devices by JAX's collectives and lax.ppermute only.
A program may use at most 128 MiB of HBM per device.

v0:
```python
import jax
import jax.numpy as jnp
from jax import lax
from jax.sharding import PartitionSpec as P

HEAD_DIM = 64
STEP = 7


NORM_EPS = 1e-06


def norm_rows(rows, gain, shift):
    centered = rows - jnp.mean(rows, -1, keepdims=True)
    inverse = lax.rsqrt(jnp.mean(centered * centered, -1, keepdims=True) + NORM_EPS)
    scaled = centered * inverse
    return (scaled * gain + shift, scaled, inverse)


def norm_back(grad_normed, scaled, inverse, gain):
    grad_scaled = grad_normed * gain
    mean_grad = jnp.mean(grad_scaled, -1, keepdims=True)
    mean_cross = jnp.mean(grad_scaled * scaled, -1, keepdims=True)
    return inverse * (grad_scaled - mean_grad - scaled * mean_cross)


def column_dot(left, right):
    return lax.dot_general(
        left, right, (((0,), (0,)), ((), ())), preferred_element_type=jnp.float32
    )


def row_dot(left, right):
    return lax.dot_general(
        left, right, (((1,), (1,)), ((), ())), preferred_element_type=jnp.float32
    )


def exact_gelu(values):
    return jax.nn.gelu(values, approximate=False)


def adamw(master, moment, second, grad, rate, decay):
    moment = 0.9 * moment + 0.1 * grad
    second = 0.999 * second + 0.001 * grad * grad
    fixed_first = moment / (1.0 - 0.9**STEP)
    fixed_second = second / (1.0 - 0.999**STEP)
    master = master - rate * (fixed_first / (jnp.sqrt(fixed_second) + 1e-08) + decay * master)
    return (master, moment, second, master.astype(jnp.bfloat16))


def local(
    patches,
    cotangent,
    mask_rank,
    mask_count,
    image_count,
    entry_weight,
    entry_moment,
    entry_second,
    entry_bias,
    entry_bias_moment,
    entry_bias_second,
    exit_weight,
    exit_moment,
    exit_second,
    expand_weight,
    expand_moment,
    expand_second,
    expand_bias,
    expand_bias_moment,
    expand_bias_second,
    reduce_weight,
    reduce_moment,
    reduce_second,
    vectors,
    vectors_moment,
    vectors_second,
    position,
    position_moment,
    position_second,
):
    half = jnp.bfloat16
    single = jnp.float32
    gathered = (
        lax.all_gather(entry_weight.astype(half), "dp", axis=1, tiled=True),
        lax.all_gather(entry_bias.astype(half), "dp", axis=2, tiled=True),
        lax.all_gather(exit_weight.astype(half), "dp", axis=1, tiled=True),
        lax.all_gather(expand_weight.astype(half), "dp", axis=0, tiled=True),
        lax.all_gather(expand_bias.astype(half), "dp", axis=1, tiled=True),
        lax.all_gather(reduce_weight.astype(half), "dp", axis=1, tiled=True),
        lax.all_gather(vectors.astype(half), "dp", axis=1, tiled=True),
        lax.all_gather(position.astype(half), "dp", axis=1, tiled=True),
    )
    w_entry, b_entry, w_exit, w_expand, b_expand, w_reduce, table, place = gathered
    table32 = table.astype(single)
    place32 = place.astype(single)
    images, patch_count, width = patches.shape
    tokens = images * patch_count
    slots = lax.broadcasted_iota(jnp.int32, (images, patch_count, 1), 0)
    live_rows = (slots < image_count[0]).astype(single).reshape(tokens, 1)
    masked = (mask_rank < mask_count[:, None]).reshape(tokens, 1)
    substituted = jnp.where(masked, table32[6], patches.reshape(tokens, width).astype(single))
    start = (substituted.reshape(images, patch_count, width) + place32[None]).reshape(tokens, width)
    normed_one, scaled_one, inverse_one = norm_rows(start, table32[0], table32[1])
    normed_one = normed_one.astype(half)
    columns = w_entry.shape[2]
    heads = columns // HEAD_DIM
    scale = HEAD_DIM ** (-0.5)
    entry_shift = b_entry[:, 0, :].astype(single)
    zero_row = jnp.zeros((1, columns), single)
    shift_three = jnp.concatenate([entry_shift[0:1], zero_row, entry_shift[1:2]], 0)
    qkv = (
        jnp.einsum("td,jde->jte", normed_one, w_entry, preferred_element_type=single)
        + shift_three[:, None, :]
    )
    qkv = qkv.astype(half).reshape(3, images, patch_count, heads, HEAD_DIM)
    query, keys, values = (qkv[0], qkv[1], qkv[2])
    scores = jnp.einsum("iqhd,ikhd->ihqk", query, keys, preferred_element_type=single) * scale
    top = jnp.max(scores, -1, keepdims=True)
    logsum = top + jnp.log(jnp.sum(jnp.exp(scores - top), -1, keepdims=True))
    probs_low = jnp.exp(scores - logsum).astype(half)
    mixed = jnp.einsum("ihqk,ikhd->iqhd", probs_low, values, preferred_element_type=single)
    mixed = mixed.astype(half).reshape(tokens, columns)
    attn_part = jnp.dot(mixed, w_exit, preferred_element_type=single)
    branch = lax.psum(attn_part.astype(jnp.bfloat16), "tensor").astype(jnp.float32)
    middle = start + branch + table32[4]
    normed_two, scaled_two, inverse_two = norm_rows(middle, table32[2], table32[3])
    normed_two = normed_two.astype(half)
    upper = jnp.dot(normed_two, w_expand, preferred_element_type=single) + b_expand[0].astype(
        single
    )
    active, gelu_back = jax.vjp(exact_gelu, upper)
    active = active.astype(half)
    down_part = jnp.dot(active, w_reduce, preferred_element_type=single)
    total = lax.psum(down_part.astype(jnp.bfloat16), "tensor").astype(jnp.float32)
    own_out = ((middle + total + table32[5]) * live_rows).astype(half)
    grad_out = cotangent.reshape(tokens, width).astype(single) * live_rows
    grad_low = grad_out.astype(half)
    grad_active = row_dot(grad_low, w_reduce)
    grad_reduce = column_dot(active, grad_low)
    grad_upper = gelu_back(grad_active)[0].astype(half)
    grad_expand = column_dot(normed_two, grad_upper)
    grad_expand_shift = jnp.sum(grad_upper.astype(single), 0)[None, :]
    partial_two = row_dot(grad_upper, w_expand)
    grad_normed_two = lax.psum(partial_two.astype(jnp.bfloat16), "tensor").astype(jnp.float32)
    grad_middle = grad_out + norm_back(grad_normed_two, scaled_two, inverse_two, table32[2])
    grad_mid_low = grad_middle.astype(half)
    grad_exit = column_dot(mixed, grad_mid_low)
    grad_mixed = (
        row_dot(grad_mid_low, w_exit).astype(half).reshape(images, patch_count, heads, HEAD_DIM)
    )
    scores = jnp.einsum("iqhd,ikhd->ihqk", query, keys, preferred_element_type=single) * scale
    probs = jnp.exp(scores - logsum)
    probs_low = probs.astype(half)
    grad_values = jnp.einsum(
        "ihqk,iqhd->ikhd", probs_low, grad_mixed, preferred_element_type=single
    ).astype(half)
    grad_probs = jnp.einsum("iqhd,ikhd->ihqk", grad_mixed, values, preferred_element_type=single)
    grad_scores = (probs * (grad_probs - jnp.sum(probs * grad_probs, -1, keepdims=True))).astype(
        half
    )
    grad_query = (
        jnp.einsum("ihqk,ikhd->iqhd", grad_scores, keys, preferred_element_type=single) * scale
    ).astype(half)
    grad_keys = (
        jnp.einsum("ihqk,iqhd->ikhd", grad_scores, query, preferred_element_type=single) * scale
    ).astype(half)
    grad_qkv = jnp.stack([grad_query, grad_keys, grad_values]).reshape(3, tokens, columns)
    grad_entry = jnp.einsum("td,jte->jde", normed_one, grad_qkv, preferred_element_type=single)
    column_sums = jnp.sum(grad_qkv.astype(single), 1)
    grad_entry_shift = jnp.stack([column_sums[0], column_sums[2]])[:, None, :]
    partial_one = jnp.einsum("jte,jde->td", grad_qkv, w_entry, preferred_element_type=single)
    grad_normed_one = lax.psum(partial_one.astype(jnp.bfloat16), "tensor").astype(jnp.float32)
    grad_start = grad_middle + norm_back(grad_normed_one, scaled_one, inverse_one, table32[0])
    grad_token = jnp.sum(jnp.where(masked, grad_start, 0.0), 0)
    grad_part = jnp.where(masked, 0.0, grad_start).astype(half)
    grad_table = jnp.stack(
        [
            jnp.sum(grad_normed_one * scaled_one, 0),
            jnp.sum(grad_normed_one, 0),
            jnp.sum(grad_normed_two * scaled_two, 0),
            jnp.sum(grad_normed_two, 0),
            jnp.sum(grad_middle, 0),
            jnp.sum(grad_out, 0),
            grad_token,
        ]
    )
    grad_place = jnp.sum(grad_start.reshape(images, patch_count, width), 0)
    block_out = own_out.reshape(images, patch_count, width)
    patch_grad = grad_part.reshape(images, patch_count, width)
    summed = (
        lax.psum_scatter(grad_entry, "dp", scatter_dimension=1, tiled=True),
        lax.psum_scatter(grad_entry_shift, "dp", scatter_dimension=2, tiled=True),
        lax.psum_scatter(grad_exit, "dp", scatter_dimension=1, tiled=True),
        lax.psum_scatter(grad_expand, "dp", scatter_dimension=0, tiled=True),
        lax.psum_scatter(grad_expand_shift, "dp", scatter_dimension=1, tiled=True),
        lax.psum_scatter(grad_reduce, "dp", scatter_dimension=1, tiled=True),
        lax.psum_scatter(grad_table, "dp", scatter_dimension=1, tiled=True),
        lax.psum_scatter(grad_place, "dp", scatter_dimension=1, tiled=True),
    )
    entry = adamw(entry_weight, entry_moment, entry_second, summed[0], 0.05, 0.05)
    entry_b = adamw(entry_bias, entry_bias_moment, entry_bias_second, summed[1], 0.3, 0.0)
    exits = adamw(exit_weight, exit_moment, exit_second, summed[2], 0.05, 0.05)
    expand = adamw(expand_weight, expand_moment, expand_second, summed[3], 0.05, 0.05)
    expand_b = adamw(expand_bias, expand_bias_moment, expand_bias_second, summed[4], 0.3, 0.0)
    reduce_w = adamw(reduce_weight, reduce_moment, reduce_second, summed[5], 0.05, 0.05)
    table_new = adamw(vectors, vectors_moment, vectors_second, summed[6], 0.3, 0.0)
    place_new = adamw(position, position_moment, position_second, summed[7], 0.1, 0.0)
    return (
        block_out,
        patch_grad,
        entry[0],
        entry[1],
        entry[2],
        entry[3],
        entry_b[0],
        entry_b[1],
        entry_b[2],
        entry_b[3],
        exits[0],
        exits[1],
        exits[2],
        exits[3],
        expand[0],
        expand[1],
        expand[2],
        expand[3],
        expand_b[0],
        expand_b[1],
        expand_b[2],
        expand_b[3],
        reduce_w[0],
        reduce_w[1],
        reduce_w[2],
        reduce_w[3],
        table_new[0],
        table_new[1],
        table_new[2],
        table_new[3],
        place_new[0],
        place_new[1],
        place_new[2],
        place_new[3],
    )


def solution(mesh):
    placed = (
        P("dp", None, None),
        P("dp", None, None),
        P("dp", None),
        P("dp"),
        P("dp"),
        P(None, "dp", "tensor"),
        P(None, "dp", "tensor"),
        P(None, "dp", "tensor"),
        P(None, "tensor", "dp"),
        P(None, "tensor", "dp"),
        P(None, "tensor", "dp"),
        P("tensor", "dp"),
        P("tensor", "dp"),
        P("tensor", "dp"),
        P("dp", "tensor"),
        P("dp", "tensor"),
        P("dp", "tensor"),
        P("tensor", "dp"),
        P("tensor", "dp"),
        P("tensor", "dp"),
        P("tensor", "dp"),
        P("tensor", "dp"),
        P("tensor", "dp"),
        P(None, "dp"),
        P(None, "dp"),
        P(None, "dp"),
        P(None, "dp"),
        P(None, "dp"),
        P(None, "dp"),
    )
    return jax.shard_map(
        local,
        mesh=mesh,
        in_specs=placed,
        out_specs=(
            P("dp", None, None),
            P("dp", None, None),
            P(None, "dp", "tensor"),
            P(None, "dp", "tensor"),
            P(None, "dp", "tensor"),
            P(None, "dp", "tensor"),
            P(None, "tensor", "dp"),
            P(None, "tensor", "dp"),
            P(None, "tensor", "dp"),
            P(None, "tensor", "dp"),
            P("tensor", "dp"),
            P("tensor", "dp"),
            P("tensor", "dp"),
            P("tensor", "dp"),
            P("dp", "tensor"),
            P("dp", "tensor"),
            P("dp", "tensor"),
            P("dp", "tensor"),
            P("tensor", "dp"),
            P("tensor", "dp"),
            P("tensor", "dp"),
            P("tensor", "dp"),
            P("tensor", "dp"),
            P("tensor", "dp"),
            P("tensor", "dp"),
            P("tensor", "dp"),
            P(None, "dp"),
            P(None, "dp"),
            P(None, "dp"),
            P(None, "dp"),
            P(None, "dp"),
            P(None, "dp"),
            P(None, "dp"),
            P(None, "dp"),
        ),
        check_vma=False,
    )
```

profile of v0, /device:TPU:0, one launch (start us, length us, event | category | flops | bytes accessed | tf_op | source)
XLA Modules:
  0.0 940.3 jit_solution(10742835543429647552)
XLA Ops:
  8.9 27.9 %all-gather = bf16[8,96,7]{1,2,0:T(8,128)(2,1)S(1)} all-gather(bf16[1,96,7]{1,2,0:T(8,128)(2,1)S(1)} %convert_bitcast_fusion), channel_id=1, replica_groups=mesh['dp'=8,'tensor'=4] {'dp'}, dimensions={0}, use_global_device_ids=true | all-gather | bytes 12096 | tf_op jit(solution)/shard_map/all_gather | solution.py:92
  38.5 31.0 %all_gather.25 = bf16[196,768]{0,1:T(8,128)(2,1)S(1)} all-gather(bf16[196,96]{0,1:T(8,128)(2,1)S(1)} %convert_element_type.185), channel_id=1, replica_groups=mesh['dp'=8,'tensor'=4] {'dp'}, dimensions={1}, use_global_device_ids=true | all-gather | bytes 338688 | tf_op jit(solution)/shard_map/all_gather | solution.py:93
  80.1 5.3 reshape.210
  85.7 35.5 %all_gather.26 = bf16[3,768,192]{2,0,1:T(4,128)(2,1)S(1)} all-gather(bf16[3,96,192]{2,0,1:T(4,128)(2,1)S(1)} %copy.324), channel_id=1, replica_groups=mesh['dp'=8,'tensor'=4] {'dp'}, dimensions={1}, use_global_device_ids=true | all-gather | bytes 995328 | tf_op jit(solution)/shard_map/all_gather | solution.py:86
  122.2 30.8 %all_gather.27 = bf16[2,1,192]{1,0,2:T(2,128)(2,1)S(1)} all-gather(bf16[2,1,24]{1,0,2:T(2,128)(2,1)S(1)} %copy.327), channel_id=1, replica_groups=mesh['dp'=8,'tensor'=4] {'dp'}, dimensions={2}, use_global_device_ids=true | all-gather | bytes 864 | tf_op jit(solution)/shard_map/all_gather | solution.py:87
  170.0 31.0 %all_gather.28 = bf16[192,768]{0,1:T(8,128)(2,1)S(1)} all-gather(bf16[192,96]{0,1:T(8,128)(2,1)S(1)} %copy.333), channel_id=1, replica_groups=mesh['dp'=8,'tensor'=4] {'dp'}, dimensions={1}, use_global_device_ids=true | all-gather | bytes 331776 | tf_op jit(solution)/shard_map/all_gather | solution.py:88
  206.6 19.9 %all-reduce = bf16[768]{0:T(1024)(128)(2,1)S(1)} all-reduce(bf16[768]{0:T(1024)(128)(2,1)S(1)} %dynamic-update-slice), channel_id=1, replica_groups=mesh['dp'=8,'tensor'=4] {'dp'}, use_global_device_ids=true, to_apply=%add | all-reduce | flops 768 | bytes 3072
  229.3 5.2 reshape.217
  235.4 23.6 %all-reduce.7.cloned.1.call-done = bf16[1568,768]{1,0:T(8,128)(2,1)} async-done(((bf16[1568,768]{1,0:T(8,128)(2,1)}), bf16[1568,768]{1,0:T(8,128)(2,1)}) %all-reduce.7.cloned.1.call-update) | async-done | bytes 2408464 | tf_op jit(solution)/shard_map/psum | solution.py:126
  267.2 15.3 %multiply_convert_fusion.2 = (bf16[1568,768]{1,0:T(8,128)(2,1)S(1)}, f32[1568,768]{1,0:T(8,128)}, f32[1568,768]{1,0:T(8,128)}) fusion(f32[768]{0:T(1024)S(1)} %add.321, bf16[1568,768]{1,0:T(8,128)(2,1)} %add_convert_fusion.1, bf16[768,768]{1,0:T(8,128)(2,1)} %all-gather.4.cloned.1.call-done), kind=kOutput, calls=%fused_computation.35 | convolution fusion | flops 1929166848 | bytes 15633408 | tf_op jit(solution)/shard_map/dot_general | solution.py:130
  283.8 6.4 fusion.58
  290.3 69.8 %reduce-scatter.21.cloned.1.call-done = f32[768,96]{0,1:T(8,128)} async-done(((f32[768,768]{0,1:T(8,128)}), f32[768,96]{0,1:T(8,128)}) %reduce-scatter.21.cloned.1.call-update) | async-done | bytes 294928 | tf_op jit(solution)/shard_map/reduce_scatter | solution.py:198
  362.6 40.6 %all-gather.6.cloned.1.call-done = bf16[768,768]{0,1:T(8,128)(2,1)} async-done(((bf16[768,96]{0,1:T(8,128)(2,1)}), bf16[768,768]{0,1:T(8,128)(2,1)}) %all-gather.6.cloned.1.call-update) | async-done | bytes 1179664 | tf_op jit(solution)/shard_map/all_gather | solution.py:91
  403.1 9.9 %convert_reduce_fusion.2 = (f32[768]{0:T(1024)}, bf16[1568,768]{1,0:T(8,128)(2,1)S(1)}) fusion(f32[1568,768]{1,0:T(8,128)} %get-tuple-element.328, bf16[768,768]{0,1:T(8,128)(2,1)} %all-gather.6.cloned.1.call-done, f32[1568,768]{1,0:T(8,128)} %reshape.217, f32[1568]{0:T(1024)S(1)} %convert_element_type.207, f32[1568,768]{1,0:T(8,128)} %get-tuple-element.343, ...), kind=kOutput, calls=%fused_computation.31 | convolution fusion | flops 1872567552 | bytes 18051200 | tf_op jit(solution)/shard_map/dot_general | solution.py:34
  418.0 5.5 convolution_convert_fusion.1
  423.5 49.6 %all-reduce.9.cloned.1.call-done = bf16[1568,768]{1,0:T(8,128)(2,1)} async-done(((bf16[1568,768]{1,0:T(8,128)(2,1)}), bf16[1568,768]{1,0:T(8,128)(2,1)}) %all-reduce.9.cloned.1.call-update) | async-done | bytes 2408464 | tf_op jit(solution)/shard_map/psum | solution.py:146
  473.1 5.9 fusion.15
  479.0 6.1 fusion.65
  492.2 4.5 multiply_reduce_fusion
  519.0 5.2 bitcast_convert_fusion
  531.5 88.6 %all-reduce.11.cloned.1.call-done = (bf16[1568,768]{1,0:T(8,128)(2,1)}, bf16[1568,768]{1,0:T(8,128)(2,1)}) async-done(((bf16[1568,768]{1,0:T(8,128)(2,1)}, bf16[1568,768]{1,0:T(8,128)(2,1)}), (bf16[1568,768]{1,0:T(8,128)(2,1)}, bf16[1568,768]{1,0:T(8,128)(2,1)})) %all-reduce.11.cloned.1.call-update) | async-done | bytes 4816912 | tf_op jit(solution)/shard_map/psum | solution.py:136
  620.1 5.3 fusion.16
  625.5 7.7 select_reduce_fusion
  634.3 6.4 fusion.85
  640.7 4.7 fusion.26
  660.7 21.4 %all-reduce.1 = f32[2,1,192]{2,1,0:T(1,128)S(1)} all-reduce(f32[2,1,192]{2,1,0:T(1,128)S(1)} %broadcast_in_dim.64), channel_id=3, replica_groups=mesh['dp'=8,'tensor'=4] {'dp'}, use_global_device_ids=true, to_apply=%region_17.18.clone | all-reduce | flops 384 | bytes 3072
  685.1 5.3 multiply_convert_fusion.1
  694.9 5.2 reshape.215
  712.7 8.2 reduce-scatter.29.cloned.1.call-done
  723.2 70.3 %reduce-scatter.19.cloned.1.call-done = f32[96,768]{1,0:T(8,128)} async-done(((f32[768,768]{1,0:T(8,128)}), f32[96,768]{1,0:T(8,128)}) %reduce-scatter.19.cloned.1.call-update) | async-done | bytes 294928 | tf_op jit(solution)/shard_map/reduce_scatter | solution.py:196
  795.7 67.6 %reduce-scatter.23.cloned.1.call-done = f32[96,576]{1,0:T(8,128)} async-done(((f32[768,576]{1,0:T(8,128)}), f32[96,576]{1,0:T(8,128)}) %reduce-scatter.23.cloned.1.call-update) | async-done | bytes 221200
  869.2 59.5 %reduce-scatter.31.cloned.1.call-done = f32[96,196]{1,0:T(8,128)} async-done(((f32[768,196]{1,0:T(8,128)}), f32[96,196]{1,0:T(8,128)}) %reduce-scatter.31.cloned.1.call-update) | async-done | bytes 75280
  (286 shorter events, 142.3 us)
Async XLA Ops:
  8.0 66.3 %copy-start.3 = (bf16[8,196,768]{2,0,1:T(8,128)(2,1)S(1)}, bf16[8,196,768]{2,0,1:T(8,128)(2,1)}, u32[]{:S(2)}) copy-start(bf16[8,196,768]{2,0,1:T(8,128)(2,1)} %param.29) | copy-start | bytes 7225348
  8.1 250.9 %all-reduce.7.cloned.1.call-start = ((), (), s32[]{:S(2)}) async-start(), calls=%async_computation.7 | async-start | bytes 4816896 | tf_op jit(solution)/shard_map/psum | solution.py:126
  37.6 116.6 %copy-start.36 = (f32[768]{0:T(1024)}, f32[768]{0:T(1024)S(1)}, u32[]{:S(2)}) copy-start(f32[768]{0:T(1024)S(1)} %get-tuple-element.287) | copy-start | bytes 9220
  74.3 79.9 %copy-start.28 = (f32[1568]{0:T(1024)}, f32[1568]{0:T(1024)S(1)}, u32[]{:S(2)}) copy-start(f32[1568]{0:T(1024)S(1)} %div.147) | copy-start | bytes 18820
  85.4 36.7 %copy-start.53 = (f32[2,1,24]{2,1,0:T(1,128)S(1)}, f32[2,1,24]{2,1,0:T(1,128)}, u32[]{:S(2)}) copy-start(f32[2,1,24]{2,1,0:T(1,128)} %param.37) | copy-start | bytes 580
  85.5 71.7 %copy-start.30 = (f32[1568]{0:T(1024)}, f32[1568]{0:T(1024)S(1)}, u32[]{:S(2)}) copy-start(f32[1568]{0:T(1024)S(1)} %rsqrt.20) | copy-start | bytes 18820
  122.1 37.0 %copy-start.21 = (bf16[3,768,192]{1,2,0:T(8,128)(2,1)}, bf16[3,768,192]{1,2,0:T(8,128)(2,1)S(1)}, u32[]{:S(2)}) copy-start(bf16[3,768,192]{1,2,0:T(8,128)(2,1)S(1)} %copy.325) | copy-start | bytes 2654212
  166.6 38.5 %copy-start.57 = (f32[1,96]{1,0:T(1,128)S(1)}, f32[1,96]{1,0:T(1,128)}, u32[]{:S(2)}) copy-start(f32[1,96]{1,0:T(1,128)} %param.46) | copy-start | bytes 1156
  166.6 38.5 %copy-start.50 = (u32[32]{0:T(128)S(1)}, u32[32]{0:T(128)}, u32[]{:S(2)}) copy-start(u32[32]{0:T(128)} %constant.33) | copy-start | bytes 388
  166.6 59.9 %copy-start.4 = (bf16[8,196,768]{2,0,1:T(8,128)(2,1)S(1)}, bf16[8,196,768]{2,0,1:T(8,128)(2,1)}, u32[]{:S(2)}) copy-start(bf16[8,196,768]{2,0,1:T(8,128)(2,1)} %param.30) | copy-start | bytes 7225348
  169.9 59.4 %copy-start.13 = (bf16[1568,192]{0,1:T(8,128)(2,1)}, bf16[1568,192]{0,1:T(8,128)(2,1)S(1)}, u32[]{:S(2)}) copy-start(bf16[1568,192]{0,1:T(8,128)(2,1)S(1)} %reshape.211) | copy-start | bytes 1806340
  203.3 63.9 %all-gather.4.cloned.1.call-start = ((), (), s32[]{:S(2)}) async-start(), calls=%async_computation.8 | async-start | bytes 1327104 | tf_op jit(solution)/shard_map/all_gather | solution.py:89
  205.0 155.1 %reduce-scatter.21.cloned.1.call-start = ((), (), s32[]{:S(2)}) async-start(), calls=%async_computation.12 | async-start | bytes 2654208 | tf_op jit(solution)/shard_map/reduce_scatter | solution.py:198
  235.4 243.7 %copy-start.34 = (f32[1568]{0:T(1024)}, f32[1568]{0:T(1024)S(1)}, u32[]{:S(2)}) copy-start(f32[1568]{0:T(1024)S(1)} %convert_element_type.207) | copy-start | bytes 18820
  283.8 76.3 %copy-start.26 = (f32[768,96]{0,1:T(8,128)S(1)}, f32[768,96]{0,1:T(8,128)}, u32[]{:S(2)}) copy-start(f32[768,96]{0,1:T(8,128)} %param.49) | copy-start | bytes 884740
  283.8 76.3 %copy-start.27 = (f32[768,96]{0,1:T(8,128)S(1)}, f32[768,96]{0,1:T(8,128)}, u32[]{:S(2)}) copy-start(f32[768,96]{0,1:T(8,128)} %param.50) | copy-start | bytes 884740
  290.2 112.9 %all-gather.6.cloned.1.call-start = ((), (), s32[]{:S(2)}) async-start(), calls=%async_computation.9 | async-start | bytes 1327104 | tf_op jit(solution)/shard_map/all_gather | solution.py:91
  362.4 110.7 %all-reduce.9.cloned.1.call-start = ((), (), s32[]{:S(2)}) async-start(), calls=%async_computation.10 | async-start | bytes 4816896 | tf_op jit(solution)/shard_map/psum | solution.py:146
  418.0 202.1 %all-reduce.11.cloned.1.call-start = ((), (), s32[]{:S(2)}) async-start(), calls=%async_computation.18 | async-start | bytes 9633792 | tf_op jit(solution)/shard_map/psum | solution.py:136
  524.3 133.8 %reduce-scatter.27.cloned.1.call-start = ((), (), s32[]{:S(2)}) async-start(), calls=%async_computation.15 | async-start | bytes 442368
  525.0 95.0 %copy-start.29 = (f32[1568]{0:T(1024)S(1)}, f32[1568]{0:T(1024)}, u32[]{:S(2)}) copy-start(f32[1568]{0:T(1024)} %copy-done.28) | copy-start | bytes 18820
  525.0 95.0 %copy-start.31 = (f32[1568]{0:T(1024)S(1)}, f32[1568]{0:T(1024)}, u32[]{:S(2)}) copy-start(f32[1568]{0:T(1024)} %copy-done.30) | copy-start | bytes 18820
  525.1 95.0 %copy-start.37 = (f32[768]{0:T(1024)S(1)}, f32[768]{0:T(1024)}, u32[]{:S(2)}) copy-start(f32[768]{0:T(1024)} %copy-done.36) | copy-start | bytes 9220
  526.9 156.4 %reduce-scatter.25.cloned.1.call-start = ((), (), s32[]{:S(2)}) async-start(), calls=%async_computation.14 | async-start | bytes 884736
  531.4 189.6 %reduce-scatter.29.cloned.1.call-start = ((), (), s32[]{:S(2)}) async-start(), calls=%async_computation.16 | async-start | bytes 442368
  634.2 159.2 %reduce-scatter.19.cloned.1.call-start = ((), (), s32[]{:S(2)}) async-start(), calls=%async_computation.11 | async-start | bytes 2654208 | tf_op jit(solution)/shard_map/reduce_scatter | solution.py:196
  640.6 222.6 %reduce-scatter.23.cloned.1.call-start = ((), (), s32[]{:S(2)}) async-start(), calls=%async_computation.13 | async-start | bytes 2211840
  651.4 33.7 %copy-start.35 = (f32[1568]{0:T(1024)S(1)}, f32[1568]{0:T(1024)}, u32[]{:S(2)}) copy-start(f32[1568]{0:T(1024)} %copy-done.34) | copy-start | bytes 18820
  651.4 33.7 %copy-start.41 = (f32[768]{0:T(1024)S(1)}, f32[768]{0:T(1024)}, u32[]{:S(2)}) copy-start(f32[768]{0:T(1024)} %get-tuple-element.282) | copy-start | bytes 9220
  651.4 277.3 %reduce-scatter.31.cloned.1.call-start = ((), (), s32[]{:S(2)}) async-start(), calls=%async_computation.17 | async-start | bytes 884736
  708.2 85.3 %copy-start.18 = (f32[96,768]{1,0:T(8,128)S(1)}, f32[96,768]{1,0:T(8,128)}, u32[]{:S(2)}) copy-start(f32[96,768]{1,0:T(8,128)} %param.43) | copy-start | bytes 884740
  712.7 217.0 %copy-start.22 = (f32[196,96]{1,0:T(8,128)S(1)}, f32[196,96]{1,0:T(8,128)}, u32[]{:S(2)}) copy-start(f32[196,96]{1,0:T(8,128)} %copy.352) | copy-start | bytes 225796
  (43 other events, 408.3 us)
Sparse Core Ops, SparseCore 0:
  203.4 55.5 all-reduce.6
  418.1 54.9 all-reduce.8
  524.4 95.6 all-reduce.10
Sparse Core Ops, SparseCore 1:
  206.5 40.1 all-gather.3
  290.3 69.7 reduce-scatter.20
  362.8 40.3 all-gather.5
  528.4 62.2 reduce-scatter.26
  594.0 62.3 reduce-scatter.24
  659.6 61.3 reduce-scatter.28
  724.4 69.0 reduce-scatter.18
  796.8 66.4 reduce-scatter.22
  866.4 62.2 reduce-scatter.30
where the time goes:
time: 946 us; the launch traced here: 940 us
  waiting for transfers between devices  478 us (51%)
  blocking collectives  197 us (21%)
  local copies, waits for them, and re-layouts  97.7 us (10%)
  matrix products  77.9 us (8%)
  other arithmetic  69.7 us (7%)
  between operations  18.7 us (2%)
    unnamed x17, waiting for transfers between devices  136 us
    psum x1, waiting for transfers between devices, local(): lax.psum(down_part.astype(jnp.bfloat16), 'tensor').astype(jnp.float32)  88.6 us
    reduce_scatter x1, waiting for transfers between devices, local(): lax.psum_scatter(grad_expand, 'dp', scatter_dimension=0, tiled=True)  70.3 us
    reduce_scatter x1, waiting for transfers between devices, local(): lax.psum_scatter(grad_reduce, 'dp', scatter_dimension=1, tiled=True)  69.8 us
    psum x1, waiting for transfers between devices, local(): lax.psum(partial_two.astype(jnp.bfloat16), 'tensor').astype(jnp.float32)  49.6 us
    unnamed x2, blocking collectives  41.3 us
    unnamed x160, local copies, waits for them, and re-layouts  41 us
    all_gather x1, waiting for transfers between devices, local(): lax.all_gather(reduce_weight.astype(half), 'dp', axis=1, tiled=True)  40.6 us
  transfers between devices with their start and end apart: 12, of which 9 were waited for; matrix products, arithmetic and copies ran while one was open for 12% of the time, Pallas kernels for 0%

commit v1 on v0

v1 whole, which is shorter than its diff:
```python
import functools

import jax
import jax.numpy as jnp
from jax import lax
from jax.experimental import pallas as pl
from jax.experimental.pallas import tpu as pltpu
from jax.sharding import PartitionSpec as P

HEAD_DIM = 64
STEP = 7
NORM_EPS = 1e-06
HALF = jnp.bfloat16
SINGLE = jnp.float32
VMEM = pl.BlockSpec(memory_space=pltpu.VMEM)
SMEM = pl.BlockSpec(memory_space=pltpu.SMEM)
ANY = pl.BlockSpec(memory_space=pl.ANY)
CHUNK = 16
SMALL_ROWS = 80
PLACE_ROWS = 64


def adamw(master, moment, second, grad, rate, decay):
    moment = 0.9 * moment + 0.1 * grad
    second = 0.999 * second + 0.001 * grad * grad
    fixed_first = moment / (1.0 - 0.9**STEP)
    fixed_second = second / (1.0 - 0.999**STEP)
    master = master - rate * (fixed_first / (jnp.sqrt(fixed_second) + 1e-08) + decay * master)
    return (master, moment, second, master.astype(jnp.bfloat16))


def dot(left, right):
    return jnp.dot(left, right, preferred_element_type=SINGLE)


def row_dot(left, right):
    return lax.dot_general(left, right, (((1,), (1,)), ((), ())), preferred_element_type=SINGLE)


def column_dot(left, right):
    return lax.dot_general(left, right, (((0,), (0,)), ((), ())), preferred_element_type=SINGLE)


def kernel_call(body, outs, operands, scratch, flops, name):
    size = lambda a: a.size * a.dtype.itemsize
    moved = sum(size(a) for a, _ in operands) + sum(size(a) for a, _ in outs)
    return pl.pallas_call(
        body,
        out_shape=[a for a, _ in outs],
        in_specs=[spec for _, spec in operands],
        out_specs=[spec for _, spec in outs],
        scratch_shapes=scratch,
        cost_estimate=pl.CostEstimate(flops=flops, bytes_accessed=moved, transcendentals=0),
        name=name,
    )(*[a for a, _ in operands])


def shape(dims, kind):
    return jax.ShapeDtypeStruct(dims, kind)


class Direct:
    def __init__(self, n_dp, n_tensor):
        self.n_dp = n_dp
        self.n_tensor = n_tensor

    def flip(self, array, axis, bits):
        count = self.n_dp if axis == "dp" else self.n_tensor
        return lax.ppermute(array, axis, [(i, i ^ bits) for i in range(count)])

    def along(self, array, name):
        axis, bits = {
            "core": ("tensor", 1),
            "x": ("tensor", 2),
            "y": ("dp", 1),
            "z1": ("dp", 2),
            "z2": ("dp", 4),
            "z3": ("dp", 6),
        }[name]
        return self.flip(array, axis, bits)

    def gather(self, shard):
        blocks = [shard] + [self.along(shard, f"z{k}") for k in (1, 2, 3)]
        first = jnp.stack(blocks[:2])
        last = jnp.stack(blocks[2:])
        first_y = self.along(first, "y")
        last_x = self.along(last, "x")
        chip = [
            (first, 0, 0, (0, 1)),
            (first_y, 0, 1, (0, 1)),
            (self.along(first, "x"), 1, 0, (0, 1)),
            (self.along(first_y, "x"), 1, 1, (0, 1)),
            (last, 0, 0, (2, 3)),
            (last_x, 1, 0, (2, 3)),
            (self.along(last, "y"), 0, 1, (2, 3)),
            (self.along(last_x, "y"), 1, 1, (2, 3)),
        ]
        pieces = []
        for core in (0, 1):
            for piece, x, y, steps in chip:
                held = self.along(piece, "core") if core else piece
                pieces.append((held, [(2 * x + core, 2 * k + y) for k in steps]))
        return pieces

    def grad_layout(self):
        layout = []
        for core in (0, 1):
            for half, steps in enumerate(((0, 1), (2, 3))):
                for first in (0, 1):
                    blocks = []
                    for second in (0, 1):
                        x, y = (first, second) if half == 0 else (second, first)
                        for k in steps:
                            blocks.append((2 * x + core, 2 * k + y))
                    layout.append(blocks)
        return layout

    def reduce(self, outs):
        sent = [self.along(piece, "core") for piece in outs[4:]]
        held = [add(kept, came) for kept, came in zip(outs[:4], sent)]
        done = []
        for half, (one, two) in enumerate((("x", "y"), ("y", "x"))):
            keep, send = held[2 * half], held[2 * half + 1]
            came = self.along(send, one)
            near = add(keep[:2], came[:2])
            far = add(keep[2:], came[2:])
            done.append(add(near, self.along(far, two)))
        near, far = done
        return [
            near[0],
            self.along(near[1], "z1"),
            self.along(far[0], "z2"),
            self.along(far[1], "z3"),
        ]


def add(left, right):
    return (left.astype(SINGLE) + right.astype(SINGLE)).astype(HALF)


def load_pieces(place_ref, piece_refs, spots, dst_ref, sems):
    copies = []
    for ref, where in zip(piece_refs, spots):
        for j, (t_flip, dp_flip) in enumerate(where):
            t = place_ref[1] ^ t_flip
            if dp_flip is None:
                dst = dst_ref.at[t]
            else:
                rows = ref.shape[1]
                row = pl.multiple_of((place_ref[0] ^ dp_flip) * rows, rows)
                dst = dst_ref.at[t, pl.ds(row, rows), :]
            copies.append(pltpu.make_async_copy(ref.at[j], dst, sems.at[len(copies)]))
    for copy in copies:
        copy.start()
    return copies


def store_grads(place_ref, src_ref, out_refs, layout, rows, sems):
    copies = []
    for ref, where in zip(out_refs, layout):
        for j, (t_flip, dp_flip) in enumerate(where):
            t = place_ref[1] ^ t_flip
            if dp_flip is None:
                src = src_ref.at[t]
            else:
                row = pl.multiple_of((place_ref[0] ^ dp_flip) * rows, rows)
                src = src_ref.at[t, pl.ds(row, rows), :]
            copies.append(pltpu.make_async_copy(src, ref.at[j], sems.at[len(copies)]))
    for copy in copies:
        copy.start()
    return copies


def wait_all(copies):
    for copy in copies:
        copy.wait()


def fold(rows):
    return rows[:8] + rows[8:]


def norm_scaled(rows):
    width = rows.shape[-1]
    centered = rows - jnp.sum(rows, -1, keepdims=True) * (1.0 / width)
    inverse = lax.rsqrt(jnp.sum(centered * centered, -1, keepdims=True) * (1.0 / width) + NORM_EPS)
    return centered * inverse, inverse


def norm_grad(grad, scaled, inverse, gain):
    width = grad.shape[-1]
    scale = 1.0 / width
    e = grad * gain
    mean_e = jnp.sum(e, -1, keepdims=True) * scale
    mean_cross = jnp.sum(e * scaled, -1, keepdims=True) * scale
    return inverse * (e - mean_e - scaled * mean_cross)


def start_body(
    images, patches, pad, packed, place_ref, patch_ref, cot_ref, mask_ref, live_ref, *rest
):
    if packed:
        (small_ref, start_ref, normed_ref, low_ref, table_ref, entry_ref, expand_ref, pair, both, spot, sems) = rest
    else:
        (spot, table_in, entry_in, expand_in, start_ref, normed_ref, low_ref, table_ref, entry_ref, expand_ref, pair, both, sems) = rest
    t = place_ref[1]
    copies = [
        pltpu.make_async_copy(patch_ref.at[pl.ds(images * t, images)], pair, sems.at[0]),
        pltpu.make_async_copy(cot_ref.at[pl.ds(images * t, images)], both, sems.at[1]),
    ]
    for copy in copies:
        copy.start()
    n_tensor = entry_ref.shape[0]
    columns = entry_ref.shape[2] // 3
    entry_ref[...] = jnp.zeros_like(entry_ref)
    if packed:
        n_dp = small_ref.shape[0] // n_tensor
        part = spot.shape[1] // n_dp
        for dp_at in range(n_dp):
            for t_at in range(n_tensor):
                t_flip = t ^ t_at
                dp_flip = place_ref[0] ^ dp_at
                slot = (t_flip & 1) * 16 + (t_flip >> 1) * 8 + (dp_flip & 1) * 4 + (dp_flip >> 1)
                block = small_ref[slot].astype(SINGLE)
                spot[PLACE_ROWS * t_at : PLACE_ROWS * (t_at + 1), part * dp_at : part * (dp_at + 1)] = block[:PLACE_ROWS, :part]
                bias = block[PLACE_ROWS : PLACE_ROWS + 8]
                expand_ref[t_at, :, part * dp_at : part * (dp_at + 1)] = bias[0:1, :part]
                own = part // n_tensor
                entry_ref[t_at, :, own * dp_at : own * (dp_at + 1)] = bias[1:2, :own]
                entry_ref[t_at, :, 2 * columns + own * dp_at : 2 * columns + own * (dp_at + 1)] = bias[2:3, :own]
        table_ref[...] = spot[200:208, :]
    else:
        table_ref[...] = table_in[...]
        entry_ref[...] = entry_in[...]
        expand_ref[...] = expand_in[...]
    wait_all(copies)
    start_ref[...] = jnp.zeros_like(start_ref)
    token = table_ref[6:7, :]
    low_ref[...] = jnp.zeros_like(low_ref)
    for i in range(images):
        rows = pl.ds(i * pad, patches)
        picked = jnp.where(mask_ref[rows, :] > 0.5, token, pair[i].astype(SINGLE))
        start_ref[rows, :] = picked + spot[:patches, :]
        low_ref[rows, :] = (both[i].astype(SINGLE) * live_ref[i]).astype(HALF)
    gain, shift = table_ref[0:1, :], table_ref[1:2, :]

    def one(j, carry):
        rows = pl.ds(pl.multiple_of(j * CHUNK, CHUNK), CHUNK)
        scaled, _ = norm_scaled(start_ref[rows, :])
        normed_ref[rows, :] = (scaled * gain + shift).astype(HALF)
        return carry

    lax.fori_loop(0, start_ref.shape[0] // CHUNK, one, 0)


def attend_body(
    images, patches, pad, spots, place_ref, normed_ref, bias_ref, *rest
):
    n = len(spots)
    piece_refs = rest[:n]
    qkv_ref, probs_ref, mixed_ref, full_ref, held, sems, out_sem = rest[n:]
    columns = mixed_ref.shape[2]
    heads = columns // HEAD_DIM
    wait_all(load_pieces(place_ref, piece_refs, spots, held, sems))
    out = pltpu.make_async_copy(held, full_ref, out_sem)
    out.start()
    lanes = lax.broadcasted_iota(jnp.int32, (pad, pad), 1)

    def one(t, carry):
        qkv = dot(normed_ref[...], held[t, :, : 3 * columns]) + bias_ref[t]
        qkv_ref[t] = qkv.astype(HALF)
        for i in range(images):
            rows = slice(i * pad, (i + 1) * pad)
            for h in range(heads):
                at = h * HEAD_DIM
                query = qkv_ref[t, rows, at : at + HEAD_DIM]
                keys = qkv_ref[t, rows, columns + at : columns + at + HEAD_DIM]
                values = qkv_ref[t, rows, 2 * columns + at : 2 * columns + at + HEAD_DIM]
                scores = row_dot(query, keys) * HEAD_DIM ** (-0.5)
                scores = jnp.where(lanes < patches, scores, -1e30)
                risen = jnp.exp(scores - jnp.max(scores, -1, keepdims=True))
                probs = (risen * (1.0 / jnp.sum(risen, -1, keepdims=True))).astype(HALF)
                probs_ref[t, i * heads + h] = probs
                mixed_ref[t, rows, at : at + HEAD_DIM] = dot(probs, values).astype(HALF)
        return carry

    lax.fori_loop(0, held.shape[0], one, 0)
    out.wait()


def up_body(spots, layout, rows_out, place_ref, start_ref, mixed_ref, full_ref, low_ref, table_ref, bias_ref, *rest):
    n, m = len(spots), len(layout)
    piece_refs = rest[:n]
    middle_ref, normed_ref, active_ref, slope_ref, expand_ref = rest[n : n + 5]
    out_refs = rest[n + 5 : n + 5 + m]
    held, upper, grads, sems, out_sem, grad_sems = rest[n + 5 + m :]
    n_tensor = held.shape[0]
    tokens = start_ref.shape[0]
    columns = mixed_ref.shape[2]
    copies = load_pieces(place_ref, piece_refs, spots, held, sems)
    middle_ref[...] = start_ref[...] + table_ref[4:5, :]

    def leave(t, carry):
        middle_ref[...] += row_dot(mixed_ref[t], full_ref[t, :, 3 * columns :])
        return carry

    lax.fori_loop(0, n_tensor, leave, 0)
    gain, shift = table_ref[2:3, :], table_ref[3:4, :]

    def one(j, carry):
        rows = pl.ds(pl.multiple_of(j * CHUNK, CHUNK), CHUNK)
        scaled, _ = norm_scaled(middle_ref[rows, :])
        normed_ref[rows, :] = (scaled * gain + shift).astype(HALF)
        return carry

    lax.fori_loop(0, tokens // CHUNK, one, 0)
    wait_all(copies)
    out = pltpu.make_async_copy(held, expand_ref, out_sem)
    out.start()

    def up(t, carry):
        upper[...] = dot(normed_ref[...], held[t]) + bias_ref[t]

        def bend(j, inner):
            rows = pl.ds(pl.multiple_of(j * CHUNK, CHUNK), CHUNK)
            u = upper[rows, :]
            cdf = 0.5 * (1.0 + lax.erf(u * 0.7071067811865476))
            active_ref[t, rows, :] = (u * cdf).astype(HALF)
            slope = cdf + u * (jnp.exp(u * u * -0.5) * 0.3989422804014327)
            slope_ref[t, rows, :] = slope.astype(HALF)
            return inner

        lax.fori_loop(0, tokens // CHUNK, bend, 0)
        grads[t] = column_dot(low_ref[...], active_ref[t]).astype(HALF)
        return carry

    lax.fori_loop(0, n_tensor, up, 0)
    wait_all(store_grads(place_ref, grads, out_refs, layout, rows_out, grad_sems))
    out.wait()


def down_body(spots, layout, rows_out, place_ref, low_ref, slope_ref, normed_ref, *rest):
    n, m = len(spots), len(layout)
    piece_refs = rest[:n]
    grad_upper_ref, reduce_ref, sums_ref = rest[n : n + 3]
    out_refs = rest[n + 3 : n + 3 + m]
    held, upper, grads, sems, out_sem, grad_sems = rest[n + 3 + m :]
    n_tensor = held.shape[0]
    tokens, width = low_ref.shape
    wait_all(load_pieces(place_ref, piece_refs, spots, held, sems))
    out = pltpu.make_async_copy(held, reduce_ref, out_sem)
    out.start()

    def up(t, carry):
        upper[...] = dot(low_ref[...], held[t])

        def bend(j, total):
            rows = pl.ds(pl.multiple_of(j * CHUNK, CHUNK), CHUNK)
            grad = (upper[rows, :] * slope_ref[t, rows, :].astype(SINGLE)).astype(HALF)
            grad_upper_ref[t, rows, :] = grad
            return total + fold(grad.astype(SINGLE))

        total = lax.fori_loop(0, tokens // CHUNK, bend, jnp.zeros((8, upper.shape[1]), SINGLE))
        sums_ref[t] = total
        grads[t] = column_dot(normed_ref[...], grad_upper_ref[t]).astype(HALF)
        return carry

    lax.fori_loop(0, n_tensor, up, 0)
    wait_all(store_grads(place_ref, grads, out_refs, layout, rows_out, grad_sems))
    out.wait()


def middle_body(grad_upper_ref, expand_ref, full_ref, middle_ref, low_ref, table_ref, grad_ref, half_ref, mixed_ref, sums_ref, normed_grad):
    n_tensor, tokens, columns = mixed_ref.shape
    normed_grad[...] = row_dot(grad_upper_ref[0], expand_ref[0])

    def back(t, carry):
        normed_grad[...] += row_dot(grad_upper_ref[t], expand_ref[t])
        return carry

    lax.fori_loop(1, n_tensor, back, 0)
    gain = table_ref[2:3, :]

    def one(j, carry):
        rows = pl.ds(pl.multiple_of(j * CHUNK, CHUNK), CHUNK)
        scaled, inverse = norm_scaled(middle_ref[rows, :])
        grad = normed_grad[rows, :]
        low = low_ref[rows, :].astype(SINGLE)
        out = low + norm_grad(grad, scaled, inverse, gain)
        grad_ref[rows, :] = out
        half_ref[rows, :] = out.astype(HALF)
        parts = (grad * scaled, grad, out, low)
        return tuple(c + fold(p) for c, p in zip(carry, parts))

    zero = jnp.zeros((8, low_ref.shape[1]), SINGLE)
    totals = lax.fori_loop(0, tokens // CHUNK, one, (zero,) * 4)
    for row, total in enumerate(totals):
        sums_ref[row] = total

    def mix(t, carry):
        mixed_ref[t] = dot(half_ref[...], full_ref[t, :, 3 * columns :]).astype(HALF)
        return carry

    lax.fori_loop(0, n_tensor, mix, 0)


def attend_back_body(images, pad, layout, rows_out, place_ref, qkv_ref, probs_ref, grad_mixed_ref, normed_ref, half_ref, mixed_ref, *rest):
    m = len(layout)
    grad_ref, sums_ref = rest[:2]
    out_refs = rest[2 : 2 + m]
    grads, grad_sems = rest[2 + m :]
    n_tensor, tokens, columns = mixed_ref.shape
    heads = columns // HEAD_DIM
    scale = HEAD_DIM ** (-0.5)

    def one(t, carry):
        for i in range(images):
            rows = slice(i * pad, (i + 1) * pad)
            for h in range(heads):
                at = h * HEAD_DIM
                query = qkv_ref[t, rows, at : at + HEAD_DIM]
                keys = qkv_ref[t, rows, columns + at : columns + at + HEAD_DIM]
                values = qkv_ref[t, rows, 2 * columns + at : 2 * columns + at + HEAD_DIM]
                grad = grad_mixed_ref[t, rows, at : at + HEAD_DIM]
                low = probs_ref[t, i * heads + h]
                probs = low.astype(SINGLE)
                grad_ref[t, rows, 2 * columns + at : 2 * columns + at + HEAD_DIM] = column_dot(low, grad).astype(HALF)
                grad_probs = row_dot(grad, values)
                inner = jnp.sum(probs * grad_probs, -1, keepdims=True)
                grad_scores = (probs * (grad_probs - inner)).astype(HALF)
                grad_ref[t, rows, at : at + HEAD_DIM] = (dot(grad_scores, keys) * scale).astype(HALF)
                grad_ref[t, rows, columns + at : columns + at + HEAD_DIM] = (column_dot(grad_scores, query) * scale).astype(HALF)
        total = grad_ref[t].astype(SINGLE)
        sums_ref[t] = jnp.sum(total.reshape(tokens // 8, 8, 3 * columns), 0)
        grads[t, :, : 3 * columns] = column_dot(normed_ref[...], grad_ref[t]).astype(HALF)
        grads[t, :, 3 * columns :] = column_dot(half_ref[...], mixed_ref[t]).astype(HALF)
        return carry

    lax.fori_loop(0, n_tensor, one, 0)
    wait_all(store_grads(place_ref, grads, out_refs, layout, rows_out, grad_sems))


def output_body(images, patches, pad, live_ref, middle_ref, active_ref, reduce_ref, table_ref, out_ref, total, low):
    n_tensor = active_ref.shape[0]
    total[...] = middle_ref[...] + table_ref[5:6, :]

    def one(t, carry):
        total[...] += row_dot(active_ref[t], reduce_ref[t])
        return carry

    lax.fori_loop(0, n_tensor, one, 0)
    for i in range(images):
        out_ref[i] = (total[pl.ds(i * pad, patches), :] * live_ref[i]).astype(HALF)


def end_body(images, patches, pad, packed, place_ref, grad_qkv_ref, full_ref, start_ref, grad_middle_ref, mask_ref, table_ref, sums_two_ref, sums_entry_ref, sums_expand_ref, *rest):
    if packed:
        out_ref, small_ref, normed_grad, ended, low, spot = rest
    else:
        out_ref, spot, entry_ref, expand_ref, normed_grad, ended, low = rest
    n_tensor = grad_qkv_ref.shape[0]
    tokens, width = start_ref.shape
    columns = grad_qkv_ref.shape[2] // 3
    normed_grad[...] = row_dot(grad_qkv_ref[0], full_ref[0, :, : 3 * columns])

    def back(t, carry):
        normed_grad[...] += row_dot(grad_qkv_ref[t], full_ref[t, :, : 3 * columns])
        return carry

    lax.fori_loop(1, n_tensor, back, 0)
    gain = table_ref[0:1, :]

    def one(j, carry):
        rows = pl.ds(pl.multiple_of(j * CHUNK, CHUNK), CHUNK)
        scaled, inverse = norm_scaled(start_ref[rows, :])
        grad = normed_grad[rows, :]
        out = grad_middle_ref[rows, :] + norm_grad(grad, scaled, inverse, gain)
        ended[rows, :] = out
        masked = mask_ref[rows, :] > 0.5
        low[rows, :] = jnp.where(masked, 0.0, out).astype(HALF)
        parts = (grad * scaled, grad, jnp.where(masked, out, 0.0))
        return tuple(c + fold(p) for c, p in zip(carry, parts))

    zero = jnp.zeros((8, width), SINGLE)
    totals = lax.fori_loop(0, tokens // CHUNK, one, (zero,) * 3)
    for i in range(images):
        out_ref[i] = low[pl.ds(i * pad, patches), :]
    place = ended[:pad, :]
    for i in range(1, images):
        place = place + ended[i * pad : (i + 1) * pad, :]
    column = lambda total: jnp.sum(total, 0, keepdims=True)
    spot[...] = jnp.zeros_like(spot)
    spot[:pad, :] = place
    rows = [column(totals[0]), column(totals[1])]
    rows += [column(sums_two_ref[row]) for row in range(4)]
    rows += [column(totals[2])]
    for row, total in enumerate(rows):
        spot[200 + row : 201 + row, :] = total
    if not packed:
        for t in range(n_tensor):
            entry_ref[t] = column(sums_entry_ref[t])
            expand_ref[t] = column(sums_expand_ref[t])
        return
    n_dp = small_ref.shape[0] // n_tensor
    part = width // n_dp
    own = part // n_tensor
    small_ref[...] = jnp.zeros_like(small_ref)
    for t_at in range(n_tensor):
        entry = column(sums_entry_ref[t_at])
        expand = column(sums_expand_ref[t_at])
        for dp_at in range(n_dp):
            t_flip = place_ref[1] ^ t_at
            dp_flip = place_ref[0] ^ dp_at
            slot = (t_flip & 1) * 16 + (t_flip >> 1) * 8 + (dp_flip & 1) * 4 + (dp_flip >> 1)
            block = spot[PLACE_ROWS * t_at : PLACE_ROWS * (t_at + 1), part * dp_at : part * (dp_at + 1)]
            small_ref[slot, :PLACE_ROWS, :part] = block
            small_ref[slot, PLACE_ROWS : PLACE_ROWS + 1, :part] = expand[:, part * dp_at : part * (dp_at + 1)]
            small_ref[slot, PLACE_ROWS + 1 : PLACE_ROWS + 2, :own] = entry[:, own * dp_at : own * (dp_at + 1)]
            small_ref[slot, PLACE_ROWS + 2 : PLACE_ROWS + 3, :own] = entry[:, 2 * columns + own * dp_at : 2 * columns + own * (dp_at + 1)]


def place_body(images, place_ref, own_ref, core_ref, x_ref, far_ref, out_ref):
    t = place_ref[1]
    for flip, ref in enumerate((own_ref, core_ref, x_ref, far_ref)):
        out_ref[pl.ds((t ^ flip) * images, images)] = ref[...]


def local(sizes, *arguments):
    (patches, cotangent, mask_rank, mask_count, image_count,
     entry_weight, entry_moment, entry_second, entry_bias, entry_bias_moment, entry_bias_second,
     exit_weight, exit_moment, exit_second, expand_weight, expand_moment, expand_second,
     expand_bias, expand_bias_moment, expand_bias_second, reduce_weight, reduce_moment, reduce_second,
     vectors, vectors_moment, vectors_second, position, position_moment, position_second) = arguments
    n_dp, n_tensor = sizes
    direct = n_dp == 8 and n_tensor == 4
    dp, tensor = lax.axis_index("dp"), lax.axis_index("tensor")
    at = jnp.stack([dp, tensor]).astype(jnp.int32)
    slots, patch_count, width = patches.shape
    images = slots // n_tensor
    pad = -(-patch_count // CHUNK) * CHUNK
    tokens = images * pad
    columns = entry_weight.shape[2]
    hidden = expand_weight.shape[1]
    rows = entry_weight.shape[1]
    heads = columns // HEAD_DIM

    attn_shard = jnp.concatenate(
        [entry_weight[0], entry_weight[1], entry_weight[2], exit_weight.T], 1
    ).astype(HALF)
    expand_shard = expand_weight.astype(HALF)
    reduce_shard = reduce_weight.T.astype(HALF)

    own = lambda array: lax.dynamic_slice_in_dim(array, tensor * images, images, 0)
    masked = (own(mask_rank) < own(mask_count)[:, None]).astype(SINGLE)
    mask = jnp.pad(masked, ((0, 0), (0, pad - patch_count))).reshape(tokens, 1)
    live = (tensor * images + jnp.arange(images, dtype=jnp.int32) < image_count[0]).astype(SINGLE)

    swap = Direct(n_dp, n_tensor)
    if direct:
        part_rows = jnp.concatenate(
            [
                position.astype(HALF),
                jnp.zeros((200 - patch_count, rows), HALF),
                vectors.astype(HALF),
                jnp.zeros((4 * PLACE_ROWS - 207, rows), HALF),
            ]
        )
        block = lax.dynamic_slice_in_dim(part_rows, tensor * PLACE_ROWS, PLACE_ROWS, 0)
        bias_rows = jnp.concatenate(
            [
                expand_bias.astype(HALF),
                jnp.pad(entry_bias[:, 0, :].astype(HALF), ((0, 0), (0, rows - entry_bias.shape[2]))),
                jnp.zeros((SMALL_ROWS - PLACE_ROWS - 3, rows), HALF),
            ]
        )
        small = jnp.pad(jnp.concatenate([block, bias_rows]), ((0, 0), (0, 128 - rows)))
        small = jnp.stack([small] + [swap.along(small, f"z{k}") for k in (1, 2, 3)])
        for name in ("y", "x", "core"):
            small = jnp.concatenate([small, swap.along(small, name)])
        attn_pieces = swap.gather(attn_shard)
        expand_pieces = swap.gather(expand_shard)
        reduce_pieces = swap.gather(reduce_shard)
        layout = swap.grad_layout()
        grad_outs = [shape((4, rows, width), HALF) for _ in layout]
        rows_out = rows
    else:
        def gather(shard):
            whole = lax.all_gather(shard, "dp", axis=0, tiled=True)
            whole = lax.all_gather(whole, "tensor", axis=0)
            turned = [lax.dynamic_index_in_dim(whole, tensor ^ t, 0) for t in range(n_tensor)]
            return [(turned[t], [(t, None)]) for t in range(n_tensor)]

        attn_pieces = gather(attn_shard)
        expand_pieces = gather(expand_shard)
        reduce_pieces = gather(reduce_shard)
        layout = [[(t, None)] for t in range(n_tensor)]
        grad_outs = [shape((1, width, width), HALF) for _ in layout]
        rows_out = width
        everywhere = lambda array, axis: lax.all_gather(array.astype(HALF), "dp", axis=axis, tiled=True)
        place = jnp.pad(everywhere(position, 1), ((0, 256 - patch_count), (0, 0))).astype(SINGLE)
        table_in = jnp.pad(everywhere(vectors, 1), ((0, 1), (0, 0))).astype(SINGLE)
        both = lax.all_gather(everywhere(entry_bias, 2), "tensor", axis=1, tiled=True)
        entry_in = jnp.concatenate([both[0], jnp.zeros_like(both[0]), both[1]], 1)
        entry_in = entry_in.astype(SINGLE)[:, None, :]
        expand_in = lax.all_gather(everywhere(expand_bias, 1), "tensor", axis=0, tiled=True)
        expand_in = expand_in.astype(SINGLE)[:, None, :]

    def pieces_of(pieces):
        return [(piece, ANY) for piece, _ in pieces], [where for _, where in pieces]

    copies = sum(len(where) for where in layout)
    held = pltpu.VMEM((n_tensor, width, width), HALF)
    wide = pltpu.VMEM((tokens, width), SINGLE)
    many = pltpu.SemaphoreType.DMA((copies,))
    one_sem = pltpu.SemaphoreType.DMA
    dense = 2 * tokens * width * width

    small_in = [(small, VMEM)] if direct else [(a, VMEM) for a in (place, table_in, entry_in, expand_in)]
    start_scratch = [pltpu.VMEM((images, patch_count, width), HALF)] * 2
    if direct:
        start_scratch.append(pltpu.VMEM((4 * PLACE_ROWS, width), SINGLE))
    start, normed_one, low, table, entry_shift, expand_shift = kernel_call(
        functools.partial(start_body, images, patch_count, pad, direct),
        [
            (shape((tokens, width), SINGLE), VMEM),
            (shape((tokens, width), HALF), VMEM),
            (shape((tokens, width), HALF), VMEM),
            (shape((8, width), SINGLE), VMEM),
            (shape((n_tensor, 1, 3 * columns), SINGLE), VMEM),
            (shape((n_tensor, 1, hidden), SINGLE), VMEM),
        ],
        [(at, SMEM), (patches, ANY), (cotangent, ANY), (mask, VMEM), (live, SMEM)] + small_in,
        start_scratch + [one_sem((2,))],
        0,
        "start",
    )

    operands, spots = pieces_of(attn_pieces)
    qkv, probs, mixed, attn_full = kernel_call(
        functools.partial(attend_body, images, patch_count, pad, spots),
        [
            (shape((n_tensor, tokens, 3 * columns), HALF), VMEM),
            (shape((n_tensor, images * heads, pad, pad), HALF), VMEM),
            (shape((n_tensor, tokens, columns), HALF), VMEM),
            (shape((n_tensor, width, width), HALF), ANY),
        ],
        [(at, SMEM), (normed_one, VMEM), (entry_shift, VMEM)] + operands,
        [held, many, one_sem],
        6 * dense,
        "attend",
    )

    operands, spots = pieces_of(expand_pieces)
    middle, normed_two, active, slope, expand_full, *grad_reduce = kernel_call(
        functools.partial(up_body, spots, layout, rows_out),
        [
            (shape((tokens, width), SINGLE), VMEM),
            (shape((tokens, width), HALF), VMEM),
            (shape((n_tensor, tokens, hidden), HALF), VMEM),
            (shape((n_tensor, tokens, hidden), HALF), VMEM),
            (shape((n_tensor, width, hidden), HALF), ANY),
        ]
        + [(a, ANY) for a in grad_outs],
        [(at, SMEM)]
        + [(a, VMEM) for a in (start, mixed, attn_full, low, table, expand_shift)]
        + operands,
        [held, wide, held, many, one_sem, many],
        12 * dense,
        "up",
    )

    operands, spots = pieces_of(reduce_pieces)
    grad_upper, reduce_full, sums_expand, *grad_expand = kernel_call(
        functools.partial(down_body, spots, layout, rows_out),
        [
            (shape((n_tensor, tokens, hidden), HALF), VMEM),
            (shape((n_tensor, width, hidden), HALF), ANY),
            (shape((n_tensor, 8, hidden), SINGLE), VMEM),
        ]
        + [(a, ANY) for a in grad_outs],
        [(at, SMEM)] + [(a, VMEM) for a in (low, slope, normed_two)] + operands,
        [held, wide, held, many, one_sem, many],
        10 * dense,
        "down",
    )

    grad_middle, grad_half, grad_mixed, sums_two = kernel_call(
        middle_body,
        [
            (shape((tokens, width), SINGLE), VMEM),
            (shape((tokens, width), HALF), VMEM),
            (shape((n_tensor, tokens, columns), HALF), VMEM),
            (shape((4, 8, width), SINGLE), VMEM),
        ],
        [(a, VMEM) for a in (grad_upper, expand_full, attn_full, middle, low, table)],
        [wide],
        6 * dense,
        "middle",
    )

    grad_qkv, sums_entry, *grad_attn = kernel_call(
        functools.partial(attend_back_body, images, pad, layout, rows_out),
        [
            (shape((n_tensor, tokens, 3 * columns), HALF), VMEM),
            (shape((n_tensor, 8, 3 * columns), SINGLE), VMEM),
        ]
        + [(a, ANY) for a in grad_outs],
        [(at, SMEM)]
        + [(a, VMEM) for a in (qkv, probs, grad_mixed, normed_one, grad_half, mixed)],
        [held, many],
        16 * dense,
        "attend_back",
    )

    (own_out,) = kernel_call(
        functools.partial(output_body, images, patch_count, pad),
        [(shape((images, patch_count, width), HALF), VMEM)],
        [(live, SMEM)] + [(a, VMEM) for a in (middle, active, reduce_full, table)],
        [wide, pltpu.VMEM((tokens, width), HALF)],
        4 * dense,
        "output",
    )

    small_out = (
        [(shape((n_dp * n_tensor, SMALL_ROWS, 128), SINGLE), VMEM)]
        if direct
        else [
            (shape((4 * PLACE_ROWS, width), SINGLE), VMEM),
            (shape((n_tensor, 1, 3 * columns), SINGLE), VMEM),
            (shape((n_tensor, 1, hidden), SINGLE), VMEM),
        ]
    )
    end_scratch = [wide, wide, pltpu.VMEM((tokens, width), HALF)]
    if direct:
        end_scratch.append(pltpu.VMEM((4 * PLACE_ROWS, width), SINGLE))
    own_grad, *small_grads = kernel_call(
        functools.partial(end_body, images, patch_count, pad, direct),
        [(shape((images, patch_count, width), HALF), VMEM)] + small_out,
        [(at, SMEM)]
        + [
            (a, VMEM)
            for a in (grad_qkv, attn_full, start, grad_middle, mask, table, sums_two, sums_entry, sums_expand)
        ],
        end_scratch,
        4 * dense,
        "end",
    )

    def spread(piece):
        far = swap.along(piece, "x")
        near = swap.along(piece, "core")
        return kernel_call(
            functools.partial(place_body, images),
            [(shape(patches.shape, HALF), VMEM)],
            [(at, SMEM)]
            + [(a, VMEM) for a in (piece, near, far, swap.along(far, "core"))],
            [],
            0,
            "spread",
        )[0]

    block_out = spread(own_out)
    patch_grad = spread(own_grad)

    if direct:
        def total(outs):
            parts = swap.reduce(outs)
            return sum(part.astype(SINGLE) for part in parts)

        reduced = total(grad_reduce).T
        expanded = total(grad_expand)
        attn = total(grad_attn)
        (small,) = small_grads
        small = small.astype(HALF)
        for name, count in (("core", 16), ("x", 8), ("y", 4)):
            small = add(small[:count], swap.along(small[count:], name))
        small = sum(
            part.astype(SINGLE)
            for part in [small[0]] + [swap.along(small[k], f"z{k}") for k in (1, 2, 3)]
        )
        pair = jnp.stack([small, swap.along(small, "core")])
        four = jnp.concatenate([pair, swap.along(pair, "x")])
        four = [lax.dynamic_index_in_dim(four, tensor ^ t, 0, keepdims=False) for t in range(n_tensor)]
        spot = jnp.concatenate([part[:PLACE_ROWS, :rows] for part in four])
        grad_place = spot[:patch_count]
        grad_table = spot[200:207]
        grad_expand_shift = small[PLACE_ROWS : PLACE_ROWS + 1, :rows]
        grad_entry_shift = small[PLACE_ROWS + 1 : PLACE_ROWS + 3, : entry_bias.shape[2]][:, None, :]
    else:
        def total(outs):
            turned = jnp.concatenate([out.astype(SINGLE) for out in outs])
            turned = jnp.concatenate(
                [lax.dynamic_index_in_dim(turned, tensor ^ t, 0) for t in range(n_tensor)]
            )
            mine = lax.psum_scatter(turned, "tensor", scatter_dimension=0, tiled=True)[0]
            return lax.psum_scatter(mine, "dp", scatter_dimension=0, tiled=True)

        reduced = total(grad_reduce).T
        expanded = total(grad_expand)
        attn = total(grad_attn)
        spot, entry_part, expand_part = small_grads
        spot = lax.psum(lax.psum_scatter(spot, "dp", scatter_dimension=1, tiled=True), "tensor")
        grad_place = spot[:patch_count]
        grad_table = spot[200:207]
        share = lambda array, axis: lax.psum_scatter(
            lax.psum_scatter(array, "tensor", scatter_dimension=0, tiled=True)[0],
            "dp",
            scatter_dimension=axis,
            tiled=True,
        )
        grad_expand_shift = share(expand_part, 1)
        ends = [share(entry_part[:, :, first : first + columns], 1) for first in (0, 2 * columns)]
        grad_entry_shift = jnp.stack(ends)

    grad_entry = jnp.stack([attn[:, j * columns : (j + 1) * columns] for j in range(3)])
    grad_exit = attn[:, 3 * columns :].T

    entry = adamw(entry_weight, entry_moment, entry_second, grad_entry, 0.05, 0.05)
    entry_b = adamw(entry_bias, entry_bias_moment, entry_bias_second, grad_entry_shift, 0.3, 0.0)
    exits = adamw(exit_weight, exit_moment, exit_second, grad_exit, 0.05, 0.05)
    expand = adamw(expand_weight, expand_moment, expand_second, expanded, 0.05, 0.05)
    expand_b = adamw(expand_bias, expand_bias_moment, expand_bias_second, grad_expand_shift, 0.3, 0.0)
    reduce_w = adamw(reduce_weight, reduce_moment, reduce_second, reduced, 0.05, 0.05)
    table_new = adamw(vectors, vectors_moment, vectors_second, grad_table, 0.3, 0.0)
    place_new = adamw(position, position_moment, position_second, grad_place, 0.1, 0.0)
    return (block_out, patch_grad, *entry, *entry_b, *exits, *expand, *expand_b, *reduce_w, *table_new, *place_new)


def solution(mesh):
    images = P("dp", None, None)
    entry = P(None, "dp", "tensor")
    entry_bias = P(None, "tensor", "dp")
    outer = P("tensor", "dp")
    expand = P("dp", "tensor")
    table = P(None, "dp")
    weights = (entry, entry_bias, outer, expand, outer, outer, table, table)
    placed = (images, images, P("dp", None), P("dp"), P("dp"))
    placed += tuple(spec for spec in weights for _ in range(3))
    given = (images, images) + tuple(spec for spec in weights for _ in range(4))
    sizes = (mesh.shape["dp"], mesh.shape["tensor"])
    return jax.shard_map(
        functools.partial(local, sizes),
        mesh=mesh,
        in_specs=placed,
        out_specs=given,
        check_vma=False,
    )
```

time: 946 us -> 431 us (0.46)
  waiting for transfers between devices: 478 us -> 124 us
  blocking collectives: 197 us -> 0 us
  Pallas kernels: 0 us -> 137 us
  starting transfers between devices: 0.69 us -> 84.8 us
  matrix products: 77.9 us -> 0 us
  local copies, waits for them, and re-layouts: 97.7 us -> 49.1 us
  other arithmetic: 69.7 us -> 32.2 us
  between operations: 18.7 us -> 2.65 us
    psum x3 -> x0, waiting for transfers between devices: 162 us -> none  [the longest x1 88.6 us: local(): lax.psum(down_part.astype(jnp.bfloat16), 'tensor').astype(jnp.float32)]
    all_gather x5 -> x0, blocking collectives: 156 us -> none  [the longest x1 35.5 us: local(): lax.all_gather(entry_weight.astype(half), 'dp', axis=1, tiled=True)]
    reduce_scatter x2 -> x0, waiting for transfers between devices: 140 us -> none  [the longest x1 70.3 us: local(): lax.psum_scatter(grad_expand, 'dp', scatter_dimension=0, tiled=True)]
    pallas_call x0 -> x10, Pallas kernels: none -> 137 us  [kernel_call(): pl.pallas_call(body, out_shape=[a for a, _ in outs], in_specs=[spec for _...]
    unnamed x17 -> x0, waiting for transfers between devices: 136 us -> none
    ppermute x0 -> x104, waiting for transfers between devices: none -> 124 us  [flip(): return lax.ppermute(array, axis, [(i, i ^ bits) for i in range(count)])]
    ppermute x0 -> x104, starting transfers between devices: none -> 84.8 us  [flip(): return lax.ppermute(array, axis, [(i, i ^ bits) for i in range(count)])]
    dot_general x16 -> x0, matrix products: 71.8 us -> none  [the longest x1 15.3 us: local(): jnp.dot(normed_two, w_expand, preferred_element_type=single)]
  transfers between devices with their start and end apart: 12 -> 104, of which waited for: 9 -> 33; matrix products, arithmetic and copies ran while one was open for 12% -> 16% of each run, Pallas kernels for 0% -> 9%
where the time goes in v1:
time: 431 us; the launch traced here: 430 us
  Pallas kernels  137 us (32%)
  waiting for transfers between devices  124 us (29%)
  starting transfers between devices  84.8 us (20%)
  local copies, waits for them, and re-layouts  49.1 us (11%)
  other arithmetic  32.2 us (7%)
    pallas_call x10, Pallas kernels, kernel_call(): pl.pallas_call(body, out_shape=[a for a, _ in outs], in_specs=[spec for _...  137 us
    ppermute x104, waiting for transfers between devices, flip(): return lax.ppermute(array, axis, [(i, i ^ bits) for i in range(count)])  124 us
    ppermute x104, starting transfers between devices, flip(): return lax.ppermute(array, axis, [(i, i ^ bits) for i in range(count)])  84.8 us
    unnamed x194, local copies, waits for them, and re-layouts  31.2 us
    convert_element_type x27, other arithmetic, add(): return (left.astype(SINGLE) + right.astype(SINGLE)).astype(HALF)  18.2 us
    ppermute x6, local copies, waits for them, and re-layouts, flip(): return lax.ppermute(array, axis, [(i, i ^ bits) for i in range(count)])  9.64 us
  transfers between devices with their start and end apart: 104, of which 33 were waited for; matrix products, arithmetic and copies ran while one was open for 16% of the time, Pallas kernels for 9%

profile of v1, /device:TPU:0, one launch (start us, length us, event | category | flops | bytes accessed | tf_op | source)
XLA Modules:
  0.0 429.7 jit_solution(16049418386186480769)
XLA Ops:
  4.2 3.1 collective-permute-start
  26.3 3.6 collective-permute-done.10
  32.2 5.7 %collective-permute-done.27 = bf16[96,768]{1,0:T(8,128)(2,1)S(1)} collective-permute-done((bf16[96,768]{1,0:T(8,128)(2,1)S(1)}, bf16[96,768]{1,0:T(8,128)(2,1)S(1)}, u32[]{:S(2)}, u32[]{:S(2)}) %collective-permute-start.27) | collective-permute-done | bytes 147488 | tf_op jit(solution)/shard_map/ppermute | solution.py:69
  41.8 10.2 %collective-permute-done.7.rest_1_ = bf16[2,96,768]{2,1,0:T(8,128)(2,1)} collective-permute-done((bf16[2,96,768]{2,1,0:T(8,128)(2,1)S(1)}, bf16[2,96,768]{2,1,0:T(8,128)(2,1)}, u32[]{:S(2)}, u32[]{:S(2)}) %collective-permute-start.7) | collective-permute-done | bytes 294944 | tf_op jit(solution)/shard_map/ppermute | solution.py:69
  63.2 3.2 collective-permute-done.30.rest_6_
  69.0 4.3 collective-permute-done.14.rest_7_
  88.7 9.2 %start.1 = (f32[416,768]{1,0:T(8,128)}, bf16[416,768]{1,0:T(8,128)(2,1)}, bf16[416,768]{1,0:T(8,128)(2,1)}, f32[8,768]{1,0:T(8,128)}, f32[4,1,576]{2,1,0:T(1,128)}, /*index=5*/f32[4,1,768]{2,1,0:T(1,128)}) custom-call(s32[2]{0:T(128)} %pad_add_fusion.place_ref, bf16[8,196,768]{2,1,0:T(8,128)(2,1)} %copy.171.patch_ref, bf16[8,196,768]{2,1,0:T(8,128)(2,1)} %copy.172.cot_ref, ...), custom_call_target="tpu_custom_call" | custom-call | bytes 8075920 | tf_op jit(solution)/shard_map/start/pallas_call | solution.py:47
  97.9 14.6 %attend.1 = (bf16[4,416,576]{2,1,0:T(8,128)(2,1)}, bf16[4,6,208,208]{3,2,1,0:T(8,128)(2,1)}, bf16[4,416,192]{2,1,0:T(8,128)(2,1)}, bf16[4,768,768]{2,1,0:T(8,128)(2,1)}) custom-call(s32[2]{0:T(128)} %pad_add_fusion.place_ref, bf16[416,768]{1,0:T(8,128)(2,1)} %get-tuple-element.85.normed_ref, f32[4,1,576]{2,1,0:T(1,128)} %get-tuple-element.86.bias_ref, ...), custom_call_target="tpu_custom_call" | custom-call | flops 2944401408 | bytes 14717960 | tf_op jit(solution)/shard_map/attend/pallas_call | solution.py:47
  113.7 26.1 %up.1 = (f32[416,768]{1,0:T(8,128)}, bf16[416,768]{1,0:T(8,128)(2,1)}, bf16[4,416,768]{2,1,0:T(8,128)(2,1)}, bf16[4,416,768]{2,1,0:T(8,128)(2,1)}, bf16[4,768,76...) custom-call(s32[2]{0:T(128)} %pad_add_fusion.place_ref, ...), custom_call_target="tpu_custom_call" | custom-call | flops 5888802816 | bytes 28495880 | tf_op jit(solution)/shard_map/up/pallas_call | solution.py:47
  144.9 14.1 %collective-permute-done.93 = bf16[4,96,768]{2,1,0:T(8,128)(2,1)S(1)} collective-permute-done((bf16[4,96,768]{2,1,0:T(8,128)(2,1)S(1)}, bf16[4,96,768]{2,1,0:T(8,128)(2,1)S(1)}, u32[]{:S(2)}, u32[]{:S(2)}) %collective-permute-start.93) | collective-permute-done | bytes 589856 | tf_op jit(solution)/shard_map/ppermute | solution.py:69
  161.5 6.1 %collective-permute-done.94 = bf16[2,96,768]{2,1,0:T(8,128)(2,1)S(1)} collective-permute-done((bf16[2,96,768]{2,1,0:T(8,128)(2,1)S(1)}, bf16[2,96,768]{2,1,0:T(8,128)(2,1)S(1)}, u32[]{:S(2)}, u32[]{:S(2)}) %collective-permute-start.94) | collective-permute-done | bytes 294944 | tf_op jit(solution)/shard_map/ppermute | solution.py:69
  168.7 3.1 collective-permute-start.100
  174.5 7.5 %collective-permute-done.100 = bf16[96,768]{1,0:T(8,128)(2,1)S(1)} collective-permute-done((bf16[96,768]{1,0:T(8,128)(2,1)S(1)}, bf16[96,768]{1,0:T(8,128)(2,1)S(1)}, u32[]{:S(2)}, u32[]{:S(2)}) %collective-permute-start.100) | collective-permute-done | bytes 147488 | tf_op jit(solution)/shard_map/ppermute | solution.py:69
  183.2 3.9 collective-permute-start.44
  187.8 8.8 %collective-permute-done.44 = bf16[96,768]{1,0:T(8,128)(2,1)S(1)} collective-permute-done((bf16[96,768]{1,0:T(8,128)(2,1)S(1)}, bf16[96,768]{1,0:T(8,128)(2,1)S(1)}, u32[]{:S(2)}, u32[]{:S(2)}) %collective-permute-start.44) | collective-permute-done | bytes 147488 | tf_op jit(solution)/shard_map/ppermute | solution.py:69
  200.9 5.7 %collective-permute-done.46.rest_5_ = bf16[2,96,768]{2,1,0:T(8,128)(2,1)S(1)} collective-permute-done((bf16[2,96,768]{2,1,0:T(8,128)(2,1)S(1)}, bf16[2,96,768]{2,1,0:T(8,128)(2,1)S(1)}, u32[]{:S(2)}, u32[]{:S(2)}) %collective-permute-start.46) | collective-permute-done | bytes 294944 | tf_op jit(solution)/shard_map/ppermute | solution.py:69
  208.8 5.8 %collective-permute-done.41.rest_1_ = bf16[2,96,768]{2,1,0:T(8,128)(2,1)S(1)} collective-permute-done((bf16[2,96,768]{2,1,0:T(8,128)(2,1)S(1)}, bf16[2,96,768]{2,1,0:T(8,128)(2,1)S(1)}, u32[]{:S(2)}, u32[]{:S(2)}) %collective-permute-start.41) | collective-permute-done | bytes 294944 | tf_op jit(solution)/shard_map/ppermute | solution.py:69
  215.5 3.8 collective-permute-done.48.rest_7_
  223.7 17.9 %down.1 = (bf16[4,416,768]{2,1,0:T(8,128)(2,1)}, bf16[4,768,768]{2,1,0:T(8,128)(2,1)}, f32[4,8,768]{2,1,0:T(8,128)}, bf16[4,96,768]{2,1,0:T(8,128)(2,1)}, bf16[4...) custom-call(s32[2]{0:T(128)} %pad_add_fusion.place_ref, ...), custom_call_target="tpu_custom_call" | custom-call | flops 4907335680 | bytes 20643848 | tf_op jit(solution)/shard_map/down/pallas_call | solution.py:47
  241.6 17.6 %middle.1 = (f32[416,768]{1,0:T(8,128)}, bf16[416,768]{1,0:T(8,128)(2,1)}, bf16[4,416,192]{2,1,0:T(8,128)(2,1)}, f32[4,8,768]{2,1,0:T(8,128)}) custom-call(bf16[4,416,768]{2,1,0:T(8,128)(2,1)} %get-tuple-element.99.grad_upper_ref, bf16[4,768,768]{2,1,0:T(8,128)(2,1)} %get-tuple-element.100.expand_ref, bf16[4,768,768]{2,1,0:T(8,128)(2,1)} %get-tuple-element.88.full_ref, ...), custom_call_target="tpu_custom_call" | custom-call | flops 2944401408 | bytes 16588800 | tf_op jit(solution)/shard_map/middle/pallas_call | solution.py:47
  259.3 21.5 %attend_back.1 = (bf16[4,416,576]{2,1,0:T(8,128)(2,1)}, f32[4,8,576]{2,1,0:T(8,128)}, bf16[4,96,768]{2,1,0:T(8,128)(2,1)}, bf16[4,96,768]{2,1,0:T(8,128)(2,1)}, ...) custom-call(s32[2]{0:T(128)} %pad_add_fusion.place_ref, ...), custom_call_target="tpu_custom_call" | custom-call | flops 7851737088 | bytes 13258760 | tf_op jit(solution)/shard_map/attend_back/pallas_call | solution.py:47
  280.8 15.7 %end.1 = (bf16[2,196,768]{2,1,0:T(8,128)(2,1)}, f32[32,80,128]{2,1,0:T(8,128)}) custom-call(s32[2]{0:T(128)} %pad_add_fusion.place_ref, bf16[4,416,576]{2,1,0:T(8,128)(2,1)} %get-tuple-element.103.grad_qkv_ref, bf16[4,768,768]{2,1,0:T(8,128)(2,1)} %get-tuple-element.88.full_ref, f32[416,768]{1,0:T(8,128)} %get-tuple-element.84.start_ref, ...), custom_call_target="tpu_custom_call" | custom-call | flops 1962934272 | bytes 11400840 | tf_op jit(solution)/shard_map/end/pallas_call | solution.py:47
  306.8 7.6 %output.1.own_ref = bf16[2,196,768]{2,1,0:T(8,128)(2,1)} custom-call(f32[2]{0:T(128)} %compare_convert_fusion.live_ref, f32[416,768]{1,0:T(8,128)} %get-tuple-element.92.middle_ref, bf16[4,416,768]{2,1,0:T(8,128)(2,1)} %get-tuple-element.93.active_ref, bf16[4,768,768]{2,1,0:T(8,128)(2,1)} %get-tuple-element.96.reduce_ref, f32[8,768]{1,0:T(8,128)} %get-tuple-element.90.table_ref), custom_call_target="tpu_custom_call" | custom-call | flops 1962934272 | bytes 9179144 | tf_op jit(solution)/shard_map/output/pallas_call | solution.py:47
  321.1 3.5 collective-permute-start.77
  342.8 3.4 collective-permute-done.58
  356.6 4.2 collective-permute-done.82
  365.8 6.3 %collective-permute-done.65 = bf16[4,96,768]{2,1,0:T(8,128)(2,1)} collective-permute-done((bf16[4,96,768]{2,1,0:T(8,128)(2,1)}, bf16[4,96,768]{2,1,0:T(8,128)(2,1)}, u32[]{:S(2)}, u32[]{:S(2)}) %collective-permute-start.65) | collective-permute-done | bytes 589856 | tf_op jit(solution)/shard_map/ppermute | solution.py:69
  381.2 3.3 spread.3
  384.4 3.6 copy.199
  389.9 3.3 spread.2
  393.2 3.6 copy.198
  410.9 10.6 %collective-permute-done.72 = bf16[96,768]{1,0:T(8,128)(2,1)S(1)} collective-permute-done((bf16[96,768]{1,0:T(8,128)(2,1)S(1)}, bf16[96,768]{1,0:T(8,128)(2,1)S(1)}, u32[]{:S(2)}, u32[]{:S(2)}) %collective-permute-start.72) | collective-permute-done | bytes 147488 | tf_op jit(solution)/shard_map/ppermute | solution.py:69
  (477 shorter events, 166.2 us)
Async XLA Ops:
  12.0 17.9 %collective-permute-start.10 = (bf16[96,768]{1,0:T(8,128)(2,1)S(1)}, bf16[96,768]{1,0:T(8,128)(2,1)S(1)}, u32[]{:S(2)}, u32[]{:S(2)}) collective-permute-start(bf16[96,768]{1,0:T(8,128)(2,1)S(1)} %pad_maximum_fusion.8), channel_id=1, source_target_pairs={{0,16},{4,20},{8,24},{12,28},{16,0},{20,4},{24,8},{28,12},{1,17},{... | collective-permute-start | bytes 442376 | tf_op jit(solution)/shard_map/ppermute | solution.py:69
  14.0 16.0 %collective-permute-start.11 = (bf16[96,768]{1,0:T(8,128)(2,1)S(1)}, bf16[96,768]{1,0:T(8,128)(2,1)S(1)}, u32[]{:S(2)}, u32[]{:S(2)}) collective-permute-start(bf16[96,768]{1,0:T(8,128)(2,1)S(1)} %pad_maximum_fusion.8), channel_id=1, source_target_pairs={{0,24},{4,28},{8,16},{12,20},{16,8},{20,12},{24,0},{28,4},{1,25},{... | collective-permute-start | bytes 442376 | tf_op jit(solution)/shard_map/ppermute | solution.py:69
  17.2 20.7 %collective-permute-start.27 = (bf16[96,768]{1,0:T(8,128)(2,1)S(1)}, bf16[96,768]{1,0:T(8,128)(2,1)S(1)}, u32[]{:S(2)}, u32[]{:S(2)}) collective-permute-start(bf16[96,768]{1,0:T(8,128)(2,1)S(1)} %convert_element_type.432), channel_id=1, source_target_pairs={{0,16},{4,20},{8,24},{12,28},{16,0},{20,4},{24,8},{28,12},{1,17},{... | collective-permute-start | bytes 442376 | tf_op jit(solution)/shard_map/ppermute | solution.py:69
  23.6 15.8 %collective-permute-start.28 = (bf16[96,768]{1,0:T(8,128)(2,1)S(1)}, bf16[96,768]{1,0:T(8,128)(2,1)S(1)}, u32[]{:S(2)}, u32[]{:S(2)}) collective-permute-start(bf16[96,768]{1,0:T(8,128)(2,1)S(1)} %convert_element_type.432), channel_id=1, source_target_pairs={{0,24},{4,28},{8,16},{12,20},{16,8},{20,12},{24,0},{28,4},{1,25},{... | collective-permute-start | bytes 442376 | tf_op jit(solution)/shard_map/ppermute | solution.py:69
  40.1 16.1 %collective-permute-start.8 = (bf16[2,96,768]{2,1,0:T(8,128)(2,1)S(1)}, bf16[2,96,768]{2,1,0:T(8,128)(2,1)}, u32[]{:S(2)}, u32[]{:S(2)}) collective-permute-start(bf16[2,96,768]{2,1,0:T(8,128)(2,1)S(1)} %pad_maximum_fusion.rest_0_), channel_id=1, source_target_pairs={{0,2},{1,3},{2,0},{3,1},{4,6},{5,7},{6,4},{7,5},{8,10},{9,11},{10,... | collective-permute-start | bytes 884744 | tf_op jit(solution)/shard_map/ppermute | solution.py:69
  85.5 27.0 %collective-permute-start.33 = (bf16[2,96,768]{2,1,0:T(8,128)(2,1)S(1)}, bf16[2,96,768]{2,1,0:T(8,128)(2,1)S(1)}, u32[]{:S(2)}, u32[]{:S(2)}) collective-permute-start(bf16[2,96,768]{2,1,0:T(8,128)(2,1)S(1)} %copy-done.55), channel_id=1, source_target_pairs={{0,1},{1,0},{2,3},{3,2},{4,5},{5,4},{6,7},{7,6},{8,9},{9,8},{10,11... | collective-permute-start | bytes 884744 | tf_op jit(solution)/shard_map/ppermute | solution.py:69
  85.8 26.8 %collective-permute-start.38 = (bf16[2,96,768]{2,1,0:T(8,128)(2,1)S(1)}, bf16[2,96,768]{2,1,0:T(8,128)(2,1)S(1)}, u32[]{:S(2)}, u32[]{:S(2)}) collective-permute-start(bf16[2,96,768]{2,1,0:T(8,128)(2,1)S(1)} %copy-done.58), channel_id=1, source_target_pairs={{0,1},{1,0},{2,3},{3,2},{4,5},{5,4},{6,7},{7,6},{8,9},{9,8},{10,11... | collective-permute-start | bytes 884744 | tf_op jit(solution)/shard_map/ppermute | solution.py:69
  87.3 25.3 %collective-permute-start.34 = (bf16[2,96,768]{2,1,0:T(8,128)(2,1)S(1)}, bf16[2,96,768]{2,1,0:T(8,128)(2,1)S(1)}, u32[]{:S(2)}, u32[]{:S(2)}) collective-permute-start(bf16[2,96,768]{2,1,0:T(8,128)(2,1)S(1)} %copy-done.62), channel_id=1, source_target_pairs={{0,1},{1,0},{2,3},{3,2},{4,5},{5,4},{6,7},{7,6},{8,9},{9,8},{10,11... | collective-permute-start | bytes 884744 | tf_op jit(solution)/shard_map/ppermute | solution.py:69
  87.4 25.3 %collective-permute-start.39 = (bf16[2,96,768]{2,1,0:T(8,128)(2,1)}, bf16[2,96,768]{2,1,0:T(8,128)(2,1)S(1)}, u32[]{:S(2)}, u32[]{:S(2)}) collective-permute-start(bf16[2,96,768]{2,1,0:T(8,128)(2,1)} %collective-permute-done.31.rest_7_), channel_id=1, source_target_pairs={{0,1},{1,0},{2,3},{3,2},{4,5},{5,4},{6,7},{7,6},{8,9},{9,8},{10,11... | collective-permute-start | bytes 884744 | tf_op jit(solution)/shard_map/ppermute | solution.py:69
  87.9 24.8 %collective-permute-start.35 = (bf16[2,96,768]{2,1,0:T(8,128)(2,1)}, bf16[2,96,768]{2,1,0:T(8,128)(2,1)S(1)}, u32[]{:S(2)}, u32[]{:S(2)}) collective-permute-start(bf16[2,96,768]{2,1,0:T(8,128)(2,1)} %collective-permute-done.26.rest_3_), channel_id=1, source_target_pairs={{0,1},{1,0},{2,3},{3,2},{4,5},{5,4},{6,7},{7,6},{8,9},{9,8},{10,11... | collective-permute-start | bytes 884744 | tf_op jit(solution)/shard_map/ppermute | solution.py:69
  143.3 15.7 %collective-permute-start.93 = (bf16[4,96,768]{2,1,0:T(8,128)(2,1)S(1)}, bf16[4,96,768]{2,1,0:T(8,128)(2,1)S(1)}, u32[]{:S(2)}, u32[]{:S(2)}) collective-permute-start(bf16[4,96,768]{2,1,0:T(8,128)(2,1)S(1)} %add_convert_fusion.2), channel_id=1, source_target_pairs={{0,2},{1,3},{2,0},{3,1},{4,6},{5,7},{6,4},{7,5},{8,10},{9,11},{10,... | collective-permute-start | bytes 1769480 | tf_op jit(solution)/shard_map/ppermute | solution.py:69
  143.9 15.7 %collective-permute-start.96 = (bf16[4,96,768]{2,1,0:T(8,128)(2,1)S(1)}, bf16[4,96,768]{2,1,0:T(8,128)(2,1)S(1)}, u32[]{:S(2)}, u32[]{:S(2)}) collective-permute-start(bf16[4,96,768]{2,1,0:T(8,128)(2,1)S(1)} %copy-done.52), channel_id=1, source_target_pairs={{0,1},{1,0},{2,3},{3,2},{4,5},{5,4},{6,7},{7,6},{8,9},{9,8},{10,11... | collective-permute-start | bytes 1769480 | tf_op jit(solution)/shard_map/ppermute | solution.py:69
  144.2 15.7 %collective-permute-start.98 = (bf16[4,96,768]{2,1,0:T(8,128)(2,1)S(1)}, bf16[4,96,768]{2,1,0:T(8,128)(2,1)S(1)}, u32[]{:S(2)}, u32[]{:S(2)}) collective-permute-start(bf16[4,96,768]{2,1,0:T(8,128)(2,1)S(1)} %add_convert_fusion), channel_id=1, source_target_pairs={{0,4},{4,0},{8,12},{12,8},{16,20},{20,16},{24,28},{28,24},{1,5},{5... | collective-permute-start | bytes 1769480 | tf_op jit(solution)/shard_map/ppermute | solution.py:69
  304.0 33.4 %collective-permute-start.61 = (bf16[2,196,768]{2,0,1:T(2,128)(2,1)}, bf16[2,196,768]{2,0,1:T(2,128)(2,1)}, u32[]{:S(2)}, u32[]{:S(2)}) collective-permute-start(bf16[2,196,768]{2,0,1:T(2,128)(2,1)} %copy.181), channel_id=1, source_target_pairs={{0,2},{1,3},{2,0},{3,1},{4,6},{5,7},{6,4},{7,5},{8,10},{9,11},{10,... | collective-permute-start | bytes 1806344 | tf_op jit(solution)/shard_map/ppermute | solution.py:69
  305.6 28.8 %collective-permute-start.60 = (bf16[2,196,768]{2,0,1:T(2,128)(2,1)}, bf16[2,196,768]{2,0,1:T(2,128)(2,1)}, u32[]{:S(2)}, u32[]{:S(2)}) collective-permute-start(bf16[2,196,768]{2,0,1:T(2,128)(2,1)} %copy.181), channel_id=1, source_target_pairs={{0,1},{1,0},{2,3},{3,2},{4,5},{5,4},{6,7},{7,6},{8,9},{9,8},{10,11... | collective-permute-start | bytes 1806344 | tf_op jit(solution)/shard_map/ppermute | solution.py:69
  329.8 16.5 %collective-permute-start.58 = (bf16[2,196,768]{2,0,1:T(2,128)(2,1)S(1)}, bf16[2,196,768]{2,0,1:T(2,128)(2,1)S(1)}, u32[]{:S(2)}, u32[]{:S(2)}) collective-permute-start(bf16[2,196,768]{2,0,1:T(2,128)(2,1)S(1)} %copy.175), channel_id=1, source_target_pairs={{0,2},{1,3},{2,0},{3,1},{4,6},{5,7},{6,4},{7,5},{8,10},{9,11},{10,... | collective-permute-start | bytes 1806344 | tf_op jit(solution)/shard_map/ppermute | solution.py:69
  332.9 15.8 %collective-permute-start.103 = (f32[2,80,128]{2,1,0:T(8,128)S(1)}, f32[2,80,128]{2,1,0:T(8,128)S(1)}, u32[]{:S(2)}, u32[]{:S(2)}) collective-permute-start(f32[2,80,128]{2,1,0:T(8,128)S(1)} %pad_maximum_fusion.13), channel_id=1, source_target_pairs={{0,2},{1,3},{2,0},{3,1},{4,6},{5,7},{6,4},{7,5},{8,10},{9,11},{10,... | collective-permute-start | bytes 245768 | tf_op jit(solution)/shard_map/ppermute | solution.py:69
  334.5 26.3 %collective-permute-start.82 = (bf16[4,96,768]{2,1,0:T(8,128)(2,1)}, bf16[4,96,768]{2,1,0:T(8,128)(2,1)}, u32[]{:S(2)}, u32[]{:S(2)}) collective-permute-start(bf16[4,96,768]{2,1,0:T(8,128)(2,1)} %add_convert_fusion.6), channel_id=1, source_target_pairs={{0,2},{1,3},{2,0},{3,1},{4,6},{5,7},{6,4},{7,5},{8,10},{9,11},{10,... | collective-permute-start | bytes 1769480 | tf_op jit(solution)/shard_map/ppermute | solution.py:69
  337.4 25.1 %collective-permute-start.87 = (bf16[4,96,768]{2,1,0:T(8,128)(2,1)}, bf16[4,96,768]{2,1,0:T(8,128)(2,1)}, u32[]{:S(2)}, u32[]{:S(2)}) collective-permute-start(bf16[4,96,768]{2,1,0:T(8,128)(2,1)} %add_convert_fusion.4), channel_id=1, source_target_pairs={{0,4},{4,0},{8,12},{12,8},{16,20},{20,16},{24,28},{28,24},{1,5},{5... | collective-permute-start | bytes 1769480 | tf_op jit(solution)/shard_map/ppermute | solution.py:69
  340.9 31.2 %collective-permute-start.65 = (bf16[4,96,768]{2,1,0:T(8,128)(2,1)}, bf16[4,96,768]{2,1,0:T(8,128)(2,1)}, u32[]{:S(2)}, u32[]{:S(2)}) collective-permute-start(bf16[4,96,768]{2,1,0:T(8,128)(2,1)} %add_convert_fusion.10), channel_id=1, source_target_pairs={{0,2},{1,3},{2,0},{3,1},{4,6},{5,7},{6,4},{7,5},{8,10},{9,11},{10,... | collective-permute-start | bytes 1769480 | tf_op jit(solution)/shard_map/ppermute | solution.py:69
  346.3 28.3 %collective-permute-start.70 = (bf16[4,96,768]{2,1,0:T(8,128)(2,1)}, bf16[4,96,768]{2,1,0:T(8,128)(2,1)}, u32[]{:S(2)}, u32[]{:S(2)}) collective-permute-start(bf16[4,96,768]{2,1,0:T(8,128)(2,1)} %add_convert_fusion.8), channel_id=1, source_target_pairs={{0,4},{4,0},{8,12},{12,8},{16,20},{20,16},{24,28},{28,24},{1,5},{5... | collective-permute-start | bytes 1769480 | tf_op jit(solution)/shard_map/ppermute | solution.py:69
  348.7 28.7 %collective-permute-start.62 = (bf16[2,196,768]{2,0,1:T(2,128)(2,1)}, bf16[2,196,768]{2,0,1:T(2,128)(2,1)}, u32[]{:S(2)}, u32[]{:S(2)}) collective-permute-start(bf16[2,196,768]{2,0,1:T(2,128)(2,1)} %collective-permute-done.61), channel_id=1, source_target_pairs={{0,1},{1,0},{2,3},{3,2},{4,5},{5,4},{6,7},{7,6},{8,9},{9,8},{10,11... | collective-permute-start | bytes 1806344 | tf_op jit(solution)/shard_map/ppermute | solution.py:69
  360.8 27.2 %collective-permute-start.59 = (bf16[2,196,768]{2,0,1:T(2,128)(2,1)S(1)}, bf16[2,196,768]{2,0,1:T(2,128)(2,1)}, u32[]{:S(2)}, u32[]{:S(2)}) collective-permute-start(bf16[2,196,768]{2,0,1:T(2,128)(2,1)S(1)} %collective-permute-done.58), channel_id=1, source_target_pairs={{0,1},{1,0},{2,3},{3,2},{4,5},{5,4},{6,7},{7,6},{8,9},{9,8},{10,11... | collective-permute-start | bytes 1806344 | tf_op jit(solution)/shard_map/ppermute | solution.py:69
  362.5 34.2 %collective-permute-start.83 = (bf16[2,96,768]{2,1,0:T(8,128)(2,1)}, bf16[2,96,768]{2,1,0:T(8,128)(2,1)}, u32[]{:S(2)}, u32[]{:S(2)}) collective-permute-start(bf16[2,96,768]{2,1,0:T(8,128)(2,1)} %add_convert_fusion.23), channel_id=1, source_target_pairs={{0,4},{4,0},{8,12},{12,8},{16,20},{20,16},{24,28},{28,24},{1,5},{5... | collective-permute-start | bytes 884744 | tf_op jit(solution)/shard_map/ppermute | solution.py:69
  372.1 33.7 %collective-permute-start.88 = (bf16[2,96,768]{2,1,0:T(8,128)(2,1)}, bf16[2,96,768]{2,1,0:T(8,128)(2,1)}, u32[]{:S(2)}, u32[]{:S(2)}) collective-permute-start(bf16[2,96,768]{2,1,0:T(8,128)(2,1)} %add_convert_fusion.20), channel_id=1, source_target_pairs={{0,2},{1,3},{2,0},{3,1},{4,6},{5,7},{6,4},{7,5},{8,10},{9,11},{10,... | collective-permute-start | bytes 884744 | tf_op jit(solution)/shard_map/ppermute | solution.py:69
  374.5 24.4 %collective-permute-start.66 = (bf16[2,96,768]{2,1,0:T(8,128)(2,1)}, bf16[2,96,768]{2,1,0:T(8,128)(2,1)}, u32[]{:S(2)}, u32[]{:S(2)}) collective-permute-start(bf16[2,96,768]{2,1,0:T(8,128)(2,1)} %add_convert_fusion.29), channel_id=1, source_target_pairs={{0,4},{4,0},{8,12},{12,8},{16,20},{20,16},{24,28},{28,24},{1,5},{5... | collective-permute-start | bytes 884744 | tf_op jit(solution)/shard_map/ppermute | solution.py:69
  377.4 24.5 %collective-permute-start.71 = (bf16[2,96,768]{2,1,0:T(8,128)(2,1)}, bf16[2,96,768]{2,1,0:T(8,128)(2,1)}, u32[]{:S(2)}, u32[]{:S(2)}) collective-permute-start(bf16[2,96,768]{2,1,0:T(8,128)(2,1)} %add_convert_fusion.26), channel_id=1, source_target_pairs={{0,2},{1,3},{2,0},{3,1},{4,6},{5,7},{6,4},{7,5},{8,10},{9,11},{10,... | collective-permute-start | bytes 884744 | tf_op jit(solution)/shard_map/ppermute | solution.py:69
  398.6 27.3 %collective-permute-start.84 = (bf16[96,768]{1,0:T(8,128)(2,1)}, bf16[96,768]{1,0:T(8,128)(2,1)}, u32[]{:S(2)}, u32[]{:S(2)}) collective-permute-start(bf16[96,768]{1,0:T(8,128)(2,1)} %slice_bitcast_fusion.6), channel_id=1, source_target_pairs={{0,8},{4,12},{8,0},{12,4},{16,24},{20,28},{24,16},{28,20},{1,9},{5... | collective-permute-start | bytes 442376 | tf_op jit(solution)/shard_map/ppermute | solution.py:69
  403.1 18.4 %collective-permute-start.72 = (bf16[96,768]{1,0:T(8,128)(2,1)S(1)}, bf16[96,768]{1,0:T(8,128)(2,1)S(1)}, u32[]{:S(2)}, u32[]{:S(2)}) collective-permute-start(bf16[96,768]{1,0:T(8,128)(2,1)S(1)} %get-tuple-element.311), channel_id=1, source_target_pairs={{0,16},{4,20},{8,24},{12,28},{16,0},{20,4},{24,8},{28,12},{1,17},{... | collective-permute-start | bytes 442376 | tf_op jit(solution)/shard_map/ppermute | solution.py:69
  403.2 18.2 %collective-permute-start.73 = (bf16[96,768]{1,0:T(8,128)(2,1)S(1)}, bf16[96,768]{1,0:T(8,128)(2,1)S(1)}, u32[]{:S(2)}, u32[]{:S(2)}) collective-permute-start(bf16[96,768]{1,0:T(8,128)(2,1)S(1)} %get-tuple-element.312), channel_id=1, source_target_pairs={{0,24},{4,28},{8,16},{12,20},{16,8},{20,12},{24,0},{28,4},{1,25},{... | collective-permute-start | bytes 442376 | tf_op jit(solution)/shard_map/ppermute | solution.py:69
  407.8 19.8 %collective-permute-start.89 = (bf16[96,768]{1,0:T(8,128)(2,1)}, bf16[96,768]{1,0:T(8,128)(2,1)S(1)}, u32[]{:S(2)}, u32[]{:S(2)}) collective-permute-start(bf16[96,768]{1,0:T(8,128)(2,1)} %get-tuple-element.306), channel_id=1, source_target_pairs={{0,16},{4,20},{8,24},{12,28},{16,0},{20,4},{24,8},{28,12},{1,17},{... | collective-permute-start | bytes 442376 | tf_op jit(solution)/shard_map/ppermute | solution.py:69
  408.1 19.5 %collective-permute-start.90 = (bf16[96,768]{1,0:T(8,128)(2,1)}, bf16[96,768]{1,0:T(8,128)(2,1)S(1)}, u32[]{:S(2)}, u32[]{:S(2)}) collective-permute-start(bf16[96,768]{1,0:T(8,128)(2,1)} %get-tuple-element.307), channel_id=1, source_target_pairs={{0,24},{4,28},{8,16},{12,20},{16,8},{20,12},{24,0},{28,4},{1,25},{... | collective-permute-start | bytes 442376 | tf_op jit(solution)/shard_map/ppermute | solution.py:69
  (157 other events, 1296.7 us)

commit v2 on v1

v2 whole, which is shorter than its diff:
```python
import functools

import jax
import jax.numpy as jnp
from jax import lax
from jax.experimental import pallas as pl
from jax.experimental.pallas import tpu as pltpu
from jax.sharding import PartitionSpec as P

HEAD_DIM = 64
STEP = 7
NORM_EPS = 1e-06
HALF = jnp.bfloat16
SINGLE = jnp.float32
VMEM = pl.BlockSpec(memory_space=pltpu.VMEM)
SMEM = pl.BlockSpec(memory_space=pltpu.SMEM)
ANY = pl.BlockSpec(memory_space=pl.ANY)
CHUNK = 16
COST = 0.001
SMALL_ROWS = 80
PLACE_ROWS = 64


def adamw(master, moment, second, grad, rate, decay):
    moment = 0.9 * moment + 0.1 * grad
    second = 0.999 * second + 0.001 * grad * grad
    fixed_first = moment / (1.0 - 0.9**STEP)
    fixed_second = second / (1.0 - 0.999**STEP)
    master = master - rate * (fixed_first / (jnp.sqrt(fixed_second) + 1e-08) + decay * master)
    return (master, moment, second, master.astype(jnp.bfloat16))


def dot(left, right):
    return jnp.dot(left, right, preferred_element_type=SINGLE)


def row_dot(left, right):
    return lax.dot_general(left, right, (((1,), (1,)), ((), ())), preferred_element_type=SINGLE)


def column_dot(left, right):
    return lax.dot_general(left, right, (((0,), (0,)), ((), ())), preferred_element_type=SINGLE)


def kernel_call(body, outs, operands, scratch, microseconds, name):
    flops = int(microseconds * 1e9 * COST)
    moved = 1024
    return pl.pallas_call(
        body,
        out_shape=[a for a, _ in outs],
        in_specs=[spec for _, spec in operands],
        out_specs=[spec for _, spec in outs],
        scratch_shapes=scratch,
        cost_estimate=pl.CostEstimate(flops=flops, bytes_accessed=moved, transcendentals=0),
        name=name,
    )(*[a for a, _ in operands])


def shape(dims, kind):
    return jax.ShapeDtypeStruct(dims, kind)


def add(*parts):
    total = parts[0].astype(SINGLE)
    for part in parts[1:]:
        total = total + part.astype(SINGLE)
    return total.astype(HALF)


def after(value, *others):
    return lax.optimization_barrier((value, *others))[0]


class Swap:
    def __init__(self, n_dp, n_tensor):
        self.n_dp = n_dp
        self.n_tensor = n_tensor

    def flip(self, array, axis, bits):
        count = self.n_dp if axis == "dp" else self.n_tensor
        return lax.ppermute(array, axis, [(i, i ^ bits) for i in range(count)])

    def along(self, array, name):
        axis, bits = {
            "core": ("tensor", 1),
            "x": ("tensor", 2),
            "y": ("dp", 1),
            "z1": ("dp", 2),
            "z2": ("dp", 4),
            "z3": ("dp", 6),
        }[name]
        return self.flip(array, axis, bits)

    def gather_line(self, shard):
        first = jnp.stack([shard, self.along(shard, "z2")])
        return first, self.along(first, "z1")

    def gather_plane(self, first, last):
        first = jnp.concatenate([first, self.along(first, "y")])
        last = jnp.concatenate([last, self.along(last, "x")])
        first_x = self.along(first, "x")
        last_y = self.along(last, "y")
        return [
            (first, [(0, 0), (0, 4), (0, 1), (0, 5)]),
            (first_x, [(1, 0), (1, 4), (1, 1), (1, 5)]),
            (last, [(0, 2), (0, 6), (1, 2), (1, 6)]),
            (last_y, [(0, 3), (0, 7), (1, 3), (1, 7)]),
        ]

    def plane_first(self, shard):
        pair = jnp.stack([shard, self.along(shard, "x")])
        return jnp.concatenate([pair, self.along(pair, "y")])

    def line_last(self, four):
        eight = jnp.concatenate([four, self.along(four, "z2")])
        spots = lambda k: [(x, 2 * k + y) for y in (0, 1) for x in (0, 1)]
        return [(eight, spots(0) + spots(2)), (self.along(eight, "z1"), spots(1) + spots(3))]

    def grad_layout(self):
        layout = []
        for half, steps in enumerate(((0, 2), (1, 3))):
            for first in (0, 1):
                blocks = []
                for second in (0, 1):
                    x, y = (first, second) if half == 0 else (second, first)
                    for k in steps:
                        blocks.append((x, 2 * k + y))
                layout.append(blocks)
        return layout

    def reduce(self, outs):
        came_a = self.along(outs[1], "x")
        came_b = self.along(outs[3], "y")
        far_b = self.along(add(outs[2][2:], came_b[2:]), "x")
        far_a = self.along(add(outs[0][2:], came_a[2:]), "y")
        over = self.along(add(outs[2][:2], came_b[:2], far_b), "z1")
        parts = (outs[0], came_a, far_a, over)
        there = self.along(add(*[part[1] for part in parts]), "z2")
        return [part[0] for part in parts] + [there]

    def grad_layout_line(self):
        spots = lambda k: [(x, 2 * k + y) for y in (0, 1) for x in (0, 1)]
        return [spots(0), spots(2), spots(1) + spots(3)]

    def reduce_line(self, outs):
        came = self.along(outs[2], "z1")
        there = self.along(add(outs[1], came[4:]), "z2")
        parts = (outs[0], came[:4], there)
        over = self.along(add(*[part[2:] for part in parts]), "y")
        parts = (*parts, over)
        last = self.along(add(*[part[1] for part in parts]), "x")
        return [part[0] for part in parts] + [last]


def load_pieces(place_ref, piece_refs, spots, dst_ref, sems):
    copies = []
    for ref, where in zip(piece_refs, spots):
        for j, (pair_flip, dp_flip) in enumerate(where):
            if dp_flip is None:
                dst = dst_ref.at[pair_flip]
            else:
                rows = ref.shape[1]
                row = pl.multiple_of((place_ref[0] ^ dp_flip) * rows, rows)
                dst = dst_ref.at[pair_flip, pl.ds(row, rows), :]
            copies.append(pltpu.make_async_copy(ref.at[j], dst, sems.at[len(copies)]))
    for copy in copies:
        copy.start()
    return copies


def store_grads(place_ref, src_ref, out_refs, layout, rows, sems):
    copies = []
    for ref, where in zip(out_refs, layout):
        for j, (pair_flip, dp_flip) in enumerate(where):
            if dp_flip is None:
                src = src_ref.at[pair_flip]
            else:
                row = pl.multiple_of((place_ref[0] ^ dp_flip) * rows, rows)
                src = src_ref.at[pair_flip, pl.ds(row, rows), :]
            copies.append(pltpu.make_async_copy(src, ref.at[j], sems.at[len(copies)]))
    for copy in copies:
        copy.start()
    return copies


def wait_all(copies):
    for copy in copies:
        copy.wait()


def fold(rows):
    return rows[:8] + rows[8:]


def norm_scaled(rows):
    scale = 1.0 / rows.shape[-1]
    centered = rows - jnp.sum(rows, -1, keepdims=True) * scale
    inverse = lax.rsqrt(jnp.sum(centered * centered, -1, keepdims=True) * scale + NORM_EPS)
    return centered * inverse, inverse


def norm_grad(grad, scaled, inverse, gain):
    scale = 1.0 / grad.shape[-1]
    e = grad * gain
    mean_e = jnp.sum(e, -1, keepdims=True) * scale
    mean_cross = jnp.sum(e * scaled, -1, keepdims=True) * scale
    return inverse * (e - mean_e - scaled * mean_cross)


def over_rows(tokens, body, init):
    def one(j, carry):
        return body(pl.ds(pl.multiple_of(j * CHUNK, CHUNK), CHUNK), carry)

    return lax.fori_loop(0, tokens // CHUNK, one, init)


def small_slot(place_ref, t_at, dp_at):
    t_flip = place_ref[1] ^ t_at
    dp_flip = place_ref[0] ^ dp_at
    return (t_flip & 1) * 16 + (t_flip >> 1) * 8 + (dp_flip & 1) * 4 + (dp_flip >> 1)


def start_body(images, patches, pad, packed, place_ref, patch_ref, cot_ref, mask_ref, live_ref, *rest):
    if packed:
        (small_ref, start_ref, normed_ref, low_ref, table_ref, entry_ref, expand_ref, pair, both, spot, sems) = rest
    else:
        (spot, table_in, entry_in, expand_in, start_ref, normed_ref, low_ref, table_ref, entry_ref, expand_ref, pair, both, sems) = rest
    first = (place_ref[1] >> 1) * images
    copies = [
        pltpu.make_async_copy(patch_ref.at[pl.ds(first, images)], pair, sems.at[0]),
        pltpu.make_async_copy(cot_ref.at[pl.ds(first, images)], both, sems.at[1]),
    ]
    for copy in copies:
        copy.start()
    n_tensor = entry_ref.shape[0]
    columns = entry_ref.shape[2] // 3
    entry_ref[...] = jnp.zeros_like(entry_ref)
    if packed:
        n_dp = small_ref.shape[0] // n_tensor
        part = spot.shape[1] // n_dp
        own = part // n_tensor
        for dp_at in range(n_dp):
            for t_at in range(n_tensor):
                block = small_ref[small_slot(place_ref, t_at, dp_at)].astype(SINGLE)
                spot[PLACE_ROWS * t_at : PLACE_ROWS * (t_at + 1), part * dp_at : part * (dp_at + 1)] = block[:PLACE_ROWS, :part]
                bias = block[PLACE_ROWS : PLACE_ROWS + 8]
                expand_ref[t_at, :, part * dp_at : part * (dp_at + 1)] = bias[0:1, :part]
                entry_ref[t_at, :, own * dp_at : own * (dp_at + 1)] = bias[1:2, :own]
                entry_ref[t_at, :, 2 * columns + own * dp_at : 2 * columns + own * (dp_at + 1)] = bias[2:3, :own]
        table_ref[...] = spot[200:208, :]
    else:
        table_ref[...] = table_in[...]
        entry_ref[...] = entry_in[...]
        expand_ref[...] = expand_in[...]
    wait_all(copies)
    token = table_ref[6:7, :]
    empty = jnp.zeros((CHUNK, start_ref.shape[1]), SINGLE)
    for i in range(images):
        start_ref[(i + 1) * pad - CHUNK : (i + 1) * pad, :] = empty
        low_ref[(i + 1) * pad - CHUNK : (i + 1) * pad, :] = empty.astype(HALF)
        rows = pl.ds(i * pad, patches)
        picked = jnp.where(mask_ref[rows, :] > 0.5, token, pair[i].astype(SINGLE))
        start_ref[rows, :] = picked + spot[:patches, :]
        low_ref[rows, :] = (both[i].astype(SINGLE) * live_ref[i]).astype(HALF)
    gain, shift = table_ref[0:1, :], table_ref[1:2, :]

    def one(rows, carry):
        scaled, _ = norm_scaled(start_ref[rows, :])
        normed_ref[rows, :] = (scaled * gain + shift).astype(HALF)
        return carry

    over_rows(start_ref.shape[0], one, 0)


def attend_body(images, patches, pad, spots, place_ref, normed_ref, bias_ref, *rest):
    n = len(spots)
    piece_refs = rest[:n]
    qkv_ref, probs_ref, mixed_ref, branch_ref, full_ref, held, total, sems, out_sem = rest[n:]
    columns = mixed_ref.shape[2]
    heads = columns // HEAD_DIM
    wait_all(load_pieces(place_ref, piece_refs, spots, held, sems))
    out = pltpu.make_async_copy(held, full_ref, out_sem)
    out.start()
    lanes = lax.broadcasted_iota(jnp.int32, (pad, pad), 1)

    for b in range(held.shape[0]):
        qkv = dot(normed_ref[...], held[b, :, : 3 * columns]) + bias_ref[place_ref[1] ^ (2 * b)]
        qkv_ref[b] = qkv.astype(HALF)

        def one(i, carry):
            rows = pl.ds(pl.multiple_of(i * pad, CHUNK), pad)
            for h in range(heads):
                at = h * HEAD_DIM
                query = qkv_ref[b, rows, at : at + HEAD_DIM]
                keys = qkv_ref[b, rows, columns + at : columns + at + HEAD_DIM]
                values = qkv_ref[b, rows, 2 * columns + at : 2 * columns + at + HEAD_DIM]
                scores = row_dot(query, keys) * HEAD_DIM ** (-0.5)
                scores = jnp.where(lanes < patches, scores, -1e30)
                risen = jnp.exp(scores - jnp.max(scores, -1, keepdims=True))
                probs = (risen * (1.0 / jnp.sum(risen, -1, keepdims=True))).astype(HALF)
                probs_ref[b, i * heads + h] = probs
                mixed_ref[b, rows, at : at + HEAD_DIM] = dot(probs, values).astype(HALF)
            return carry

        lax.fori_loop(0, images, one, 0)
        part = row_dot(mixed_ref[b], held[b, :, 3 * columns :])
        if b == 0:
            total[...] = part
        elif b < held.shape[0] - 1:
            total[...] += part
        else:
            branch_ref[...] = (total[...] + part).astype(HALF)
    out.wait()


def up_body(spots, layout, rows_out, place_ref, start_ref, branch_ref, came_ref, low_ref, table_ref, bias_ref, *rest):
    n, m = len(spots), len(layout)
    piece_refs = rest[:n]
    middle_ref, normed_ref, active_ref, slope_ref, expand_ref = rest[n : n + 5]
    out_refs = rest[n + 5 : n + 5 + m]
    held, upper, grads, sems, out_sem, grad_sems = rest[n + 5 + m :]
    tokens = start_ref.shape[0]
    copies = load_pieces(place_ref, piece_refs, spots, held, sems)
    gain, shift, bias = table_ref[2:3, :], table_ref[3:4, :], table_ref[4:5, :]

    def one(rows, carry):
        branch = branch_ref[rows, :].astype(SINGLE) + came_ref[rows, :].astype(SINGLE)
        middle = start_ref[rows, :] + branch + bias
        middle_ref[rows, :] = middle
        scaled, _ = norm_scaled(middle)
        normed_ref[rows, :] = (scaled * gain + shift).astype(HALF)
        return carry

    over_rows(tokens, one, 0)
    wait_all(copies)
    out = pltpu.make_async_copy(held, expand_ref, out_sem)
    out.start()

    def up(b, carry):
        upper[...] = dot(normed_ref[...], held[b]) + bias_ref[place_ref[1] ^ (2 * b)]

        def bend(rows, inner):
            u = upper[rows, :]
            cdf = 0.5 * (1.0 + lax.erf(u * 0.7071067811865476))
            active_ref[b, rows, :] = (u * cdf).astype(HALF)
            slope = cdf + u * (jnp.exp(u * u * -0.5) * 0.3989422804014327)
            slope_ref[b, rows, :] = slope.astype(HALF)
            return inner

        over_rows(tokens, bend, 0)
        grads[b] = column_dot(low_ref[...], active_ref[b]).astype(HALF)
        return carry

    lax.fori_loop(0, held.shape[0], up, 0)
    wait_all(store_grads(place_ref, grads, out_refs, layout, rows_out, grad_sems))
    out.wait()


def down_body(spots, place_ref, low_ref, slope_ref, expand_ref, *rest):
    n = len(spots)
    piece_refs = rest[:n]
    grad_upper_ref, normed_grad_ref, reduce_ref, sums_ref, held, upper, total, sems, out_sem = rest[n:]
    tokens = low_ref.shape[0]
    wait_all(load_pieces(place_ref, piece_refs, spots, held, sems))
    out = pltpu.make_async_copy(held, reduce_ref, out_sem)
    out.start()
    for b in range(held.shape[0]):
        upper[...] = dot(low_ref[...], held[b])

        def bend(rows, sums):
            grad = (upper[rows, :] * slope_ref[b, rows, :].astype(SINGLE)).astype(HALF)
            grad_upper_ref[b, rows, :] = grad
            return sums + fold(grad.astype(SINGLE))

        sums_ref[b] = over_rows(tokens, bend, jnp.zeros((8, upper.shape[1]), SINGLE))
        part = row_dot(grad_upper_ref[b], expand_ref[b])
        if b == 0:
            total[...] = part
        elif b < held.shape[0] - 1:
            total[...] += part
        else:
            normed_grad_ref[...] = (total[...] + part).astype(HALF)
    out.wait()


def expand_body(layout, rows_out, place_ref, normed_ref, grad_upper_ref, *rest):
    out_refs = rest[: len(layout)]
    grads, grad_sems = rest[len(layout) :]

    def one(b, carry):
        grads[b] = column_dot(normed_ref[...], grad_upper_ref[b]).astype(HALF)
        return carry

    lax.fori_loop(0, grads.shape[0], one, 0)
    wait_all(store_grads(place_ref, grads, out_refs, layout, rows_out, grad_sems))


def back_body(images, pad, layout, rows_out, place_ref, normed_grad_ref, came_ref, middle_ref, low_ref, table_ref, full_ref, qkv_ref, probs_ref, normed_ref, mixed_ref, *rest):
    m = len(layout)
    grad_middle_ref, grad_qkv_ref, sums_two_ref, sums_entry_ref = rest[:4]
    out_refs = rest[4 : 4 + m]
    half, grad_mixed, grads, grad_sems = rest[4 + m :]
    blocks, tokens, columns = mixed_ref.shape
    heads = columns // HEAD_DIM
    scale = HEAD_DIM ** (-0.5)
    gain = table_ref[2:3, :]

    def one(rows, carry):
        scaled, inverse = norm_scaled(middle_ref[rows, :])
        grad = normed_grad_ref[rows, :].astype(SINGLE) + came_ref[rows, :].astype(SINGLE)
        low = low_ref[rows, :].astype(SINGLE)
        out = low + norm_grad(grad, scaled, inverse, gain)
        grad_middle_ref[rows, :] = out
        half[rows, :] = out.astype(HALF)
        parts = (grad * scaled, grad, out, low)
        return tuple(c + fold(p) for c, p in zip(carry, parts))

    zero = jnp.zeros((8, low_ref.shape[1]), SINGLE)
    totals = over_rows(tokens, one, (zero,) * 4)
    for row, total in enumerate(totals):
        sums_two_ref[row] = total

    for b in range(blocks):
        grad_mixed[...] = dot(half[...], full_ref[b, :, 3 * columns :]).astype(HALF)

        def attend(i, carry):
            rows = pl.ds(pl.multiple_of(i * pad, CHUNK), pad)
            for h in range(heads):
                at = h * HEAD_DIM
                query = qkv_ref[b, rows, at : at + HEAD_DIM]
                keys = qkv_ref[b, rows, columns + at : columns + at + HEAD_DIM]
                values = qkv_ref[b, rows, 2 * columns + at : 2 * columns + at + HEAD_DIM]
                grad = grad_mixed[rows, at : at + HEAD_DIM]
                low = probs_ref[b, i * heads + h]
                probs = low.astype(SINGLE)
                grad_qkv_ref[b, rows, 2 * columns + at : 2 * columns + at + HEAD_DIM] = column_dot(low, grad).astype(HALF)
                grad_probs = row_dot(grad, values)
                inner = jnp.sum(probs * grad_probs, -1, keepdims=True)
                grad_scores = (probs * (grad_probs - inner)).astype(HALF)
                grad_qkv_ref[b, rows, at : at + HEAD_DIM] = (dot(grad_scores, keys) * scale).astype(HALF)
                grad_qkv_ref[b, rows, columns + at : columns + at + HEAD_DIM] = (column_dot(grad_scores, query) * scale).astype(HALF)
            return carry

        lax.fori_loop(0, images, attend, 0)
        grads[b, :, : 3 * columns] = column_dot(normed_ref[...], grad_qkv_ref[b]).astype(HALF)
        grads[b, :, 3 * columns :] = column_dot(half[...], mixed_ref[b]).astype(HALF)

        def sums(rows, total):
            return total + fold(grad_qkv_ref[b, rows, :].astype(SINGLE))

        sums_entry_ref[b] = over_rows(tokens, sums, jnp.zeros((8, 3 * columns), SINGLE))
    wait_all(store_grads(place_ref, grads, out_refs, layout, rows_out, grad_sems))


def normed_body(place_ref, grad_qkv_ref, full_ref, keep_ref, send_ref, total):
    blocks = grad_qkv_ref.shape[0]
    width = grad_qkv_ref.shape[2]
    total[...] = row_dot(grad_qkv_ref[0], full_ref[0, :, :width])
    for b in range(1, blocks):
        total[...] += row_dot(grad_qkv_ref[b], full_ref[b, :, :width])
    count = keep_ref.shape[0]
    core = place_ref[1] & 1
    keep_ref[...] = total[pl.ds(pl.multiple_of(core * count, count), count), :]
    send_ref[...] = total[pl.ds(pl.multiple_of((1 - core) * count, count), count), :].astype(HALF)


def output_body(place_ref, middle_ref, active_ref, reduce_ref, table_ref, keep_ref, send_ref, total):
    total[...] = row_dot(active_ref[0], reduce_ref[0])
    for b in range(1, active_ref.shape[0]):
        total[...] += row_dot(active_ref[b], reduce_ref[b])
    count = keep_ref.shape[0]
    core = place_ref[1] & 1
    rows = pl.ds(pl.multiple_of(core * count, count), count)
    keep_ref[...] = total[rows, :] + middle_ref[rows, :] + table_ref[5:6, :]
    send_ref[...] = total[pl.ds(pl.multiple_of((1 - core) * count, count), count), :].astype(HALF)


def end_body(images, patches, pad, packed, place_ref, keep_ref, came_ref, start_ref, grad_middle_ref, mask_ref, table_ref, sums_two_ref, sums_entry_ref, sums_expand_ref, *rest):
    if packed:
        out_ref, small_ref, ended, spot = rest
    else:
        out_ref, spot, entry_ref, expand_ref, ended = rest
    count, width = keep_ref.shape
    columns = sums_entry_ref.shape[2] // 3
    blocks = sums_entry_ref.shape[0]
    core = place_ref[1] & 1
    gain = table_ref[0:1, :]

    def one(j, carry):
        rows = pl.ds(pl.multiple_of(j * CHUNK, CHUNK), CHUNK)
        far = pl.ds(pl.multiple_of(core * count + j * CHUNK, CHUNK), CHUNK)
        scaled, inverse = norm_scaled(start_ref[far, :])
        grad = keep_ref[rows, :] + came_ref[rows, :].astype(SINGLE)
        out = grad_middle_ref[far, :] + norm_grad(grad, scaled, inverse, gain)
        ended[rows, :] = out
        masked = mask_ref[far, :] > 0.5
        out_ref[rows, :] = jnp.where(masked, 0.0, out).astype(HALF)
        parts = (grad * scaled, grad, jnp.where(masked, out, 0.0))
        return tuple(c + fold(p) for c, p in zip(carry, parts))

    zero = jnp.zeros((8, width), SINGLE)
    totals = lax.fori_loop(0, count // CHUNK, one, (zero,) * 3)
    place = ended[:pad, :]
    for i in range(1, images):
        place = place + ended[i * pad : (i + 1) * pad, :]
    column = lambda total: jnp.sum(total, 0, keepdims=True)
    spot[...] = jnp.zeros_like(spot)
    spot[:pad, :] = place
    once = jnp.where(core == 0, 1.0, 0.0)
    rows = [column(totals[0]), column(totals[1])]
    rows += [column(sums_two_ref[row]) * once for row in range(4)]
    rows += [column(totals[2])]
    for row, total in enumerate(rows):
        spot[200 + row : 201 + row, :] = total
    if not packed:
        entry_ref[...] = jnp.zeros_like(entry_ref)
        expand_ref[...] = jnp.zeros_like(expand_ref)
        for b in range(blocks):
            entry_ref[place_ref[1] ^ (2 * b)] = column(sums_entry_ref[b])
            expand_ref[place_ref[1] ^ (2 * b)] = column(sums_expand_ref[b])
        return
    n_tensor = 2 * blocks
    n_dp = small_ref.shape[0] // n_tensor
    part = width // n_dp
    own = part // n_tensor
    small_ref[...] = jnp.zeros_like(small_ref)
    for dp_at in range(n_dp):
        for t_at in range(n_tensor):
            slot = small_slot(place_ref, t_at, dp_at)
            block = spot[PLACE_ROWS * t_at : PLACE_ROWS * (t_at + 1), part * dp_at : part * (dp_at + 1)]
            small_ref[slot, :PLACE_ROWS, :part] = block.astype(HALF)
        for b in range(blocks):
            dp_flip = place_ref[0] ^ dp_at
            slot = b * 8 + (dp_flip & 1) * 4 + (dp_flip >> 1)
            entry = column(sums_entry_ref[b])
            expand = column(sums_expand_ref[b])
            wide = expand[:, part * dp_at : part * (dp_at + 1)]
            short = entry[:, own * dp_at : own * (dp_at + 1)]
            shorter = entry[:, 2 * columns + own * dp_at : 2 * columns + own * (dp_at + 1)]
            fill = lambda row: jnp.concatenate([row, jnp.zeros((1, 128 - row.shape[1]), SINGLE)], 1)
            tall = jnp.concatenate([fill(wide), fill(short), fill(shorter), jnp.zeros((CHUNK - 3, 128), SINGLE)], 0)
            small_ref[slot, PLACE_ROWS:, :] = tall.astype(HALF)


def place_body(images, patches, pad, place_ref, own_ref, core_ref, x_ref, far_ref, out_ref):
    for flip, ref in enumerate((own_ref, core_ref, x_ref, far_ref)):
        for i in range(images):
            out_ref[(place_ref[1] ^ flip) * images + i] = ref[i * pad : i * pad + patches, :]


def local(sizes, *arguments):
    (patches, cotangent, mask_rank, mask_count, image_count,
     entry_weight, entry_moment, entry_second, entry_bias, entry_bias_moment, entry_bias_second,
     exit_weight, exit_moment, exit_second, expand_weight, expand_moment, expand_second,
     expand_bias, expand_bias_moment, expand_bias_second, reduce_weight, reduce_moment, reduce_second,
     vectors, vectors_moment, vectors_second, position, position_moment, position_second) = arguments
    n_dp, n_tensor = sizes
    blocks = n_tensor // 2
    direct = n_dp == 8 and n_tensor == 4
    dp, tensor = lax.axis_index("dp"), lax.axis_index("tensor")
    at = jnp.stack([dp, tensor]).astype(jnp.int32)
    slots, patch_count, width = patches.shape
    images = slots // blocks
    share = images // 2
    pad = -(-patch_count // CHUNK) * CHUNK
    tokens = images * pad
    columns = entry_weight.shape[2]
    hidden = expand_weight.shape[1]
    rows = entry_weight.shape[1]
    heads = columns // HEAD_DIM
    swap = Swap(n_dp, n_tensor)

    attn_shard = jnp.concatenate(
        [entry_weight[0], entry_weight[1], entry_weight[2], exit_weight.T], 1
    ).astype(HALF)
    expand_shard = expand_weight.astype(HALF)
    reduce_shard = reduce_weight.T.astype(HALF)

    first_image = (tensor // 2) * images
    own = lambda array: lax.dynamic_slice_in_dim(array, first_image, images, 0)
    masked = (own(mask_rank) < own(mask_count)[:, None]).astype(SINGLE)
    mask = jnp.pad(masked, ((0, 0), (0, pad - patch_count))).reshape(tokens, 1)
    live = (first_image + jnp.arange(images, dtype=jnp.int32) < image_count[0]).astype(SINGLE)

    if direct:
        part_rows = jnp.concatenate(
            [
                position.astype(HALF),
                jnp.zeros((200 - patch_count, rows), HALF),
                vectors.astype(HALF),
                jnp.zeros((4 * PLACE_ROWS - 207, rows), HALF),
            ]
        )
        block = lax.dynamic_slice_in_dim(part_rows, tensor * PLACE_ROWS, PLACE_ROWS, 0)
        bias_rows = jnp.concatenate(
            [
                expand_bias.astype(HALF),
                jnp.pad(entry_bias[:, 0, :].astype(HALF), ((0, 0), (0, rows - entry_bias.shape[2]))),
                jnp.zeros((SMALL_ROWS - PLACE_ROWS - 3, rows), HALF),
            ]
        )
        small = jnp.pad(jnp.concatenate([block, bias_rows]), ((0, 0), (0, 128 - rows)))
        attn_line = swap.gather_line(attn_shard)
        small = jnp.stack([small] + [swap.along(small, f"z{k}") for k in (1, 2, 3)])
        for name in ("y", "x", "core"):
            small = jnp.concatenate([small, swap.along(small, name)])
        reduce_plane = swap.plane_first(reduce_shard)
        expand_line = swap.gather_line(after(expand_shard, *attn_line))
        attn_pieces = swap.gather_plane(*attn_line)
        reduce_pieces = swap.line_last(after(reduce_plane, *expand_line))
        arrived = [attn_pieces[1][0], attn_pieces[3][0]]
        expand_line = lax.optimization_barrier((*expand_line, *arrived))
        expand_pieces = swap.gather_plane(*expand_line[:2])
        layout = swap.grad_layout()
        layout_line = swap.grad_layout_line()
        grad_outs = [shape((len(where), rows, width), HALF) for where in layout]
        grad_outs_line = [shape((len(where), rows, width), HALF) for where in layout_line]
        rows_out = rows
    else:
        def gather(shard):
            whole = lax.all_gather(shard, "dp", axis=0, tiled=True)
            return [
                ((swap.flip(whole, "tensor", 2 * b) if b else whole)[None], [(b, None)])
                for b in range(blocks)
            ]

        attn_pieces = gather(attn_shard)
        expand_pieces = gather(expand_shard)
        reduce_pieces = gather(reduce_shard)
        layout = layout_line = [[(b, None)] for b in range(blocks)]
        grad_outs = grad_outs_line = [shape((1, width, width), HALF) for _ in layout]
        rows_out = width
        everywhere = lambda array, axis: lax.all_gather(array.astype(HALF), "dp", axis=axis, tiled=True)
        place = jnp.pad(everywhere(position, 1), ((0, 256 - patch_count), (0, 0))).astype(SINGLE)
        table_in = jnp.pad(everywhere(vectors, 1), ((0, 1), (0, 0))).astype(SINGLE)
        both = lax.all_gather(everywhere(entry_bias, 2), "tensor", axis=1, tiled=True)
        entry_in = jnp.concatenate([both[0], jnp.zeros_like(both[0]), both[1]], 1)
        entry_in = entry_in.astype(SINGLE)[:, None, :]
        expand_in = lax.all_gather(everywhere(expand_bias, 1), "tensor", axis=0, tiled=True)
        expand_in = expand_in.astype(SINGLE)[:, None, :]

    def pieces_of(pieces):
        return [(piece, ANY) for piece, _ in pieces], [where for _, where in pieces]

    held = pltpu.VMEM((blocks, width, width), HALF)
    wide = pltpu.VMEM((tokens, width), SINGLE)
    sem = pltpu.SemaphoreType.DMA
    many = sem((8 * blocks,))
    whole_half = (shape((tokens, width), HALF), VMEM)
    whole_single = (shape((tokens, width), SINGLE), VMEM)
    share_half = (shape((share * pad, width), HALF), VMEM)
    share_single = (shape((share * pad, width), SINGLE), VMEM)
    hidden_half = (shape((blocks, tokens, hidden), HALF), VMEM)
    weight = (shape((blocks, width, hidden), HALF), ANY)
    qkv_half = (shape((blocks, tokens, 3 * columns), HALF), VMEM)
    at_in = [(at, SMEM)]

    small_in = [small] if direct else [place, table_in, entry_in, expand_in]
    start_scratch = [pltpu.VMEM((images, patch_count, width), HALF)] * 2
    if direct:
        start_scratch.append(pltpu.VMEM((4 * PLACE_ROWS, width), SINGLE))
    start, normed_one, low, table, entry_shift, expand_shift = kernel_call(
        functools.partial(start_body, images, patch_count, pad, direct),
        [
            whole_single,
            whole_half,
            whole_half,
            (shape((8, width), SINGLE), VMEM),
            (shape((n_tensor, 1, 3 * columns), SINGLE), VMEM),
            (shape((n_tensor, 1, hidden), SINGLE), VMEM),
        ],
        at_in
        + [(patches, ANY), (cotangent, ANY), (mask, VMEM), (live, SMEM)]
        + [(a, VMEM) for a in small_in],
        start_scratch + [sem((2,))],
        10,
        "start",
    )

    operands, spots = pieces_of(attn_pieces)
    qkv, probs, mixed, branch, attn_full = kernel_call(
        functools.partial(attend_body, images, patch_count, pad, spots),
        [
            qkv_half,
            (shape((blocks, images * heads, pad, pad), HALF), VMEM),
            (shape((blocks, tokens, columns), HALF), VMEM),
            whole_half,
            weight,
        ],
        at_in
        + [(after(normed_one, reduce_pieces[0][0]), VMEM), (entry_shift, VMEM)]
        + operands,
        [held, wide, many, sem],
        16,
        "attend",
    )
    branch_came = swap.along(branch, "core")

    operands, spots = pieces_of(expand_pieces)
    middle, normed_two, active, slope, expand_full, *grad_reduce = kernel_call(
        functools.partial(up_body, spots, layout_line, rows_out),
        [whole_single, whole_half, hidden_half, hidden_half, weight]
        + [(a, ANY) for a in grad_outs_line],
        at_in
        + [(a, VMEM) for a in (start, branch, branch_came, low, table, expand_shift)]
        + operands,
        [held, wide, held, many, sem, many],
        22,
        "up",
    )

    operands, spots = pieces_of(reduce_pieces)
    grad_upper, normed_grad, reduce_full, sums_expand = kernel_call(
        functools.partial(down_body, spots),
        [hidden_half, whole_half, weight, (shape((blocks, 8, hidden), SINGLE), VMEM)],
        at_in + [(a, VMEM) for a in (low, slope, expand_full)] + operands,
        [held, wide, wide, many, sem],
        12,
        "down",
    )
    normed_came = swap.along(normed_grad, "core")

    grad_expand = kernel_call(
        functools.partial(expand_body, layout, rows_out),
        [(a, ANY) for a in grad_outs],
        at_in + [(a, VMEM) for a in (normed_two, grad_upper)],
        [held, many],
        5,
        "expand",
    )

    grad_middle, grad_qkv, sums_two, sums_entry, *grad_attn = kernel_call(
        functools.partial(back_body, images, pad, layout, rows_out),
        [
            whole_single,
            qkv_half,
            (shape((4, 8, width), SINGLE), VMEM),
            (shape((blocks, 8, 3 * columns), SINGLE), VMEM),
        ]
        + [(a, ANY) for a in grad_outs],
        at_in
        + [(a, VMEM) for a in (normed_grad, normed_came, middle, low, table, attn_full, qkv, probs, normed_one, mixed)],
        [pltpu.VMEM((tokens, width), HALF), pltpu.VMEM((tokens, columns), HALF), held, many],
        26,
        "back",
    )

    out_keep, out_send = kernel_call(
        output_body,
        [share_single, share_half],
        at_in + [(a, VMEM) for a in (middle, after(active, grad_qkv), reduce_full, table)],
        [wide],
        6,
        "output",
    )
    out_came = swap.along(out_send, "core")
    live_rows = jnp.repeat(
        lax.dynamic_slice_in_dim(live, (tensor % 2) * share, share, 0), pad, total_repeat_length=share * pad
    )
    own_out = ((out_keep + out_came.astype(SINGLE)) * live_rows[:, None]).astype(HALF)

    grad_keep, grad_send = kernel_call(
        normed_body,
        [share_single, share_half],
        at_in + [(a, VMEM) for a in (grad_qkv, attn_full)],
        [wide],
        5,
        "normed",
    )
    grad_came = swap.along(grad_send, "core")

    small_out = (
        [(shape((n_dp * n_tensor, SMALL_ROWS, 128), HALF), VMEM)]
        if direct
        else [
            (shape((4 * PLACE_ROWS, width), SINGLE), VMEM),
            (shape((n_tensor, 1, 3 * columns), SINGLE), VMEM),
            (shape((n_tensor, 1, hidden), SINGLE), VMEM),
        ]
    )
    end_scratch = [pltpu.VMEM((share * pad, width), SINGLE)]
    if direct:
        end_scratch.append(pltpu.VMEM((4 * PLACE_ROWS, width), SINGLE))
    own_grad, *small_grads = kernel_call(
        functools.partial(end_body, share, patch_count, pad, direct),
        [share_half] + small_out,
        at_in
        + [
            (a, VMEM)
            for a in (grad_keep, grad_came, start, grad_middle, mask, table, sums_two, sums_entry, sums_expand)
        ],
        end_scratch,
        8,
        "end",
    )

    def spread(piece):
        far = swap.along(piece, "x")
        near = swap.along(piece, "core")
        return kernel_call(
            functools.partial(place_body, share, patch_count, pad),
            [(shape(patches.shape, HALF), VMEM)],
            at_in + [(a, VMEM) for a in (piece, near, far, swap.along(far, "core"))],
            [],
            3,
            "spread",
        )[0]

    block_out = spread(own_out)
    patch_grad = spread(own_grad)

    sum_up = lambda parts: sum(part.astype(SINGLE) for part in parts)
    if direct:
        grad_reduce = lax.optimization_barrier((*grad_reduce, grad_upper))[:-1]
        reduced = sum_up(swap.reduce_line(grad_reduce)).T
        expanded = sum_up(swap.reduce(grad_expand))
        attn = sum_up(swap.reduce(grad_attn))
        (small,) = small_grads
        for name, count in (("core", 16), ("x", 8), ("y", 4)):
            small = add(small[:count], swap.along(small[count:], name))
        small = sum_up([small[0]] + [swap.along(small[k], f"z{k}") for k in (1, 2, 3)])
        pair = jnp.stack([small, swap.along(small, "core")])
        four = jnp.concatenate([pair, swap.along(pair, "x")])
        four = [lax.dynamic_index_in_dim(four, tensor ^ t, 0, keepdims=False) for t in range(n_tensor)]
        spot = jnp.concatenate([part[:PLACE_ROWS, :rows] for part in four])
        grad_place = spot[:patch_count]
        grad_table = spot[200:207]
        grad_expand_shift = small[PLACE_ROWS : PLACE_ROWS + 1, :rows]
        grad_entry_shift = small[PLACE_ROWS + 1 : PLACE_ROWS + 3, : entry_bias.shape[2]][:, None, :]
    else:
        def total(outs):
            mine = outs[0][0].astype(SINGLE)
            for b in range(1, blocks):
                mine = mine + swap.flip(outs[b][0], "tensor", 2 * b).astype(SINGLE)
            return lax.psum_scatter(mine, "dp", scatter_dimension=0, tiled=True)

        reduced = total(grad_reduce).T
        expanded = total(grad_expand)
        attn = total(grad_attn)
        spot, entry_part, expand_part = small_grads
        spot = lax.psum(lax.psum_scatter(spot, "dp", scatter_dimension=1, tiled=True), "tensor")
        grad_place = spot[:patch_count]
        grad_table = spot[200:207]
        deal = lambda array, axis: lax.psum_scatter(
            lax.psum_scatter(array, "tensor", scatter_dimension=0, tiled=True)[0],
            "dp",
            scatter_dimension=axis,
            tiled=True,
        )
        grad_expand_shift = deal(expand_part, 1)
        ends = [deal(entry_part[:, :, first : first + columns], 1) for first in (0, 2 * columns)]
        grad_entry_shift = jnp.stack(ends)

    grad_entry = jnp.stack([attn[:, j * columns : (j + 1) * columns] for j in range(3)])
    grad_exit = attn[:, 3 * columns :].T

    entry = adamw(entry_weight, entry_moment, entry_second, grad_entry, 0.05, 0.05)
    entry_b = adamw(entry_bias, entry_bias_moment, entry_bias_second, grad_entry_shift, 0.3, 0.0)
    exits = adamw(exit_weight, exit_moment, exit_second, grad_exit, 0.05, 0.05)
    expand = adamw(expand_weight, expand_moment, expand_second, expanded, 0.05, 0.05)
    expand_b = adamw(expand_bias, expand_bias_moment, expand_bias_second, grad_expand_shift, 0.3, 0.0)
    reduce_w = adamw(reduce_weight, reduce_moment, reduce_second, reduced, 0.05, 0.05)
    table_new = adamw(vectors, vectors_moment, vectors_second, grad_table, 0.3, 0.0)
    place_new = adamw(position, position_moment, position_second, grad_place, 0.1, 0.0)
    return (block_out, patch_grad, *entry, *entry_b, *exits, *expand, *expand_b, *reduce_w, *table_new, *place_new)


def solution(mesh):
    images = P("dp", None, None)
    entry = P(None, "dp", "tensor")
    entry_bias = P(None, "tensor", "dp")
    outer = P("tensor", "dp")
    expand = P("dp", "tensor")
    table = P(None, "dp")
    weights = (entry, entry_bias, outer, expand, outer, outer, table, table)
    placed = (images, images, P("dp", None), P("dp"), P("dp"))
    placed += tuple(spec for spec in weights for _ in range(3))
    given = (images, images) + tuple(spec for spec in weights for _ in range(4))
    sizes = (mesh.shape["dp"], mesh.shape["tensor"])
    return jax.shard_map(
        functools.partial(local, sizes),
        mesh=mesh,
        in_specs=placed,
        out_specs=given,
        check_vma=False,
    )
```

time: 431 us -> 388 us (0.900)
  starting transfers between devices: 84.8 us -> 52.2 us
  waiting for transfers between devices: 124 us -> 92.3 us
  Pallas kernels: 137 us -> 154 us
  other arithmetic: 32.2 us -> 36.9 us
    ppermute x104 -> x56, starting transfers between devices: 84.8 us -> 52.2 us  [flip(): return lax.ppermute(array, axis, [(i, i ^ bits) for i in range(count)])]
    ppermute x104 -> x56, waiting for transfers between devices: 124 us -> 92.3 us  [flip(): return lax.ppermute(array, axis, [(i, i ^ bits) for i in range(count)])]
    pallas_call x10 -> x11, Pallas kernels: 137 us -> 154 us  [kernel_call(): pl.pallas_call(body, out_shape=[a for a, _ in outs], in_specs=[spec for _...]
    ppermute x6 -> x0, local copies, waits for them, and re-layouts: 9.64 us -> none  [flip(): return lax.ppermute(array, axis, [(i, i ^ bits) for i in range(count)])]
    unnamed x194 -> x164, local copies, waits for them, and re-layouts: 31.2 us -> 40.6 us
    convert_element_type x29 -> x13, other arithmetic: 20.2 us -> 12.2 us  [the longest x11 11.5 us: add(): return total.astype(HALF)]
    add x2 -> x5, other arithmetic: 0.08 us -> 4.9 us  [the longest x3 3.88 us: add(): total = total + part.astype(SINGLE)]
  transfers between devices with their start and end apart: 104 -> 56, of which waited for: 33 -> 16; matrix products, arithmetic and copies ran while one was open for 16% -> 18% of each run, Pallas kernels for 9% -> 29%
where the time goes in v2:
time: 388 us; the launch traced here: 386 us
  Pallas kernels  154 us (40%)
  waiting for transfers between devices  92.3 us (24%)
  starting transfers between devices  52.2 us (13%)
  local copies, waits for them, and re-layouts  48.3 us (12%)
  other arithmetic  36.9 us (10%)
    pallas_call x11, Pallas kernels, kernel_call(): pl.pallas_call(body, out_shape=[a for a, _ in outs], in_specs=[spec for _...  154 us
    ppermute x56, waiting for transfers between devices, flip(): return lax.ppermute(array, axis, [(i, i ^ bits) for i in range(count)])  92.3 us
    ppermute x56, starting transfers between devices, flip(): return lax.ppermute(array, axis, [(i, i ^ bits) for i in range(count)])  52.2 us
    unnamed x164, local copies, waits for them, and re-layouts  40.6 us
    convert_element_type x11, other arithmetic, add(): return total.astype(HALF)  11.5 us
    convert_element_type x8, other arithmetic, adamw(): return (master, moment, second, master.astype(jnp.bfloat16))  9.84 us
  transfers between devices with their start and end apart: 56, of which 16 were waited for; matrix products, arithmetic and copies ran while one was open for 18% of the time, Pallas kernels for 29%

profile of v2, /device:TPU:0, one launch (start us, length us, event | category | flops | bytes accessed | tf_op | source)
XLA Modules:
  0.0 386.2 jit_solution(15602145534559983272)
XLA Ops:
  4.2 4.1 %collective-permute-start.1 = (bf16[80,128]{1,0:T(8,128)(2,1)S(1)}, bf16[80,128]{1,0:T(8,128)(2,1)S(1)}, u32[]{:S(2)}, u32[]{:S(2)}) collective-permute-start(bf16[80,128]{1,0:T(8,128)(2,1)S(1)} %get-tuple-element.315), channel_id=1, source_target_pairs={{0,16},{4,20},{8,24},{12,28},{16,0},{20,4},{24,8},{28,12},{1,17},{... | collective-permute-start | bytes 61448 | tf_op jit(solution)/shard_map/ppermute | solution.py:81
  33.8 3.1 collective-permute-start.10
  39.7 3.3 collective-permute-done.10
  46.8 5.8 %collective-permute-done.11 = bf16[2,96,768]{2,1,0:T(8,128)(2,1)} collective-permute-done((bf16[2,96,768]{2,1,0:T(8,128)(2,1)}, bf16[2,96,768]{2,1,0:T(8,128)(2,1)}, u32[]{:S(2)}, u32[]{:S(2)}) %collective-permute-start.11) | collective-permute-done | bytes 294944 | tf_op jit(solution)/shard_map/ppermute | solution.py:81
  55.5 15.4 %start.1 = (f32[832,768]{1,0:T(8,128)}, bf16[832,768]{1,0:T(8,128)(2,1)}, bf16[832,768]{1,0:T(8,128)(2,1)}, f32[8,768]{1,0:T(8,128)}, f32[4,1,576]{2,1,0:T(1,128)}, /*index=5*/f32[4,1,768]{2,1,0:T(1,128)}) custom-call(s32[2]{0:T(128)} %pad_add_fusion.place_ref, bf16[8,196,768]{2,1,0:T(8,128)(2,1)} %copy.130.patch_ref, bf16[8,196,768]{2,1,0:T(8,128)(2,1)} %copy.131.cot_ref, ...), custom_call_target="tpu_custom_call" | custom-call | flops 10000000 | bytes 1024 | tf_op jit(solution)/shard_map/start/pallas_call | solution.py:48
  71.0 9.2 %collective-permute-done.12 = bf16[4,96,768]{2,1,0:T(8,128)(2,1)} collective-permute-done((bf16[4,96,768]{2,1,0:T(8,128)(2,1)S(1)}, bf16[4,96,768]{2,1,0:T(8,128)(2,1)}, u32[]{:S(2)}, u32[]{:S(2)}) %collective-permute-start.12) | collective-permute-done | bytes 589856 | tf_op jit(solution)/shard_map/ppermute | solution.py:81
  82.2 17.9 %attend.1 = (bf16[2,832,576]{2,1,0:T(8,128)(2,1)}, bf16[2,12,208,208]{3,2,1,0:T(8,128)(2,1)}, bf16[2,832,192]{2,1,0:T(8,128)(2,1)}, bf16[832,768]{1,0:T(8,128)(2,1)}, bf16[2,768,768]{2,1,0:T(8,128)(2,1)}) custom-call(s32[2]{0:T(128)} %pad_add_fusion.place_ref, bf16[832,768]{1,0:T(8,128)(2,1)} %get-tuple-element.100.normed_ref, ...), custom_call_target="tpu_custom_call" | custom-call | flops 16000000 | bytes 1024 | tf_op jit(solution)/shard_map/attend/pallas_call | solution.py:48
  102.9 6.9 %collective-permute-done.20 = bf16[2,96,768]{2,1,0:T(8,128)(2,1)S(1)} collective-permute-done((bf16[2,96,768]{2,1,0:T(8,128)(2,1)}, bf16[2,96,768]{2,1,0:T(8,128)(2,1)S(1)}, u32[]{:S(2)}, u32[]{:S(2)}) %collective-permute-start.20) | collective-permute-done | bytes 294944 | tf_op jit(solution)/shard_map/ppermute | solution.py:81
  111.7 13.0 %collective-permute-done.21.rest_3_ = bf16[4,96,768]{2,1,0:T(8,128)(2,1)S(1)} collective-permute-done((bf16[4,96,768]{2,1,0:T(8,128)(2,1)S(1)}, bf16[4,96,768]{2,1,0:T(8,128)(2,1)S(1)}, u32[]{:S(2)}, u32[]{:S(2)}) %collective-permute-start.21) | collective-permute-done | bytes 589856 | tf_op jit(solution)/shard_map/ppermute | solution.py:81
  126.3 27.9 %up.1 = (f32[832,768]{1,0:T(8,128)}, bf16[832,768]{1,0:T(8,128)(2,1)}, bf16[2,832,768]{2,1,0:T(8,128)(2,1)}, bf16[2,832,768]{2,1,0:T(8,128)(2,1)}, bf16[2,768,76...) custom-call(s32[2]{0:T(128)} %pad_add_fusion.place_ref, ...), custom_call_target="tpu_custom_call" | custom-call | flops 22000000 | bytes 1024 | tf_op jit(solution)/shard_map/up/pallas_call | solution.py:48
  155.3 13.3 %down.1 = (bf16[2,832,768]{2,1,0:T(8,128)(2,1)}, bf16[832,768]{1,0:T(8,128)(2,1)}, bf16[2,768,768]{2,1,0:T(8,128)(2,1)}, f32[2,8,768]{2,1,0:T(8,128)}) custom-call(s32[2]{0:T(128)} %pad_add_fusion.place_ref, bf16[832,768]{1,0:T(8,128)(2,1)} %get-tuple-element.103.low_ref, bf16[2,832,768]{2,1,0:T(8,128)(2,1)} %get-tuple-element.110.slope_ref, ...), custom_call_target="tpu_custom_call" | custom-call | flops 12000000 | bytes 1024 | tf_op jit(solution)/shard_map/down/pallas_call | solution.py:48
  168.7 6.8 %expand.1 = (bf16[4,96,768]{2,1,0:T(8,128)(2,1)}, bf16[4,96,768]{2,1,0:T(8,128)(2,1)}, bf16[4,96,768]{2,1,0:T(8,128)(2,1)}, bf16[4,96,768]{2,1,0:T(8,128)(2,1)}) custom-call(s32[2]{0:T(128)} %pad_add_fusion.place_ref, bf16[832,768]{1,0:T(8,128)(2,1)} %get-tuple-element.134.normed_ref, bf16[2,832,768]{2,1,0:T(8,128)(2,1)} %get-tuple-element.135.grad_upper_ref), custom_call_target="tpu_custom_call" | custom-call | flops 5000000 | bytes 1024 | tf_op jit(solution)/shard_map/expand/pallas_call | solution.py:48
  178.7 11.0 %collective-permute-done.46 = bf16[4,96,768]{2,1,0:T(8,128)(2,1)S(1)} collective-permute-done((bf16[4,96,768]{2,1,0:T(8,128)(2,1)}, bf16[4,96,768]{2,1,0:T(8,128)(2,1)S(1)}, u32[]{:S(2)}, u32[]{:S(2)}) %collective-permute-start.46) | collective-permute-done | bytes 589856 | tf_op jit(solution)/shard_map/ppermute | solution.py:81
  194.2 4.3 %collective-permute-done.47 = bf16[2,96,768]{2,1,0:T(8,128)(2,1)} collective-permute-done((bf16[2,96,768]{2,1,0:T(8,128)(2,1)S(1)}, bf16[2,96,768]{2,1,0:T(8,128)(2,1)}, u32[]{:S(2)}, u32[]{:S(2)}) %collective-permute-start.47) | collective-permute-done | bytes 294944 | tf_op jit(solution)/shard_map/ppermute | solution.py:81
  201.7 5.4 %collective-permute-done.50 = bf16[8,96,768]{2,1,0:T(8,128)(2,1)} collective-permute-done((bf16[8,96,768]{2,1,0:T(8,128)(2,1)}, bf16[8,96,768]{2,1,0:T(8,128)(2,1)}, u32[]{:S(2)}, u32[]{:S(2)}) %collective-permute-start.50) | collective-permute-done | bytes 1179680 | tf_op jit(solution)/shard_map/ppermute | solution.py:81
  207.1 2.0 add_convert_fusion
  209.1 3.9 %collective-permute-done.48 = bf16[2,96,768]{2,1,0:T(8,128)(2,1)S(1)} collective-permute-done((bf16[2,96,768]{2,1,0:T(8,128)(2,1)S(1)}, bf16[2,96,768]{2,1,0:T(8,128)(2,1)S(1)}, u32[]{:S(2)}, u32[]{:S(2)}) %collective-permute-start.48) | collective-permute-done | bytes 294944 | tf_op jit(solution)/shard_map/ppermute | solution.py:81
  216.8 40.5 %back.1 = (f32[832,768]{1,0:T(8,128)}, bf16[2,832,576]{2,1,0:T(8,128)(2,1)}, f32[4,8,768]{2,1,0:T(8,128)}, f32[2,8,576]{2,1,0:T(8,128)}, bf16[4,96,768]{2,1,0:T(...) custom-call(s32[2]{0:T(128)} %pad_add_fusion.place_ref, ...), custom_call_target="tpu_custom_call" | custom-call | flops 26000000 | bytes 1024 | tf_op jit(solution)/shard_map/back/pallas_call | solution.py:48
  263.2 7.2 %output.1 = (f32[416,768]{1,0:T(8,128)}, bf16[416,768]{1,0:T(8,128)(2,1)}) custom-call(s32[2]{0:T(128)} %pad_add_fusion.place_ref, f32[832,768]{1,0:T(8,128)} %get-tuple-element.108.middle_ref, bf16[2,832,768]{2,1,0:T(8,128)(2,1)} %get-tuple-element.118.active_ref, bf16[2,768,768]{2,1,0:T(8,128)(2,1)} %get-tuple-element.119.reduce_ref, ...), custom_call_target="tpu_custom_call" | custom-call | flops 6000000 | bytes 1024 | tf_op jit(solution)/shard_map/output/pallas_call | solution.py:48
  270.5 6.2 %normed.1 = (f32[416,768]{1,0:T(8,128)}, bf16[416,768]{1,0:T(8,128)(2,1)}) custom-call(s32[2]{0:T(128)} %pad_add_fusion.place_ref, bf16[2,832,576]{2,1,0:T(8,128)(2,1)} %get-tuple-element.117.grad_qkv_ref, bf16[2,768,768]{2,1,0:T(8,128)(2,1)} %get-tuple-element.113.full_ref), custom_call_target="tpu_custom_call" | custom-call | flops 5000000 | bytes 1024 | tf_op jit(solution)/shard_map/normed/pallas_call | solution.py:48
  277.2 2.5 fusion.31
  279.7 2.0 add_convert_fusion.2
  287.9 12.2 %end.1 = (bf16[416,768]{1,0:T(8,128)(2,1)}, bf16[32,80,128]{2,1,0:T(8,128)(2,1)}) custom-call(s32[2]{0:T(128)} %pad_add_fusion.place_ref, f32[416,768]{1,0:T(8,128)} %get-tuple-element.122.keep_ref, bf16[416,768]{1,0:T(8,128)(2,1)} %copy-done.24, f32[832,768]{1,0:T(8,128)} %get-tuple-element.96.start_ref, f32[832,768]{1,0:T(8,128)} %get-tuple-element.124.grad_middle_ref, ...), custom_call_target="tpu_custom_call" | custom-call | flops 8000000 | bytes 1024 | tf_op jit(solution)/shard_map/end/pallas_call | solution.py:48
  307.7 17.3 %collective-permute-done.39 = bf16[8,80,128]{2,1,0:T(8,128)(2,1)S(1)} collective-permute-done((bf16[8,80,128]{2,1,0:T(8,128)(2,1)S(1)}, bf16[8,80,128]{2,1,0:T(8,128)(2,1)S(1)}, u32[]{:S(2)}, u32[]{:S(2)}) %collective-permute-start.39) | collective-permute-done | bytes 163872 | tf_op jit(solution)/shard_map/ppermute | solution.py:81
  325.0 2.6 collective-permute-start.36
  328.7 2.2 fusion.26
  342.5 2.7 collective-permute-start.55
  345.1 7.2 %collective-permute-done.30.x_ref = bf16[416,768]{1,0:T(8,128)(2,1)S(1)} collective-permute-done((bf16[416,768]{1,0:T(8,128)(2,1)S(1)}, bf16[416,768]{1,0:T(8,128)(2,1)S(1)}, u32[]{:S(2)}, u32[]{:S(2)}) %collective-permute-start.30) | collective-permute-done | bytes 639008 | tf_op jit(solution)/shard_map/ppermute | solution.py:81
  372.5 3.3 spread.2
  375.8 3.6 copy.147
  379.3 3.3 spread.3
  382.6 3.6 copy.148
  (331 shorter events, 114.3 us)
Async XLA Ops:
  15.3 21.6 %collective-permute-start.6 = (bf16[96,768]{1,0:T(8,128)(2,1)}, bf16[96,768]{1,0:T(8,128)(2,1)S(1)}, u32[]{:S(2)}, u32[]{:S(2)}) collective-permute-start(bf16[96,768]{1,0:T(8,128)(2,1)} %get-tuple-element.287), channel_id=1, source_target_pairs={{0,2},{1,3},{2,0},{3,1},{4,6},{5,7},{6,4},{7,5},{8,10},{9,11},{10,... | collective-permute-start | bytes 442376 | tf_op jit(solution)/shard_map/ppermute | solution.py:81
  39.2 15.6 %collective-permute-start.5 = (bf16[16,80,128]{2,1,0:T(8,128)(2,1)S(1)}, bf16[16,80,128]{2,1,0:T(8,128)(2,1)S(1)}, u32[]{:S(2)}, u32[]{:S(2)}) collective-permute-start(bf16[16,80,128]{2,1,0:T(8,128)(2,1)S(1)} %get-tuple-element.292), channel_id=1, source_target_pairs={{0,1},{1,0},{2,3},{3,2},{4,5},{5,4},{6,7},{7,6},{8,9},{9,8},{10,11... | collective-permute-start | bytes 983048 | tf_op jit(solution)/shard_map/ppermute | solution.py:81
  43.9 37.4 %collective-permute-start.14 = (bf16[4,96,768]{2,1,0:T(8,128)(2,1)S(1)}, bf16[4,96,768]{2,1,0:T(8,128)(2,1)}, u32[]{:S(2)}, u32[]{:S(2)}) collective-permute-start(bf16[4,96,768]{2,1,0:T(8,128)(2,1)S(1)} %pad_maximum_fusion.1.rest_0_), channel_id=1, source_target_pairs={{0,2},{1,3},{2,0},{3,1},{4,6},{5,7},{6,4},{7,5},{8,10},{9,11},{10,... | collective-permute-start | bytes 1769480 | tf_op jit(solution)/shard_map/ppermute | solution.py:81
  52.6 27.6 %collective-permute-start.12 = (bf16[4,96,768]{2,1,0:T(8,128)(2,1)S(1)}, bf16[4,96,768]{2,1,0:T(8,128)(2,1)}, u32[]{:S(2)}, u32[]{:S(2)}) collective-permute-start(bf16[4,96,768]{2,1,0:T(8,128)(2,1)S(1)} %pad_maximum_fusion), channel_id=1, source_target_pairs={{0,16},{4,20},{8,24},{12,28},{16,0},{20,4},{24,8},{28,12},{1,17},{... | collective-permute-start | bytes 1769480 | tf_op jit(solution)/shard_map/ppermute | solution.py:81
  53.0 28.3 %collective-permute-start.16 = (bf16[4,96,768]{2,1,0:T(8,128)(2,1)S(1)}, bf16[4,96,768]{2,1,0:T(8,128)(2,1)S(1)}, u32[]{:S(2)}, u32[]{:S(2)}) collective-permute-start(bf16[4,96,768]{2,1,0:T(8,128)(2,1)S(1)} %constant_dynamic-update-slice_fusion.20.rest_2_), channel_id=1, source_target_pairs={{0,4},{4,0},{8,12},{12,8},{16,20},{20,16},{24,28},{28,24},{1,5},{5... | collective-permute-start | bytes 1769480 | tf_op jit(solution)/shard_map/ppermute | solution.py:81
  100.1 25.4 %collective-permute-start.17 = (bf16[832,768]{1,0:T(8,128)(2,1)}, bf16[832,768]{1,0:T(8,128)(2,1)}, u32[]{:S(2)}, u32[]{:S(2)}) collective-permute-start(bf16[832,768]{1,0:T(8,128)(2,1)} %get-tuple-element.102.branch_ref), channel_id=1, source_target_pairs={{0,1},{1,0},{2,3},{3,2},{4,5},{5,4},{6,7},{7,6},{8,9},{9,8},{10,11... | collective-permute-start | bytes 3833864 | tf_op jit(solution)/shard_map/ppermute | solution.py:81
  100.2 54.0 %collective-permute-start.22 = (bf16[8,96,768]{2,1,0:T(8,128)(2,1)S(1)}, bf16[8,96,768]{2,1,0:T(8,128)(2,1)S(1)}, u32[]{:S(2)}, u32[]{:S(2)}) collective-permute-start(bf16[8,96,768]{2,1,0:T(8,128)(2,1)S(1)} %constant_dynamic-update-slice_fusion.18.rest_0_), channel_id=1, source_target_pairs={{0,8},{4,12},{8,0},{12,4},{16,24},{20,28},{24,16},{28,20},{1,9},{5... | collective-permute-start | bytes 3538952 | tf_op jit(solution)/shard_map/ppermute | solution.py:81
  109.9 14.8 %collective-permute-start.21 = (bf16[4,96,768]{2,1,0:T(8,128)(2,1)S(1)}, bf16[4,96,768]{2,1,0:T(8,128)(2,1)S(1)}, u32[]{:S(2)}, u32[]{:S(2)}) collective-permute-start(bf16[4,96,768]{2,1,0:T(8,128)(2,1)S(1)} %constant_dynamic-update-slice_fusion.24.rest_2_), channel_id=1, source_target_pairs={{0,4},{4,0},{8,12},{12,8},{16,20},{20,16},{24,28},{28,24},{1,5},{5... | collective-permute-start | bytes 1769480 | tf_op jit(solution)/shard_map/ppermute | solution.py:81
  110.5 14.5 %collective-permute-start.19 = (bf16[4,96,768]{2,1,0:T(8,128)(2,1)S(1)}, bf16[4,96,768]{2,1,0:T(8,128)(2,1)S(1)}, u32[]{:S(2)}, u32[]{:S(2)}) collective-permute-start(bf16[4,96,768]{2,1,0:T(8,128)(2,1)S(1)} %constant_dynamic-update-slice_fusion.22.rest_0_), channel_id=1, source_target_pairs={{0,2},{1,3},{2,0},{3,1},{4,6},{5,7},{6,4},{7,5},{8,10},{9,11},{10,... | collective-permute-start | bytes 1769480 | tf_op jit(solution)/shard_map/ppermute | solution.py:81
  175.5 14.2 %collective-permute-start.46 = (bf16[4,96,768]{2,1,0:T(8,128)(2,1)}, bf16[4,96,768]{2,1,0:T(8,128)(2,1)S(1)}, u32[]{:S(2)}, u32[]{:S(2)}) collective-permute-start(bf16[4,96,768]{2,1,0:T(8,128)(2,1)} %get-tuple-element.139), channel_id=1, source_target_pairs={{0,4},{4,0},{8,12},{12,8},{16,20},{20,16},{24,28},{28,24},{1,5},{5... | collective-permute-start | bytes 1769480 | tf_op jit(solution)/shard_map/ppermute | solution.py:81
  176.6 15.6 %collective-permute-start.44 = (bf16[4,96,768]{2,1,0:T(8,128)(2,1)}, bf16[4,96,768]{2,1,0:T(8,128)(2,1)}, u32[]{:S(2)}, u32[]{:S(2)}) collective-permute-start(bf16[4,96,768]{2,1,0:T(8,128)(2,1)} %get-tuple-element.137), channel_id=1, source_target_pairs={{0,2},{1,3},{2,0},{3,1},{4,6},{5,7},{6,4},{7,5},{8,10},{9,11},{10,... | collective-permute-start | bytes 1769480 | tf_op jit(solution)/shard_map/ppermute | solution.py:81
  177.1 30.0 %collective-permute-start.50 = (bf16[8,96,768]{2,1,0:T(8,128)(2,1)}, bf16[8,96,768]{2,1,0:T(8,128)(2,1)}, u32[]{:S(2)}, u32[]{:S(2)}) collective-permute-start(bf16[8,96,768]{2,1,0:T(8,128)(2,1)} %get-tuple-element.144), channel_id=1, source_target_pairs={{0,8},{4,12},{8,0},{12,4},{16,24},{20,28},{24,16},{28,20},{1,9},{5... | collective-permute-start | bytes 3538952 | tf_op jit(solution)/shard_map/ppermute | solution.py:81
  178.7 37.1 %collective-permute-start.23 = (bf16[832,768]{1,0:T(8,128)(2,1)S(1)}, bf16[832,768]{1,0:T(8,128)(2,1)S(1)}, u32[]{:S(2)}, u32[]{:S(2)}) collective-permute-start(bf16[832,768]{1,0:T(8,128)(2,1)S(1)} %copy-done.8), channel_id=1, source_target_pairs={{0,1},{1,0},{2,3},{3,2},{4,5},{5,4},{6,7},{7,6},{8,9},{9,8},{10,11... | collective-permute-start | bytes 3833864 | tf_op jit(solution)/shard_map/ppermute | solution.py:81
  193.4 15.8 %collective-permute-start.45 = (bf16[2,96,768]{2,1,0:T(8,128)(2,1)S(1)}, bf16[2,96,768]{2,1,0:T(8,128)(2,1)S(1)}, u32[]{:S(2)}, u32[]{:S(2)}) collective-permute-start(bf16[2,96,768]{2,1,0:T(8,128)(2,1)S(1)} %add_convert_fusion.5), channel_id=1, source_target_pairs={{0,4},{4,0},{8,12},{12,8},{16,20},{20,16},{24,28},{28,24},{1,5},{5... | collective-permute-start | bytes 884744 | tf_op jit(solution)/shard_map/ppermute | solution.py:81
  209.1 70.6 %collective-permute-start.51 = (bf16[4,96,768]{2,1,0:T(8,128)(2,1)}, bf16[4,96,768]{2,1,0:T(8,128)(2,1)S(1)}, u32[]{:S(2)}, u32[]{:S(2)}) collective-permute-start(bf16[4,96,768]{2,1,0:T(8,128)(2,1)} %add_convert_fusion), channel_id=1, source_target_pairs={{0,16},{4,20},{8,24},{12,28},{16,0},{20,4},{24,8},{28,12},{1,17},{... | collective-permute-start | bytes 1769480 | tf_op jit(solution)/shard_map/ppermute | solution.py:81
  214.9 61.8 %collective-permute-start.49 = (bf16[96,768]{1,0:T(8,128)(2,1)}, bf16[96,768]{1,0:T(8,128)(2,1)}, u32[]{:S(2)}, u32[]{:S(2)}) collective-permute-start(bf16[96,768]{1,0:T(8,128)(2,1)} %fusion.5), channel_id=1, source_target_pairs={{0,16},{4,20},{8,24},{12,28},{16,0},{20,4},{24,8},{28,12},{1,17},{... | collective-permute-start | bytes 442376 | tf_op jit(solution)/shard_map/ppermute | solution.py:81
  257.3 25.4 %collective-permute-start.32 = (bf16[4,96,768]{2,1,0:T(8,128)(2,1)}, bf16[4,96,768]{2,1,0:T(8,128)(2,1)S(1)}, u32[]{:S(2)}, u32[]{:S(2)}) collective-permute-start(bf16[4,96,768]{2,1,0:T(8,128)(2,1)} %get-tuple-element.130), channel_id=1, source_target_pairs={{0,2},{1,3},{2,0},{3,1},{4,6},{5,7},{6,4},{7,5},{8,10},{9,11},{10,... | collective-permute-start | bytes 1769480 | tf_op jit(solution)/shard_map/ppermute | solution.py:81
  262.2 22.5 %collective-permute-start.34 = (bf16[4,96,768]{2,1,0:T(8,128)(2,1)}, bf16[4,96,768]{2,1,0:T(8,128)(2,1)}, u32[]{:S(2)}, u32[]{:S(2)}) collective-permute-start(bf16[4,96,768]{2,1,0:T(8,128)(2,1)} %get-tuple-element.132), channel_id=1, source_target_pairs={{0,4},{4,0},{8,12},{12,8},{16,20},{20,16},{24,28},{28,24},{1,5},{5... | collective-permute-start | bytes 1769480 | tf_op jit(solution)/shard_map/ppermute | solution.py:81
  270.4 30.8 %collective-permute-start.24 = (bf16[416,768]{1,0:T(8,128)(2,1)}, bf16[416,768]{1,0:T(8,128)(2,1)S(1)}, u32[]{:S(2)}, u32[]{:S(2)}) collective-permute-start(bf16[416,768]{1,0:T(8,128)(2,1)} %get-tuple-element.121), channel_id=1, source_target_pairs={{0,1},{1,0},{2,3},{3,2},{4,5},{5,4},{6,7},{7,6},{8,9},{9,8},{10,11... | collective-permute-start | bytes 1916936 | tf_op jit(solution)/shard_map/ppermute | solution.py:81
  281.7 21.2 %collective-permute-start.52 = (bf16[2,96,768]{2,1,0:T(8,128)(2,1)}, bf16[2,96,768]{2,1,0:T(8,128)(2,1)}, u32[]{:S(2)}, u32[]{:S(2)}) collective-permute-start(bf16[2,96,768]{2,1,0:T(8,128)(2,1)} %add_convert_fusion.2), channel_id=1, source_target_pairs={{0,4},{4,0},{8,12},{12,8},{16,20},{20,16},{24,28},{28,24},{1,5},{5... | collective-permute-start | bytes 884744 | tf_op jit(solution)/shard_map/ppermute | solution.py:81
  283.7 48.7 %collective-permute-start.33 = (bf16[2,96,768]{2,1,0:T(8,128)(2,1)}, bf16[2,96,768]{2,1,0:T(8,128)(2,1)}, u32[]{:S(2)}, u32[]{:S(2)}) collective-permute-start(bf16[2,96,768]{2,1,0:T(8,128)(2,1)} %add_convert_fusion.8), channel_id=1, source_target_pairs={{0,4},{4,0},{8,12},{12,8},{16,20},{20,16},{24,28},{28,24},{1,5},{5... | collective-permute-start | bytes 884744 | tf_op jit(solution)/shard_map/ppermute | solution.py:81
  286.4 19.0 %collective-permute-start.35 = (bf16[2,96,768]{2,1,0:T(8,128)(2,1)}, bf16[2,96,768]{2,1,0:T(8,128)(2,1)}, u32[]{:S(2)}, u32[]{:S(2)}) collective-permute-start(bf16[2,96,768]{2,1,0:T(8,128)(2,1)} %add_convert_fusion.7), channel_id=1, source_target_pairs={{0,2},{1,3},{2,0},{3,1},{4,6},{5,7},{6,4},{7,5},{8,10},{9,11},{10,... | collective-permute-start | bytes 884744 | tf_op jit(solution)/shard_map/ppermute | solution.py:81
  301.5 40.9 %collective-permute-start.26 = (bf16[416,768]{1,0:T(8,128)(2,1)S(1)}, bf16[416,768]{1,0:T(8,128)(2,1)S(1)}, u32[]{:S(2)}, u32[]{:S(2)}) collective-permute-start(bf16[416,768]{1,0:T(8,128)(2,1)S(1)} %multiply_convert_fusion.own_ref), channel_id=1, source_target_pairs={{0,2},{1,3},{2,0},{3,1},{4,6},{5,7},{6,4},{7,5},{8,10},{9,11},{10,... | collective-permute-start | bytes 1916936 | tf_op jit(solution)/shard_map/ppermute | solution.py:81
  303.0 68.7 %collective-permute-start.25 = (bf16[416,768]{1,0:T(8,128)(2,1)S(1)}, bf16[416,768]{1,0:T(8,128)(2,1)S(1)}, u32[]{:S(2)}, u32[]{:S(2)}) collective-permute-start(bf16[416,768]{1,0:T(8,128)(2,1)S(1)} %multiply_convert_fusion.own_ref), channel_id=1, source_target_pairs={{0,1},{1,0},{2,3},{3,2},{4,5},{5,4},{6,7},{7,6},{8,9},{9,8},{10,11... | collective-permute-start | bytes 1916936 | tf_op jit(solution)/shard_map/ppermute | solution.py:81
  304.2 23.5 %collective-permute-start.53 = (bf16[96,768]{1,0:T(8,128)(2,1)S(1)}, bf16[96,768]{1,0:T(8,128)(2,1)S(1)}, u32[]{:S(2)}, u32[]{:S(2)}) collective-permute-start(bf16[96,768]{1,0:T(8,128)(2,1)S(1)} %fusion.6), channel_id=1, source_target_pairs={{0,2},{1,3},{2,0},{3,1},{4,6},{5,7},{6,4},{7,5},{8,10},{9,11},{10,... | collective-permute-start | bytes 442376 | tf_op jit(solution)/shard_map/ppermute | solution.py:81
  305.4 19.6 %collective-permute-start.39 = (bf16[8,80,128]{2,1,0:T(8,128)(2,1)S(1)}, bf16[8,80,128]{2,1,0:T(8,128)(2,1)S(1)}, u32[]{:S(2)}, u32[]{:S(2)}) collective-permute-start(bf16[8,80,128]{2,1,0:T(8,128)(2,1)S(1)} %slice.298), channel_id=1, source_target_pairs={{0,2},{1,3},{2,0},{3,1},{4,6},{5,7},{6,4},{7,5},{8,10},{9,11},{10,... | collective-permute-start | bytes 491528 | tf_op jit(solution)/shard_map/ppermute | solution.py:81
  337.0 15.3 %collective-permute-start.30 = (bf16[416,768]{1,0:T(8,128)(2,1)S(1)}, bf16[416,768]{1,0:T(8,128)(2,1)S(1)}, u32[]{:S(2)}, u32[]{:S(2)}) collective-permute-start(bf16[416,768]{1,0:T(8,128)(2,1)S(1)} %copy-done.20), channel_id=1, source_target_pairs={{0,2},{1,3},{2,0},{3,1},{4,6},{5,7},{6,4},{7,5},{8,10},{9,11},{10,... | collective-permute-start | bytes 1916936 | tf_op jit(solution)/shard_map/ppermute | solution.py:81
  338.4 13.9 %collective-permute-start.37 = (bf16[96,768]{1,0:T(8,128)(2,1)S(1)}, bf16[96,768]{1,0:T(8,128)(2,1)S(1)}, u32[]{:S(2)}, u32[]{:S(2)}) collective-permute-start(bf16[96,768]{1,0:T(8,128)(2,1)S(1)} %fusion.4), channel_id=1, source_target_pairs={{0,16},{4,20},{8,24},{12,28},{16,0},{20,4},{24,8},{28,12},{1,17},{... | collective-permute-start | bytes 442376 | tf_op jit(solution)/shard_map/ppermute | solution.py:81
  341.3 38.0 %collective-permute-start.29 = (bf16[416,768]{1,0:T(8,128)(2,1)S(1)}, bf16[416,768]{1,0:T(8,128)(2,1)}, u32[]{:S(2)}, u32[]{:S(2)}) collective-permute-start(bf16[416,768]{1,0:T(8,128)(2,1)S(1)} %copy-done.20), channel_id=1, source_target_pairs={{0,1},{1,0},{2,3},{3,2},{4,5},{5,4},{6,7},{7,6},{8,9},{9,8},{10,11... | collective-permute-start | bytes 1916936 | tf_op jit(solution)/shard_map/ppermute | solution.py:81
  342.5 19.9 %collective-permute-start.55 = (f32[2,80,128]{2,1,0:T(8,128)}, f32[2,80,128]{2,1,0:T(8,128)}, u32[]{:S(2)}, u32[]{:S(2)}) collective-permute-start(f32[2,80,128]{2,1,0:T(8,128)} %pad_maximum_fusion.12), channel_id=1, source_target_pairs={{0,2},{1,3},{2,0},{3,1},{4,6},{5,7},{6,4},{7,5},{8,10},{9,11},{10,... | collective-permute-start | bytes 245768 | tf_op jit(solution)/shard_map/ppermute | solution.py:81
  352.3 19.4 %collective-permute-start.27 = (bf16[416,768]{1,0:T(8,128)(2,1)S(1)}, bf16[416,768]{1,0:T(8,128)(2,1)}, u32[]{:S(2)}, u32[]{:S(2)}) collective-permute-start(bf16[416,768]{1,0:T(8,128)(2,1)S(1)} %collective-permute-done.26.x_ref), channel_id=1, source_target_pairs={{0,1},{1,0},{2,3},{3,2},{4,5},{5,4},{6,7},{7,6},{8,9},{9,8},{10,11... | collective-permute-start | bytes 1916936 | tf_op jit(solution)/shard_map/ppermute | solution.py:81
  352.3 27.0 %collective-permute-start.31 = (bf16[416,768]{1,0:T(8,128)(2,1)S(1)}, bf16[416,768]{1,0:T(8,128)(2,1)}, u32[]{:S(2)}, u32[]{:S(2)}) collective-permute-start(bf16[416,768]{1,0:T(8,128)(2,1)S(1)} %collective-permute-done.30.x_ref), channel_id=1, source_target_pairs={{0,1},{1,0},{2,3},{3,2},{4,5},{5,4},{6,7},{7,6},{8,9},{9,8},{10,11... | collective-permute-start | bytes 1916936 | tf_op jit(solution)/shard_map/ppermute | solution.py:81
  (92 other events, 1040.9 us)

commit v3 on v2

--- a/solution.py
+++ b/solution.py
@@ -68,6 +68,8 @@
 
 
 def after(value, *others):
+    if isinstance(value, (list, tuple)):
+        return list(lax.optimization_barrier((*value, *others))[: len(value)])
     return lax.optimization_barrier((value, *others))[0]
 
 
@@ -92,64 +94,54 @@
         return self.flip(array, axis, bits)
 
     def gather_line(self, shard):
-        first = jnp.stack([shard, self.along(shard, "z2")])
-        return first, self.along(first, "z1")
-
-    def gather_plane(self, first, last):
+        near, far, last = (self.along(shard, name) for name in ("z1", "z2", "z3"))
+        return jnp.stack([shard, far]), jnp.stack([near, last])
+
+    def gather_side(self, first, last):
         first = jnp.concatenate([first, self.along(first, "y")])
         last = jnp.concatenate([last, self.along(last, "x")])
-        first_x = self.along(first, "x")
-        last_y = self.along(last, "y")
+        return first, last
+
+    def gather_rest(self, first, last):
         return [
             (first, [(0, 0), (0, 4), (0, 1), (0, 5)]),
-            (first_x, [(1, 0), (1, 4), (1, 1), (1, 5)]),
+            (self.along(first, "x"), [(1, 0), (1, 4), (1, 1), (1, 5)]),
             (last, [(0, 2), (0, 6), (1, 2), (1, 6)]),
-            (last_y, [(0, 3), (0, 7), (1, 3), (1, 7)]),
+            (self.along(last, "y"), [(0, 3), (0, 7), (1, 3), (1, 7)]),
         ]
 
-    def plane_first(self, shard):
-        pair = jnp.stack([shard, self.along(shard, "x")])
-        return jnp.concatenate([pair, self.along(pair, "y")])
-
-    def line_last(self, four):
-        eight = jnp.concatenate([four, self.along(four, "z2")])
-        spots = lambda k: [(x, 2 * k + y) for y in (0, 1) for x in (0, 1)]
-        return [(eight, spots(0) + spots(2)), (self.along(eight, "z1"), spots(1) + spots(3))]
-
     def grad_layout(self):
-        layout = []
-        for half, steps in enumerate(((0, 2), (1, 3))):
-            for first in (0, 1):
-                blocks = []
-                for second in (0, 1):
-                    x, y = (first, second) if half == 0 else (second, first)
-                    for k in steps:
-                        blocks.append((x, 2 * k + y))
-                layout.append(blocks)
-        return layout
-
-    def reduce(self, outs):
-        came_a = self.along(outs[1], "x")
-        came_b = self.along(outs[3], "y")
-        far_b = self.along(add(outs[2][2:], came_b[2:]), "x")
-        far_a = self.along(add(outs[0][2:], came_a[2:]), "y")
-        over = self.along(add(outs[2][:2], came_b[:2], far_b), "z1")
-        parts = (outs[0], came_a, far_a, over)
-        there = self.along(add(*[part[1] for part in parts]), "z2")
-        return [part[0] for part in parts] + [there]
-
-    def grad_layout_line(self):
-        spots = lambda k: [(x, 2 * k + y) for y in (0, 1) for x in (0, 1)]
-        return [spots(0), spots(2), spots(1) + spots(3)]
-
-    def reduce_line(self, outs):
-        came = self.along(outs[2], "z1")
-        there = self.along(add(outs[1], came[4:]), "z2")
-        parts = (outs[0], came[:4], there)
-        over = self.along(add(*[part[2:] for part in parts]), "y")
-        parts = (*parts, over)
-        last = self.along(add(*[part[1] for part in parts]), "x")
-        return [part[0] for part in parts] + [last]
+        return [
+            [
+                [(x, 0), (x, 4), (x, 1), (x, 5)],
+                [(x, 3), (x, 7)],
+                [(x, 2), (x, 6)],
+            ]
+            for x in (0, 1)
+        ]
+
+    def reduce_early(self, ones):
+        return self.along(ones[0], "x"), self.along(ones[1], "y")
+
+    def reduce_side(self, zeros, ones, early):
+        came_x, came_y = early
+        there = self.along(zeros[1], "y")
+        far_x = self.along(add(ones[2], came_y), "x")
+        far_y = self.along(add(zeros[0][2:], came_x[2:]), "y")
+        return there, far_x, far_y
+
+    def reduce_ends(self, zeros, early, side):
+        there, far_x, far_y = side
+        near = add(zeros[0][:2], early[0][:2], far_y)
+        last = add(zeros[2], there, far_x)
+        return near[0], near[1], last[0], last[1]
+
+    def reduce_line(self, own, far, near, last):
+        return [own, self.along(near, "z1"), self.along(far, "z2"), self.along(last, "z3")]
+
+
+def corner(array):
+    return array[:8, :128]
 
 
 def load_pieces(place_ref, piece_refs, spots, dst_ref, sems):
@@ -189,7 +181,7 @@
 
 
 def fold(rows):
-    return rows[:8] + rows[8:]
+    return jnp.sum(rows.reshape(-1, 8, rows.shape[1]), 0)
 
 
 def norm_scaled(rows):
@@ -208,10 +200,12 @@
 
 
 def over_rows(tokens, body, init):
+    step = 2 * CHUNK if tokens % (2 * CHUNK) == 0 else CHUNK
+
     def one(j, carry):
-        return body(pl.ds(pl.multiple_of(j * CHUNK, CHUNK), CHUNK), carry)
-
-    return lax.fori_loop(0, tokens // CHUNK, one, init)
+        return body(pl.ds(pl.multiple_of(j * step, step), step), carry)
+
+    return lax.fori_loop(0, tokens // step, one, init, unroll=2)
 
 
 def small_slot(place_ref, t_at, dp_at):
@@ -275,8 +269,10 @@
 def attend_body(images, patches, pad, spots, place_ref, normed_ref, bias_ref, *rest):
     n = len(spots)
     piece_refs = rest[:n]
-    qkv_ref, probs_ref, mixed_ref, branch_ref, full_ref, held, total, sems, out_sem = rest[n:]
-    columns = mixed_ref.shape[2]
+    branch_ref, full_ref = rest[n : n + 2]
+    per_block = rest[n + 2 : -4]
+    held, total, sems, out_sem = rest[-4:]
+    columns = held.shape[2] // 4
     heads = columns // HEAD_DIM
     wait_all(load_pieces(place_ref, piece_refs, spots, held, sems))
     out = pltpu.make_async_copy(held, full_ref, out_sem)
@@ -284,26 +280,27 @@
     lanes = lax.broadcasted_iota(jnp.int32, (pad, pad), 1)
 
     for b in range(held.shape[0]):
+        qkv_ref, probs_ref, mixed_ref = per_block[3 * b : 3 * b + 3]
         qkv = dot(normed_ref[...], held[b, :, : 3 * columns]) + bias_ref[place_ref[1] ^ (2 * b)]
-        qkv_ref[b] = qkv.astype(HALF)
-
-        def one(i, carry):
+        qkv_ref[...] = qkv.astype(HALF)
+
+        def one(i, carry, qkv_ref=qkv_ref, probs_ref=probs_ref, mixed_ref=mixed_ref):
             rows = pl.ds(pl.multiple_of(i * pad, CHUNK), pad)
             for h in range(heads):
                 at = h * HEAD_DIM
-                query = qkv_ref[b, rows, at : at + HEAD_DIM]
-                keys = qkv_ref[b, rows, columns + at : columns + at + HEAD_DIM]
-                values = qkv_ref[b, rows, 2 * columns + at : 2 * columns + at + HEAD_DIM]
+                query = qkv_ref[rows, at : at + HEAD_DIM]
+                keys = qkv_ref[rows, columns + at : columns + at + HEAD_DIM]
+                values = qkv_ref[rows, 2 * columns + at : 2 * columns + at + HEAD_DIM]
                 scores = row_dot(query, keys) * HEAD_DIM ** (-0.5)
                 scores = jnp.where(lanes < patches, scores, -1e30)
                 risen = jnp.exp(scores - jnp.max(scores, -1, keepdims=True))
                 probs = (risen * (1.0 / jnp.sum(risen, -1, keepdims=True))).astype(HALF)
-                probs_ref[b, i * heads + h] = probs
-                mixed_ref[b, rows, at : at + HEAD_DIM] = dot(probs, values).astype(HALF)
+                probs_ref[i * heads + h] = probs
+                mixed_ref[rows, at : at + HEAD_DIM] = dot(probs, values).astype(HALF)
             return carry
 
         lax.fori_loop(0, images, one, 0)
-        part = row_dot(mixed_ref[b], held[b, :, 3 * columns :])
+        part = row_dot(mixed_ref[...], held[b, :, 3 * columns :])
         if b == 0:
             total[...] = part
         elif b < held.shape[0] - 1:
@@ -395,14 +392,7 @@
     wait_all(store_grads(place_ref, grads, out_refs, layout, rows_out, grad_sems))
 
 
-def back_body(images, pad, layout, rows_out, place_ref, normed_grad_ref, came_ref, middle_ref, low_ref, table_ref, full_ref, qkv_ref, probs_ref, normed_ref, mixed_ref, *rest):
-    m = len(layout)
-    grad_middle_ref, grad_qkv_ref, sums_two_ref, sums_entry_ref = rest[:4]
-    out_refs = rest[4 : 4 + m]
-    half, grad_mixed, grads, grad_sems = rest[4 + m :]
-    blocks, tokens, columns = mixed_ref.shape
-    heads = columns // HEAD_DIM
-    scale = HEAD_DIM ** (-0.5)
+def middle_body(normed_grad_ref, came_ref, middle_ref, low_ref, table_ref, grad_middle_ref, half_ref, sums_two_ref):
     gain = table_ref[2:3, :]
 
     def one(rows, carry):
@@ -411,53 +401,66 @@
         low = low_ref[rows, :].astype(SINGLE)
         out = low + norm_grad(grad, scaled, inverse, gain)
         grad_middle_ref[rows, :] = out
-        half[rows, :] = out.astype(HALF)
+        half_ref[rows, :] = out.astype(HALF)
         parts = (grad * scaled, grad, out, low)
         return tuple(c + fold(p) for c, p in zip(carry, parts))
 
     zero = jnp.zeros((8, low_ref.shape[1]), SINGLE)
-    totals = over_rows(tokens, one, (zero,) * 4)
+    totals = over_rows(low_ref.shape[0], one, (zero,) * 4)
     for row, total in enumerate(totals):
         sums_two_ref[row] = total
 
-    for b in range(blocks):
-        grad_mixed[...] = dot(half[...], full_ref[b, :, 3 * columns :]).astype(HALF)
-
-        def attend(i, carry):
-            rows = pl.ds(pl.multiple_of(i * pad, CHUNK), pad)
-            for h in range(heads):
-                at = h * HEAD_DIM
-                query = qkv_ref[b, rows, at : at + HEAD_DIM]
-                keys = qkv_ref[b, rows, columns + at : columns + at + HEAD_DIM]
-                values = qkv_ref[b, rows, 2 * columns + at : 2 * columns + at + HEAD_DIM]
-                grad = grad_mixed[rows, at : at + HEAD_DIM]
-                low = probs_ref[b, i * heads + h]
-                probs = low.astype(SINGLE)
-                grad_qkv_ref[b, rows, 2 * columns + at : 2 * columns + at + HEAD_DIM] = column_dot(low, grad).astype(HALF)
-                grad_probs = row_dot(grad, values)
-                inner = jnp.sum(probs * grad_probs, -1, keepdims=True)
-                grad_scores = (probs * (grad_probs - inner)).astype(HALF)
-                grad_qkv_ref[b, rows, at : at + HEAD_DIM] = (dot(grad_scores, keys) * scale).astype(HALF)
-                grad_qkv_ref[b, rows, columns + at : columns + at + HEAD_DIM] = (column_dot(grad_scores, query) * scale).astype(HALF)
-            return carry
-
-        lax.fori_loop(0, images, attend, 0)
-        grads[b, :, : 3 * columns] = column_dot(normed_ref[...], grad_qkv_ref[b]).astype(HALF)
-        grads[b, :, 3 * columns :] = column_dot(half[...], mixed_ref[b]).astype(HALF)
-
-        def sums(rows, total):
-            return total + fold(grad_qkv_ref[b, rows, :].astype(SINGLE))
-
-        sums_entry_ref[b] = over_rows(tokens, sums, jnp.zeros((8, 3 * columns), SINGLE))
-    wait_all(store_grads(place_ref, grads, out_refs, layout, rows_out, grad_sems))
-
-
-def normed_body(place_ref, grad_qkv_ref, full_ref, keep_ref, send_ref, total):
-    blocks = grad_qkv_ref.shape[0]
-    width = grad_qkv_ref.shape[2]
-    total[...] = row_dot(grad_qkv_ref[0], full_ref[0, :, :width])
-    for b in range(1, blocks):
-        total[...] += row_dot(grad_qkv_ref[b], full_ref[b, :, :width])
+
+def back_body(b, images, pad, layout, rows_out, place_ref, half_ref, full_ref, qkv_ref, probs_ref, normed_ref, mixed_ref, *rest):
+    m = len(layout)
+    grad_qkv_ref, sums_entry_ref = rest[:2]
+    out_refs = rest[2 : 2 + m]
+    grad_mixed, grads, full, full_sem, grad_sems = rest[2 + m :]
+    tokens, columns = mixed_ref.shape
+    heads = columns // HEAD_DIM
+    scale = HEAD_DIM ** (-0.5)
+    copy = pltpu.make_async_copy(full_ref.at[b], full, full_sem)
+    copy.start()
+    copy.wait()
+    grad_mixed[...] = dot(half_ref[...], full[:, 3 * columns :]).astype(HALF)
+
+    def attend(i, carry):
+        rows = pl.ds(pl.multiple_of(i * pad, CHUNK), pad)
+        for h in range(heads):
+            at = h * HEAD_DIM
+            query = qkv_ref[rows, at : at + HEAD_DIM]
+            keys = qkv_ref[rows, columns + at : columns + at + HEAD_DIM]
+            values = qkv_ref[rows, 2 * columns + at : 2 * columns + at + HEAD_DIM]
+            grad = grad_mixed[rows, at : at + HEAD_DIM]
+            low = probs_ref[i * heads + h]
+            probs = low.astype(SINGLE)
+            grad_qkv_ref[rows, 2 * columns + at : 2 * columns + at + HEAD_DIM] = column_dot(low, grad).astype(HALF)
+            grad_probs = row_dot(grad, values)
+            inner = jnp.sum(probs * grad_probs, -1, keepdims=True)
+            grad_scores = (probs * (grad_probs - inner)).astype(HALF)
+            grad_qkv_ref[rows, at : at + HEAD_DIM] = (dot(grad_scores, keys) * scale).astype(HALF)
+            grad_qkv_ref[rows, columns + at : columns + at + HEAD_DIM] = (column_dot(grad_scores, query) * scale).astype(HALF)
+        return carry
+
+    lax.fori_loop(0, images, attend, 0)
+    grads[0, :, : 3 * columns] = column_dot(normed_ref[...], grad_qkv_ref[...]).astype(HALF)
+    grads[0, :, 3 * columns :] = column_dot(half_ref[...], mixed_ref[...]).astype(HALF)
+    copies = store_grads(place_ref, grads, out_refs, layout, rows_out, grad_sems)
+
+    def sums(rows, total):
+        return total + fold(grad_qkv_ref[rows, :].astype(SINGLE))
+
+    sums_entry_ref[...] = over_rows(tokens, sums, jnp.zeros((8, 3 * columns), SINGLE))
+    wait_all(copies)
+
+
+def normed_body(place_ref, full_ref, *rest):
+    grad_qkv_refs = rest[:-3]
+    keep_ref, send_ref, total = rest[-3:]
+    width = grad_qkv_refs[0].shape[1]
+    total[...] = row_dot(grad_qkv_refs[0][...], full_ref[0, :, :width])
+    for b, ref in enumerate(grad_qkv_refs[1:], 1):
+        total[...] += row_dot(ref[...], full_ref[b, :, :width])
     count = keep_ref.shape[0]
     core = place_ref[1] & 1
     keep_ref[...] = total[pl.ds(pl.multiple_of(core * count, count), count), :]
@@ -475,14 +478,15 @@
     send_ref[...] = total[pl.ds(pl.multiple_of((1 - core) * count, count), count), :].astype(HALF)
 
 
-def end_body(images, patches, pad, packed, place_ref, keep_ref, came_ref, start_ref, grad_middle_ref, mask_ref, table_ref, sums_two_ref, sums_entry_ref, sums_expand_ref, *rest):
+def end_body(images, patches, pad, packed, place_ref, keep_ref, came_ref, start_ref, grad_middle_ref, mask_ref, table_ref, sums_two_ref, sums_expand_ref, *rest):
+    blocks = sums_expand_ref.shape[0]
+    sums_entry_refs, rest = rest[:blocks], rest[blocks:]
     if packed:
         out_ref, small_ref, ended, spot = rest
     else:
         out_ref, spot, entry_ref, expand_ref, ended = rest
     count, width = keep_ref.shape
-    columns = sums_entry_ref.shape[2] // 3
-    blocks = sums_entry_ref.shape[0]
+    columns = sums_entry_refs[0].shape[1] // 3
     core = place_ref[1] & 1
     gain = table_ref[0:1, :]
 
@@ -499,7 +503,7 @@
         return tuple(c + fold(p) for c, p in zip(carry, parts))
 
     zero = jnp.zeros((8, width), SINGLE)
-    totals = lax.fori_loop(0, count // CHUNK, one, (zero,) * 3)
+    totals = lax.fori_loop(0, count // CHUNK, one, (zero,) * 3, unroll=2)
     place = ended[:pad, :]
     for i in range(1, images):
         place = place + ended[i * pad : (i + 1) * pad, :]
@@ -516,7 +520,7 @@
         entry_ref[...] = jnp.zeros_like(entry_ref)
         expand_ref[...] = jnp.zeros_like(expand_ref)
         for b in range(blocks):
-            entry_ref[place_ref[1] ^ (2 * b)] = column(sums_entry_ref[b])
+            entry_ref[place_ref[1] ^ (2 * b)] = column(sums_entry_refs[b][...])
             expand_ref[place_ref[1] ^ (2 * b)] = column(sums_expand_ref[b])
         return
     n_tensor = 2 * blocks
@@ -532,7 +536,7 @@
         for b in range(blocks):
             dp_flip = place_ref[0] ^ dp_at
             slot = b * 8 + (dp_flip & 1) * 4 + (dp_flip >> 1)
-            entry = column(sums_entry_ref[b])
+            entry = column(sums_entry_refs[b][...])
             expand = column(sums_expand_ref[b])
             wide = expand[:, part * dp_at : part * (dp_at + 1)]
             short = entry[:, own * dp_at : own * (dp_at + 1)]
@@ -600,21 +604,18 @@
             ]
         )
         small = jnp.pad(jnp.concatenate([block, bias_rows]), ((0, 0), (0, 128 - rows)))
+        small = after(small, attn_shard)
         attn_line = swap.gather_line(attn_shard)
         small = jnp.stack([small] + [swap.along(small, f"z{k}") for k in (1, 2, 3)])
-        for name in ("y", "x", "core"):
-            small = jnp.concatenate([small, swap.along(small, name)])
-        reduce_plane = swap.plane_first(reduce_shard)
+        small = jnp.concatenate([small, swap.along(small, "y")])
+        attn_side = swap.gather_side(*attn_line)
+        small = jnp.concatenate([small, swap.along(small, "x")])
         expand_line = swap.gather_line(after(expand_shard, *attn_line))
-        attn_pieces = swap.gather_plane(*attn_line)
-        reduce_pieces = swap.line_last(after(reduce_plane, *expand_line))
-        arrived = [attn_pieces[1][0], attn_pieces[3][0]]
-        expand_line = lax.optimization_barrier((*expand_line, *arrived))
-        expand_pieces = swap.gather_plane(*expand_line[:2])
+        reduce_line = swap.gather_line(after(reduce_shard, *expand_line))
+        attn_pieces = swap.gather_rest(*attn_side)
+        small = jnp.concatenate([small, swap.along(small, "core")])
         layout = swap.grad_layout()
-        layout_line = swap.grad_layout_line()
-        grad_outs = [shape((len(where), rows, width), HALF) for where in layout]
-        grad_outs_line = [shape((len(where), rows, width), HALF) for where in layout_line]
+        outs_for = lambda holds: [shape((len(where), rows, width), HALF) for where in holds]
         rows_out = rows
     else:
         def gather(shard):
@@ -627,8 +628,8 @@
         attn_pieces = gather(attn_shard)
         expand_pieces = gather(expand_shard)
         reduce_pieces = gather(reduce_shard)
-        layout = layout_line = [[(b, None)] for b in range(blocks)]
-        grad_outs = grad_outs_line = [shape((1, width, width), HALF) for _ in layout]
+        layout = [[[(b, None)]] for b in range(blocks)]
+        outs_for = lambda holds: [shape((1, width, width), HALF) for _ in holds]
         rows_out = width
         everywhere = lambda array, axis: lax.all_gather(array.astype(HALF), "dp", axis=axis, tiled=True)
         place = jnp.pad(everywhere(position, 1), ((0, 256 - patch_count), (0, 0))).astype(SINGLE)
@@ -677,30 +678,39 @@
         "start",
     )
 
+    if direct:
+        expand_side = swap.gather_side(*after(expand_line, normed_one))
+        expand_pieces = swap.gather_rest(*expand_side)
+        reduce_side = swap.gather_side(*after(reduce_line, *expand_side))
+        reduce_pieces = swap.gather_rest(*reduce_side)
+        normed_one = after(normed_one, *expand_side, *reduce_line)
+
+    per_block = [
+        (shape((tokens, 3 * columns), HALF), VMEM),
+        (shape((images * heads, pad, pad), HALF), VMEM),
+        (shape((tokens, columns), HALF), VMEM),
+    ]
     operands, spots = pieces_of(attn_pieces)
-    qkv, probs, mixed, branch, attn_full = kernel_call(
+    branch, attn_full, *kept = kernel_call(
         functools.partial(attend_body, images, patch_count, pad, spots),
-        [
-            qkv_half,
-            (shape((blocks, images * heads, pad, pad), HALF), VMEM),
-            (shape((blocks, tokens, columns), HALF), VMEM),
-            whole_half,
-            weight,
-        ],
-        at_in
-        + [(after(normed_one, reduce_pieces[0][0]), VMEM), (entry_shift, VMEM)]
-        + operands,
+        [whole_half, weight] + per_block * blocks,
+        at_in + [(normed_one, VMEM), (entry_shift, VMEM)] + operands,
         [held, wide, many, sem],
         16,
         "attend",
     )
+    if direct:
+        flag = swap.along(corner(branch), "core")
+        branch = after(branch, flag, *[piece for piece, _ in expand_pieces], *reduce_side)
     branch_came = swap.along(branch, "core")
+    flat = [where for parts in layout for where in parts]
+    by_flip = lambda outs: [outs[len(layout[0]) * b : len(layout[0]) * (b + 1)] for b in range(blocks)]
 
     operands, spots = pieces_of(expand_pieces)
     middle, normed_two, active, slope, expand_full, *grad_reduce = kernel_call(
-        functools.partial(up_body, spots, layout_line, rows_out),
+        functools.partial(up_body, spots, flat, rows_out),
         [whole_single, whole_half, hidden_half, hidden_half, weight]
-        + [(a, ANY) for a in grad_outs_line],
+        + [(a, ANY) for a in outs_for(flat)],
         at_in
         + [(a, VMEM) for a in (start, branch, branch_came, low, table, expand_shift)]
         + operands,
@@ -708,6 +718,9 @@
         22,
         "up",
     )
+    grad_reduce = by_flip(grad_reduce)
+    if direct:
+        reduce_early = swap.reduce_early(grad_reduce[1])
 
     operands, spots = pieces_of(reduce_pieces)
     grad_upper, normed_grad, reduce_full, sums_expand = kernel_call(
@@ -719,36 +732,26 @@
         "down",
     )
     normed_came = swap.along(normed_grad, "core")
+    if direct:
+        normed_two = after(normed_two, *reduce_early)
+        reduce_side = swap.reduce_side(*grad_reduce, after(reduce_early, grad_upper))
 
     grad_expand = kernel_call(
-        functools.partial(expand_body, layout, rows_out),
-        [(a, ANY) for a in grad_outs],
+        functools.partial(expand_body, flat, rows_out),
+        [(a, ANY) for a in outs_for(flat)],
         at_in + [(a, VMEM) for a in (normed_two, grad_upper)],
         [held, many],
         5,
         "expand",
     )
-
-    grad_middle, grad_qkv, sums_two, sums_entry, *grad_attn = kernel_call(
-        functools.partial(back_body, images, pad, layout, rows_out),
-        [
-            whole_single,
-            qkv_half,
-            (shape((4, 8, width), SINGLE), VMEM),
-            (shape((blocks, 8, 3 * columns), SINGLE), VMEM),
-        ]
-        + [(a, ANY) for a in grad_outs],
-        at_in
-        + [(a, VMEM) for a in (normed_grad, normed_came, middle, low, table, attn_full, qkv, probs, normed_one, mixed)],
-        [pltpu.VMEM((tokens, width), HALF), pltpu.VMEM((tokens, columns), HALF), held, many],
-        26,
-        "back",
-    )
+    grad_expand = by_flip(grad_expand)
+    if direct:
+        expand_early = swap.reduce_early(grad_expand[1])
 
     out_keep, out_send = kernel_call(
         output_body,
         [share_single, share_half],
-        at_in + [(a, VMEM) for a in (middle, after(active, grad_qkv), reduce_full, table)],
+        at_in + [(a, VMEM) for a in (middle, after(active, grad_expand[0][0]), reduce_full, table)],
         [wide],
         6,
         "output",
@@ -759,43 +762,57 @@
     )
     own_out = ((out_keep + out_came.astype(SINGLE)) * live_rows[:, None]).astype(HALF)
 
-    grad_keep, grad_send = kernel_call(
-        normed_body,
-        [share_single, share_half],
-        at_in + [(a, VMEM) for a in (grad_qkv, attn_full)],
-        [wide],
-        5,
-        "normed",
-    )
-    grad_came = swap.along(grad_send, "core")
-
-    small_out = (
-        [(shape((n_dp * n_tensor, SMALL_ROWS, 128), HALF), VMEM)]
-        if direct
-        else [
-            (shape((4 * PLACE_ROWS, width), SINGLE), VMEM),
-            (shape((n_tensor, 1, 3 * columns), SINGLE), VMEM),
-            (shape((n_tensor, 1, hidden), SINGLE), VMEM),
-        ]
-    )
-    end_scratch = [pltpu.VMEM((share * pad, width), SINGLE)]
-    if direct:
-        end_scratch.append(pltpu.VMEM((4 * PLACE_ROWS, width), SINGLE))
-    own_grad, *small_grads = kernel_call(
-        functools.partial(end_body, share, patch_count, pad, direct),
-        [share_half] + small_out,
-        at_in
-        + [
-            (a, VMEM)
-            for a in (grad_keep, grad_came, start, grad_middle, mask, table, sums_two, sums_entry, sums_expand)
-        ],
-        end_scratch,
+    if direct:
+        normed_grad = after(normed_grad, *reduce_side, out_keep)
+        reduce_ends = swap.reduce_ends(grad_reduce[0], reduce_early, after(reduce_side, out_keep))
+        reduce_parts = swap.reduce_line(*reduce_ends)
+    grad_middle, half, sums_two = kernel_call(
+        middle_body,
+        [whole_single, whole_half, (shape((4, 8, width), SINGLE), VMEM)],
+        [(a, VMEM) for a in (normed_grad, normed_came, middle, low, table)],
+        [],
         8,
-        "end",
-    )
-
-    def spread(piece):
-        far = swap.along(piece, "x")
+        "middle",
+    )
+
+    def back(b, half):
+        return kernel_call(
+            functools.partial(back_body, b, images, pad, [[(0, dp_flip) for _, dp_flip in where] for where in layout[b]], rows_out),
+            [(shape((tokens, 3 * columns), HALF), VMEM), (shape((8, 3 * columns), SINGLE), VMEM)]
+            + [(a, ANY) for a in outs_for(layout[b])],
+            at_in
+            + [(half, VMEM), (attn_full, ANY)]
+            + [(a, VMEM) for a in (*kept[3 * b : 3 * b + 2], normed_one, kept[3 * b + 2])],
+            [pltpu.VMEM((tokens, columns), HALF), pltpu.VMEM((1, width, width), HALF), pltpu.VMEM((width, width), HALF), sem, many],
+            16,
+            "back",
+        )
+
+    backs = [None] * blocks
+    if direct:
+        backs[1] = back(1, after(half, *expand_early, own_out))
+        expand_early = after(expand_early, half)
+        expand_side = swap.reduce_side(after(grad_expand[0], half), grad_expand[1], expand_early)
+        out_far = swap.along(after(own_out, half), "x")
+        flag = swap.along(corner(backs[1][1]), "core")
+        backs[0] = back(0, after(half, *expand_side, *reduce_parts, flag))
+        attn_early = swap.reduce_early(after(backs[1][2:], flag))
+        expand_ends = swap.reduce_ends(grad_expand[0], expand_early, after(expand_side, flag))
+        expand_parts = swap.reduce_line(*expand_ends)
+        flag = swap.along(corner(backs[0][1]), "core")
+        attn_side = swap.reduce_side(after(backs[0][2:], flag), backs[1][2:], attn_early)
+        before_normed = (flag, out_far, *attn_early)
+        before_end = (*expand_parts, *attn_side)
+    else:
+        for b in range(blocks):
+            backs[b] = back(b, half)
+        out_far = swap.along(own_out, "x")
+        before_normed = before_end = ()
+    grad_qkv = [outs[0] for outs in backs]
+    sums_entry = [outs[1] for outs in backs]
+    grad_attn = [outs[2:] for outs in backs]
+
+    def spread(piece, far):
         near = swap.along(piece, "core")
         return kernel_call(
             functools.partial(place_body, share, patch_count, pad),
@@ -806,21 +823,60 @@
             "spread",
         )[0]
 
-    block_out = spread(own_out)
-    patch_grad = spread(own_grad)
+    block_out = spread(own_out, out_far)
+    grad_keep, grad_send = kernel_call(
+        normed_body,
+        [share_single, share_half],
+        at_in + [(after(attn_full, *before_normed), VMEM)] + [(a, VMEM) for a in grad_qkv],
+        [wide],
+        5,
+        "normed",
+    )
+    grad_came = swap.along(grad_send, "core")
+
+    small_out = (
+        [(shape((n_dp * n_tensor, SMALL_ROWS, 128), HALF), VMEM)]
+        if direct
+        else [
+            (shape((4 * PLACE_ROWS, width), SINGLE), VMEM),
+            (shape((n_tensor, 1, 3 * columns), SINGLE), VMEM),
+            (shape((n_tensor, 1, hidden), SINGLE), VMEM),
+        ]
+    )
+    end_scratch = [pltpu.VMEM((share * pad, width), SINGLE)]
+    if direct:
+        end_scratch.append(pltpu.VMEM((4 * PLACE_ROWS, width), SINGLE))
+    own_grad, *small_grads = kernel_call(
+        functools.partial(end_body, share, patch_count, pad, direct),
+        [share_half] + small_out,
+        at_in
+        + [
+            (a, VMEM)
+            for a in (after(grad_keep, *before_end, block_out), grad_came, start, grad_middle, mask, table, sums_two, sums_expand, *sums_entry)
+        ],
+        end_scratch,
+        8,
+        "end",
+    )
+
+    grad_far = swap.along(own_grad, "x")
+    patch_grad = spread(own_grad, grad_far)
 
     sum_up = lambda parts: sum(part.astype(SINGLE) for part in parts)
     if direct:
-        grad_reduce = lax.optimization_barrier((*grad_reduce, grad_upper))[:-1]
-        reduced = sum_up(swap.reduce_line(grad_reduce)).T
-        expanded = sum_up(swap.reduce(grad_expand))
-        attn = sum_up(swap.reduce(grad_attn))
+        reduced = sum_up(reduce_parts).T
+        expanded = sum_up(expand_parts)
+        attn = sum_up(swap.reduce_line(*swap.reduce_ends(grad_attn[0], attn_early, attn_side)))
         (small,) = small_grads
-        for name, count in (("core", 16), ("x", 8), ("y", 4)):
-            small = add(small[:count], swap.along(small[count:], name))
-        small = sum_up([small[0]] + [swap.along(small[k], f"z{k}") for k in (1, 2, 3)])
-        pair = jnp.stack([small, swap.along(small, "core")])
-        four = jnp.concatenate([pair, swap.along(pair, "x")])
+        small = add(small[:16], swap.along(small[16:], "core"))
+        small = small.reshape(2, 2, 4, SMALL_ROWS, 128)
+        small = add(small[:, 0], swap.along(small[:, 1], "y"))
+        small = sum_up([small[:, 0]] + [swap.along(small[:, k], f"z{k}") for k in (1, 2, 3)])
+        small = after(small, grad_far)
+        pair = small + swap.along(small[::-1], "x")
+        other = swap.along(pair, "core")
+        small = pair[0]
+        four = jnp.stack([pair[0], other[0], pair[1], other[1]])
         four = [lax.dynamic_index_in_dim(four, tensor ^ t, 0, keepdims=False) for t in range(n_tensor)]
         spot = jnp.concatenate([part[:PLACE_ROWS, :rows] for part in four])
         grad_place = spot[:patch_count]
@@ -834,9 +890,9 @@
                 mine = mine + swap.flip(outs[b][0], "tensor", 2 * b).astype(SINGLE)
             return lax.psum_scatter(mine, "dp", scatter_dimension=0, tiled=True)
 
-        reduced = total(grad_reduce).T
-        expanded = total(grad_expand)
-        attn = total(grad_attn)
+        reduced = total([outs[0] for outs in grad_reduce]).T
+        expanded = total([outs[0] for outs in grad_expand])
+        attn = total([outs[0] for outs in grad_attn])
         spot, entry_part, expand_part = small_grads
         spot = lax.psum(lax.psum_scatter(spot, "dp", scatter_dimension=1, tiled=True), "tensor")
         grad_place = spot[:patch_count]

time: 388 us -> 326 us (0.84)
  waiting for transfers between devices: 92.3 us -> 24.5 us
  Pallas kernels: 154 us -> 132 us
  starting transfers between devices: 52.2 us -> 74 us
  other arithmetic: 36.9 us -> 41.5 us
    ppermute x56 -> x70, waiting for transfers between devices: 92.3 us -> 24.5 us  [flip(): return lax.ppermute(array, axis, [(i, i ^ bits) for i in range(count)])]
    pallas_call x11 -> x13, Pallas kernels: 154 us -> 132 us  [kernel_call(): pl.pallas_call(body, out_shape=[a for a, _ in outs], in_specs=[spec for _...]
    ppermute x56 -> x70, starting transfers between devices: 52.2 us -> 74 us  [flip(): return lax.ppermute(array, axis, [(i, i ^ bits) for i in range(count)])]
    unnamed x164 -> x171, local copies, waits for them, and re-layouts: 40.6 us -> 31 us
    another operation x5 -> x7, other arithmetic: 2.92 us -> 7.88 us  [the longest x6 7.87 us: gather_line(): return (jnp.stack([shard, far]), jnp.stack([near, last]))]
    squeeze x1 -> x7, local copies, waits for them, and re-layouts: 0.01 us -> 4.21 us  [the longest x6 4.2 us: reduce_ends(): return (near[0], near[1], last[0], last[1])]
    convert_element_type x11 -> x14, other arithmetic: 11.5 us -> 14.1 us  [add(): return total.astype(HALF)]
  transfers between devices with their start and end apart: 56 -> 70, of which waited for: 16 -> 10; matrix products, arithmetic and copies ran while one was open for 18% -> 23% of each run, Pallas kernels for 29% -> 40%
where the time goes in v3:
time: 326 us; the launch traced here: 321 us
  Pallas kernels  132 us (40%)
  starting transfers between devices  74 us (23%)
  local copies, waits for them, and re-layouts  46 us (14%)
  other arithmetic  41.5 us (13%)
  waiting for transfers between devices  24.5 us (8%)
    pallas_call x13, Pallas kernels, kernel_call(): pl.pallas_call(body, out_shape=[a for a, _ in outs], in_specs=[spec for _...  132 us
    ppermute x70, starting transfers between devices, flip(): return lax.ppermute(array, axis, [(i, i ^ bits) for i in range(count)])  74 us
    unnamed x171, local copies, waits for them, and re-layouts  31 us
    ppermute x70, waiting for transfers between devices, flip(): return lax.ppermute(array, axis, [(i, i ^ bits) for i in range(count)])  24.5 us
    convert_element_type x14, other arithmetic, add(): return total.astype(HALF)  14.1 us
    another operation x6, other arithmetic, gather_line(): return (jnp.stack([shard, far]), jnp.stack([near, last]))  7.87 us
    convert_element_type x8, other arithmetic, adamw(): return (master, moment, second, master.astype(jnp.bfloat16))  7.56 us
  transfers between devices with their start and end apart: 70, of which 10 were waited for; matrix products, arithmetic and copies ran while one was open for 23% of the time, Pallas kernels for 40%

profile of v3, /device:TPU:0, one launch (start us, length us, event | category | flops | bytes accessed | tf_op | source)
XLA Modules:
  0.0 320.7 jit_solution(11003458672021293197)
XLA Ops:
  7.6 3.1 collective-permute-start
  10.7 2.6 collective-permute-start.1
  14.1 2.9 collective-permute-start.8
  32.7 2.7 collective-permute-start.11
  37.1 1.9 copy.149.patch_ref
  39.4 2.0 copy.150.cot_ref
  46.1 2.7 collective-permute-done.9
  57.4 8.7 %start.1 = (f32[832,768]{1,0:T(8,128)}, bf16[832,768]{1,0:T(8,128)(2,1)}, bf16[832,768]{1,0:T(8,128)(2,1)}, f32[8,768]{1,0:T(8,128)}, f32[4,1,576]{2,1,0:T(1,128)}, /*index=5*/f32[4,1,768]{2,1,0:T(1,128)}) custom-call(s32[2]{0:T(128)} %pad_add_fusion.place_ref, bf16[8,196,768]{2,1,0:T(8,128)(2,1)} %copy.149.patch_ref, bf16[8,196,768]{2,1,0:T(8,128)(2,1)} %copy.150.cot_ref, ...), custom_call_target="tpu_custom_call" | custom-call | flops 10000000 | bytes 1024 | tf_op jit(solution)/shard_map/start/pallas_call | solution.py:48
  69.9 5.0 %collective-permute-done.13 = bf16[2,96,768]{2,1,0:T(8,128)(2,1)S(1)} collective-permute-done((bf16[2,96,768]{2,1,0:T(8,128)(2,1)S(1)}, bf16[2,96,768]{2,1,0:T(8,128)(2,1)S(1)}, u32[]{:S(2)}, u32[]{:S(2)}) %collective-permute-start.13) | collective-permute-done | bytes 294944 | tf_op jit(solution)/shard_map/ppermute | solution.py:83
  82.9 17.8 %attend.1 = (bf16[832,768]{1,0:T(8,128)(2,1)}, bf16[2,768,768]{2,1,0:T(8,128)(2,1)}, bf16[832,576]{1,0:T(8,128)(2,1)}, bf16[12,208,208]{2,1,0:T(8,128)(2,1)}, bf...) custom-call(s32[2]{0:T(128)} %pad_add_fusion.place_ref, ...), custom_call_target="tpu_custom_call" | custom-call | flops 16000000 | bytes 1024 | tf_op jit(solution)/shard_map/attend/pallas_call | solution.py:48
  107.3 20.2 %up.1 = (f32[832,768]{1,0:T(8,128)}, bf16[832,768]{1,0:T(8,128)(2,1)}, bf16[2,832,768]{2,1,0:T(8,128)(2,1)}, bf16[2,832,768]{2,1,0:T(8,128)(2,1)}, bf16[2,768,76...) custom-call(s32[2]{0:T(128)} %pad_add_fusion.place_ref, ...), custom_call_target="tpu_custom_call" | custom-call | flops 22000000 | bytes 1024 | tf_op jit(solution)/shard_map/up/pallas_call | solution.py:48
  135.1 13.1 %down.1 = (bf16[2,832,768]{2,1,0:T(8,128)(2,1)}, bf16[832,768]{1,0:T(8,128)(2,1)}, bf16[2,768,768]{2,1,0:T(8,128)(2,1)}, f32[2,8,768]{2,1,0:T(8,128)}) custom-call(s32[2]{0:T(128)} %pad_add_fusion.place_ref, bf16[832,768]{1,0:T(8,128)(2,1)} %get-tuple-element.147.low_ref, bf16[2,832,768]{2,1,0:T(8,128)(2,1)} %get-tuple-element.156.slope_ref, ...), custom_call_target="tpu_custom_call" | custom-call | flops 12000000 | bytes 1024 | tf_op jit(solution)/shard_map/down/pallas_call | solution.py:48
  153.6 6.5 %expand.1 = (bf16[4,96,768]{2,1,0:T(8,128)(2,1)}, bf16[2,96,768]{2,1,0:T(8,128)(2,1)}, bf16[2,96,768]{2,1,0:T(8,128)(2,1)}, bf16[4,96,768]{2,1,0:T(8,128)(2,1)},...) custom-call(s32[2]{0:T(128)} %pad_add_fusion.place_ref, bf16[832,768]{1,0:T(8,128)(2,1)} %get-tuple-element.155.normed_ref, ...), custom_call_target="tpu_custom_call" | custom-call | flops 5000000 | bytes 1024 | tf_op jit(solution)/shard_map/expand/pallas_call | solution.py:48
  160.2 7.2 %output.1 = (f32[416,768]{1,0:T(8,128)}, bf16[416,768]{1,0:T(8,128)(2,1)}) custom-call(s32[2]{0:T(128)} %pad_add_fusion.place_ref, f32[832,768]{1,0:T(8,128)} %get-tuple-element.150.middle_ref, bf16[2,832,768]{2,1,0:T(8,128)(2,1)} %get-tuple-element.160.active_ref, bf16[2,768,768]{2,1,0:T(8,128)(2,1)} %get-tuple-element.161.reduce_ref, ...), custom_call_target="tpu_custom_call" | custom-call | flops 6000000 | bytes 1024 | tf_op jit(solution)/shard_map/output/pallas_call | solution.py:48
  172.2 2.4 collective-permute-start.44
  177.6 8.8 %middle.1 = (f32[832,768]{1,0:T(8,128)}, bf16[832,768]{1,0:T(8,128)(2,1)}, f32[4,8,768]{2,1,0:T(8,128)}) custom-call(bf16[832,768]{1,0:T(8,128)(2,1)} %get-tuple-element.170.normed_grad_ref, bf16[832,768]{1,0:T(8,128)(2,1)} %copy-done.11, f32[832,768]{1,0:T(8,128)} %get-tuple-element.150.middle_ref, bf16[832,768]{1,0:T(8,128)(2,1)} %get-tuple-element.147.low_ref, ...), custom_call_target="tpu_custom_call" | custom-call | flops 8000000 | bytes 1024 | tf_op jit(solution)/shard_map/middle/pallas_call | solution.py:48
  193.0 13.9 %back.2 = (bf16[832,576]{1,0:T(8,128)(2,1)}, f32[8,576]{1,0:T(8,128)}, bf16[4,96,768]{2,1,0:T(8,128)(2,1)}, bf16[2,96,768]{2,1,0:T(8,128)(2,1)}, bf16[2,96,768]{2,1,0:T(8,128)(2,1)}) custom-call(s32[2]{0:T(128)} %pad_add_fusion.place_ref, bf16[832,768]{1,0:T(8,128)(2,1)} %get-tuple-element.192.half_ref, bf16[2,768,768]{2,1,0:T(8,128)(2,1)} %get-tuple-element.202.full_ref, ...), custom_call_target="tpu_custom_call" | custom-call | flops 16000000 | bytes 1024 | tf_op jit(solution)/shard_map/back/pallas_call | solution.py:48
  207.6 2.2 fusion.26
  213.6 14.0 %back.3 = (bf16[832,576]{1,0:T(8,128)(2,1)}, f32[8,576]{1,0:T(8,128)}, bf16[4,96,768]{2,1,0:T(8,128)(2,1)}, bf16[2,96,768]{2,1,0:T(8,128)(2,1)}, bf16[2,96,768]{2,1,0:T(8,128)(2,1)}) custom-call(s32[2]{0:T(128)} %pad_add_fusion.place_ref, bf16[832,768]{1,0:T(8,128)(2,1)} %get-tuple-element.192.half_ref, bf16[2,768,768]{2,1,0:T(8,128)(2,1)} %get-tuple-element.202.full_ref, ...), custom_call_target="tpu_custom_call" | custom-call | flops 16000000 | bytes 1024 | tf_op jit(solution)/shard_map/back/pallas_call | solution.py:48
  235.8 4.4 %collective-permute-done.48 = bf16[4,96,768]{2,1,0:T(8,128)(2,1)} collective-permute-done((bf16[4,96,768]{2,1,0:T(8,128)(2,1)}, bf16[4,96,768]{2,1,0:T(8,128)(2,1)}, u32[]{:S(2)}, u32[]{:S(2)}) %collective-permute-start.48) | collective-permute-done | bytes 589856 | tf_op jit(solution)/shard_map/ppermute | solution.py:83
  243.5 2.0 collective-permute-done.54
  247.0 6.3 %normed.1 = (f32[416,768]{1,0:T(8,128)}, bf16[416,768]{1,0:T(8,128)(2,1)}) custom-call(s32[2]{0:T(128)} %pad_add_fusion.place_ref, bf16[2,768,768]{2,1,0:T(8,128)(2,1)} %get-tuple-element.202.full_ref, bf16[832,576]{1,0:T(8,128)(2,1)} %get-tuple-element.203.rest_0_, bf16[832,576]{1,0:T(8,128)(2,1)} %get-tuple-element.204.rest_1_), custom_call_target="tpu_custom_call" | custom-call | flops 5000000 | bytes 1024 | tf_op jit(solution)/shard_map/normed/pallas_call | solution.py:48
  256.2 2.6 collective-permute-start.52
  261.3 3.3 %spread.2 = bf16[8,196,768]{2,1,0:T(8,128)(2,1)} custom-call(s32[2]{0:T(128)} %pad_add_fusion.place_ref, bf16[416,768]{1,0:T(8,128)(2,1)} %copy-done.1, bf16[416,768]{1,0:T(8,128)(2,1)} %copy-done.20, bf16[416,768]{1,0:T(8,128)(2,1)} %copy-done.21, bf16[416,768]{1,0:T(8,128)(2,1)} %copy-done.24), custom_call_target="tpu_custom_call" | custom-call | flops 3000000 | bytes 1024 | tf_op jit(solution)/shard_map/spread/pallas_call | solution.py:48
  268.0 8.8 %end.1 = (bf16[416,768]{1,0:T(8,128)(2,1)}, bf16[32,80,128]{2,1,0:T(8,128)(2,1)}) custom-call(s32[2]{0:T(128)} %pad_add_fusion.place_ref, f32[416,768]{1,0:T(8,128)} %get-tuple-element.214.keep_ref, bf16[416,768]{1,0:T(8,128)(2,1)} %copy-done.23, f32[832,768]{1,0:T(8,128)} %get-tuple-element.135.start_ref, f32[832,768]{1,0:T(8,128)} %get-tuple-element.216.grad_middle_ref, ...), custom_call_target="tpu_custom_call" | custom-call | flops 8000000 | bytes 1024 | tf_op jit(solution)/shard_map/end/pallas_call | solution.py:48
  277.9 2.3 fusion.31
  284.3 3.8 %collective-permute-done.64 = bf16[2,4,80,128]{3,2,0,1:T(8,128)(2,1)S(1)} collective-permute-done((bf16[2,4,80,128]{3,2,0,1:T(8,128)(2,1)S(1)}, bf16[2,4,80,128]{3,2,0,1:T(8,128)(2,1)S(1)}, u32[]{:S(2)}, u32[]{:S(2)}) %collective-permute-start.64) | collective-permute-done | bytes 163872 | tf_op jit(solution)/shard_map/ppermute | solution.py:83
  288.2 2.0 collective-permute-start.65
  290.2 2.5 collective-permute-start.67
  296.1 3.1 collective-permute-done.58.x_ref
  313.4 3.3 %spread.3 = bf16[8,196,768]{2,1,0:T(8,128)(2,1)} custom-call(s32[2]{0:T(128)} %pad_add_fusion.place_ref, bf16[416,768]{1,0:T(8,128)(2,1)} %get-tuple-element.219.own_ref, bf16[416,768]{1,0:T(8,128)(2,1)} %collective-permute-done.57.core_ref, bf16[416,768]{1,0:T(8,128)(2,1)} %collective-permute-done.58.x_ref, bf16[416,768]{1,0:T(8,128)(2,1)} %copy-done.22), custom_call_target="tpu_custom_call" | custom-call | flops 3000000 | bytes 1024 | tf_op jit(solution)/shard_map/spread/pallas_call | solution.py:48
  316.6 3.6 %copy.168 = bf16[8,196,768]{2,0,1:T(8,128)(2,1)} copy(bf16[8,196,768]{2,1,0:T(8,128)(2,1)} %spread.3) | data formatting | bytes 4816896
  (381 shorter events, 132.2 us)
Async XLA Ops:
  49.8 17.8 %collective-permute-start.16 = (bf16[96,768]{1,0:T(8,128)(2,1)}, bf16[96,768]{1,0:T(8,128)(2,1)}, u32[]{:S(2)}, u32[]{:S(2)}) collective-permute-start(bf16[96,768]{1,0:T(8,128)(2,1)} %convert_bitcast_fusion), channel_id=1, source_target_pairs={{0,24},{4,28},{8,16},{12,20},{16,8},{20,12},{24,0},{28,4},{1,25},{... | collective-permute-start | bytes 442376 | tf_op jit(solution)/shard_map/ppermute | solution.py:83
  51.5 26.2 %collective-permute-start.14 = (bf16[96,768]{1,0:T(8,128)(2,1)}, bf16[96,768]{1,0:T(8,128)(2,1)}, u32[]{:S(2)}, u32[]{:S(2)}) collective-permute-start(bf16[96,768]{1,0:T(8,128)(2,1)} %convert_bitcast_fusion), channel_id=1, source_target_pairs={{0,16},{4,20},{8,24},{12,28},{16,0},{20,4},{24,8},{28,12},{1,17},{... | collective-permute-start | bytes 442376 | tf_op jit(solution)/shard_map/ppermute | solution.py:83
  54.3 25.6 %collective-permute-start.20 = (bf16[4,96,768]{2,1,0:T(8,128)(2,1)S(1)}, bf16[4,96,768]{2,1,0:T(8,128)(2,1)}, u32[]{:S(2)}, u32[]{:S(2)}) collective-permute-start(bf16[4,96,768]{2,1,0:T(8,128)(2,1)S(1)} %pad_maximum_fusion.1.rest_2_), channel_id=1, source_target_pairs={{0,4},{4,0},{8,12},{12,8},{16,20},{20,16},{24,28},{28,24},{1,5},{5... | collective-permute-start | bytes 1769480 | tf_op jit(solution)/shard_map/ppermute | solution.py:83
  56.0 26.9 %collective-permute-start.18 = (bf16[4,96,768]{2,1,0:T(8,128)(2,1)S(1)}, bf16[4,96,768]{2,1,0:T(8,128)(2,1)}, u32[]{:S(2)}, u32[]{:S(2)}) collective-permute-start(bf16[4,96,768]{2,1,0:T(8,128)(2,1)S(1)} %pad_maximum_fusion.rest_0_), channel_id=1, source_target_pairs={{0,2},{1,3},{2,0},{3,1},{4,6},{5,7},{6,4},{7,5},{8,10},{9,11},{10,... | collective-permute-start | bytes 1769480 | tf_op jit(solution)/shard_map/ppermute | solution.py:83
  75.0 28.0 %collective-permute-start.22 = (bf16[4,96,768]{2,1,0:T(8,128)(2,1)S(1)}, bf16[4,96,768]{2,1,0:T(8,128)(2,1)}, u32[]{:S(2)}, u32[]{:S(2)}) collective-permute-start(bf16[4,96,768]{2,1,0:T(8,128)(2,1)S(1)} %constant_dynamic-update-slice_fusion.20.rest_2_), channel_id=1, source_target_pairs={{0,4},{4,0},{8,12},{12,8},{16,20},{20,16},{24,28},{28,24},{1,5},{5... | collective-permute-start | bytes 1769480 | tf_op jit(solution)/shard_map/ppermute | solution.py:83
  76.1 26.9 %collective-permute-start.21 = (bf16[4,96,768]{2,1,0:T(8,128)(2,1)S(1)}, bf16[4,96,768]{2,1,0:T(8,128)(2,1)}, u32[]{:S(2)}, u32[]{:S(2)}) collective-permute-start(bf16[4,96,768]{2,1,0:T(8,128)(2,1)S(1)} %constant_dynamic-update-slice_fusion.18.rest_0_), channel_id=1, source_target_pairs={{0,2},{1,3},{2,0},{3,1},{4,6},{5,7},{6,4},{7,5},{8,10},{9,11},{10,... | collective-permute-start | bytes 1769480 | tf_op jit(solution)/shard_map/ppermute | solution.py:83
  79.4 21.4 %collective-permute-start.24 = (bf16[2,96,768]{2,1,0:T(8,128)(2,1)}, bf16[2,96,768]{2,1,0:T(8,128)(2,1)}, u32[]{:S(2)}, u32[]{:S(2)}) collective-permute-start(bf16[2,96,768]{2,1,0:T(8,128)(2,1)} %pad_maximum_fusion.7), channel_id=1, source_target_pairs={{0,2},{1,3},{2,0},{3,1},{4,6},{5,7},{6,4},{7,5},{8,10},{9,11},{10,... | collective-permute-start | bytes 884744 | tf_op jit(solution)/shard_map/ppermute | solution.py:83
  79.9 21.8 %collective-permute-start.23 = (bf16[2,96,768]{2,1,0:T(8,128)(2,1)}, bf16[2,96,768]{2,1,0:T(8,128)(2,1)}, u32[]{:S(2)}, u32[]{:S(2)}) collective-permute-start(bf16[2,96,768]{2,1,0:T(8,128)(2,1)} %pad_maximum_fusion.6), channel_id=1, source_target_pairs={{0,4},{4,0},{8,12},{12,8},{16,20},{20,16},{24,28},{28,24},{1,5},{5... | collective-permute-start | bytes 884744 | tf_op jit(solution)/shard_map/ppermute | solution.py:83
  103.1 32.0 %collective-permute-start.29 = (bf16[4,96,768]{2,1,0:T(8,128)(2,1)S(1)}, bf16[4,96,768]{2,1,0:T(8,128)(2,1)}, u32[]{:S(2)}, u32[]{:S(2)}) collective-permute-start(bf16[4,96,768]{2,1,0:T(8,128)(2,1)S(1)} %constant_dynamic-update-slice_fusion.24.rest_2_), channel_id=1, source_target_pairs={{0,4},{4,0},{8,12},{12,8},{16,20},{20,16},{24,28},{28,24},{1,5},{5... | collective-permute-start | bytes 1769480 | tf_op jit(solution)/shard_map/ppermute | solution.py:83
  104.2 31.0 %collective-permute-start.28 = (bf16[4,96,768]{2,1,0:T(8,128)(2,1)S(1)}, bf16[4,96,768]{2,1,0:T(8,128)(2,1)}, u32[]{:S(2)}, u32[]{:S(2)}) collective-permute-start(bf16[4,96,768]{2,1,0:T(8,128)(2,1)S(1)} %constant_dynamic-update-slice_fusion.22.rest_0_), channel_id=1, source_target_pairs={{0,2},{1,3},{2,0},{3,1},{4,6},{5,7},{6,4},{7,5},{8,10},{9,11},{10,... | collective-permute-start | bytes 1769480 | tf_op jit(solution)/shard_map/ppermute | solution.py:83
  127.5 20.8 %collective-permute-start.26 = (bf16[4,96,768]{2,1,0:T(8,128)(2,1)}, bf16[4,96,768]{2,1,0:T(8,128)(2,1)S(1)}, u32[]{:S(2)}, u32[]{:S(2)}) collective-permute-start(bf16[4,96,768]{2,1,0:T(8,128)(2,1)} %get-tuple-element.153), channel_id=1, source_target_pairs={{0,2},{1,3},{2,0},{3,1},{4,6},{5,7},{6,4},{7,5},{8,10},{9,11},{10,... | collective-permute-start | bytes 1769480 | tf_op jit(solution)/shard_map/ppermute | solution.py:83
  129.3 19.0 %collective-permute-start.27 = (bf16[2,96,768]{2,1,0:T(8,128)(2,1)}, bf16[2,96,768]{2,1,0:T(8,128)(2,1)}, u32[]{:S(2)}, u32[]{:S(2)}) collective-permute-start(bf16[2,96,768]{2,1,0:T(8,128)(2,1)} %get-tuple-element.154), channel_id=1, source_target_pairs={{0,4},{4,0},{8,12},{12,8},{16,20},{20,16},{24,28},{28,24},{1,5},{5... | collective-permute-start | bytes 884744 | tf_op jit(solution)/shard_map/ppermute | solution.py:83
  133.9 33.5 %collective-permute-start.32 = (bf16[2,96,768]{2,1,0:T(8,128)(2,1)}, bf16[2,96,768]{2,1,0:T(8,128)(2,1)}, u32[]{:S(2)}, u32[]{:S(2)}) collective-permute-start(bf16[2,96,768]{2,1,0:T(8,128)(2,1)} %get-tuple-element.165), channel_id=1, source_target_pairs={{0,4},{4,0},{8,12},{12,8},{16,20},{20,16},{24,28},{28,24},{1,5},{5... | collective-permute-start | bytes 884744 | tf_op jit(solution)/shard_map/ppermute | solution.py:83
  148.3 28.3 %collective-permute-start.35 = (bf16[832,768]{1,0:T(8,128)(2,1)}, bf16[832,768]{1,0:T(8,128)(2,1)S(1)}, u32[]{:S(2)}, u32[]{:S(2)}) collective-permute-start(bf16[832,768]{1,0:T(8,128)(2,1)} %get-tuple-element.170.normed_grad_ref), channel_id=1, source_target_pairs={{0,1},{1,0},{2,3},{3,2},{4,5},{5,4},{6,7},{7,6},{8,9},{9,8},{10,11... | collective-permute-start | bytes 3833864 | tf_op jit(solution)/shard_map/ppermute | solution.py:83
  149.3 19.6 %collective-permute-start.34 = (bf16[2,96,768]{2,1,0:T(8,128)(2,1)}, bf16[2,96,768]{2,1,0:T(8,128)(2,1)}, u32[]{:S(2)}, u32[]{:S(2)}) collective-permute-start(bf16[2,96,768]{2,1,0:T(8,128)(2,1)} %add_convert_fusion.11), channel_id=1, source_target_pairs={{0,4},{4,0},{8,12},{12,8},{16,20},{20,16},{24,28},{28,24},{1,5},{5... | collective-permute-start | bytes 884744 | tf_op jit(solution)/shard_map/ppermute | solution.py:83
  151.1 19.0 %collective-permute-start.33 = (bf16[2,96,768]{2,1,0:T(8,128)(2,1)S(1)}, bf16[2,96,768]{2,1,0:T(8,128)(2,1)S(1)}, u32[]{:S(2)}, u32[]{:S(2)}) collective-permute-start(bf16[2,96,768]{2,1,0:T(8,128)(2,1)S(1)} %add_convert_fusion.12), channel_id=1, source_target_pairs={{0,2},{1,3},{2,0},{3,1},{4,6},{5,7},{6,4},{7,5},{8,10},{9,11},{10,... | collective-permute-start | bytes 884744 | tf_op jit(solution)/shard_map/ppermute | solution.py:83
  167.3 24.7 %collective-permute-start.30 = (bf16[416,768]{1,0:T(8,128)(2,1)}, bf16[416,768]{1,0:T(8,128)(2,1)S(1)}, u32[]{:S(2)}, u32[]{:S(2)}) collective-permute-start(bf16[416,768]{1,0:T(8,128)(2,1)} %get-tuple-element.163), channel_id=1, source_target_pairs={{0,1},{1,0},{2,3},{3,2},{4,5},{5,4},{6,7},{7,6},{8,9},{9,8},{10,11... | collective-permute-start | bytes 1916936 | tf_op jit(solution)/shard_map/ppermute | solution.py:83
  167.3 20.1 %collective-permute-start.39 = (bf16[4,96,768]{2,1,0:T(8,128)(2,1)}, bf16[4,96,768]{2,1,0:T(8,128)(2,1)}, u32[]{:S(2)}, u32[]{:S(2)}) collective-permute-start(bf16[4,96,768]{2,1,0:T(8,128)(2,1)} %get-tuple-element.178), channel_id=1, source_target_pairs={{0,2},{1,3},{2,0},{3,1},{4,6},{5,7},{6,4},{7,5},{8,10},{9,11},{10,... | collective-permute-start | bytes 1769480 | tf_op jit(solution)/shard_map/ppermute | solution.py:83
  168.9 17.5 %collective-permute-start.40 = (bf16[2,96,768]{2,1,0:T(8,128)(2,1)}, bf16[2,96,768]{2,1,0:T(8,128)(2,1)S(1)}, u32[]{:S(2)}, u32[]{:S(2)}) collective-permute-start(bf16[2,96,768]{2,1,0:T(8,128)(2,1)} %get-tuple-element.179), channel_id=1, source_target_pairs={{0,4},{4,0},{8,12},{12,8},{16,20},{20,16},{24,28},{28,24},{1,5},{5... | collective-permute-start | bytes 884744 | tf_op jit(solution)/shard_map/ppermute | solution.py:83
  172.2 19.2 %collective-permute-start.44 = (bf16[96,768]{1,0:T(8,128)(2,1)}, bf16[96,768]{1,0:T(8,128)(2,1)S(1)}, u32[]{:S(2)}, u32[]{:S(2)}) collective-permute-start(bf16[96,768]{1,0:T(8,128)(2,1)} %slice_bitcast_fusion.9), channel_id=1, source_target_pairs={{0,16},{4,20},{8,24},{12,28},{16,0},{20,4},{24,8},{28,12},{1,17},{... | collective-permute-start | bytes 442376 | tf_op jit(solution)/shard_map/ppermute | solution.py:83
  176.5 31.0 %collective-permute-start.43 = (bf16[96,768]{1,0:T(8,128)(2,1)}, bf16[96,768]{1,0:T(8,128)(2,1)}, u32[]{:S(2)}, u32[]{:S(2)}) collective-permute-start(bf16[96,768]{1,0:T(8,128)(2,1)} %get-tuple-element.366), channel_id=1, source_target_pairs={{0,8},{4,12},{8,0},{12,4},{16,24},{20,28},{24,16},{28,20},{1,9},{5... | collective-permute-start | bytes 442376 | tf_op jit(solution)/shard_map/ppermute | solution.py:83
  186.4 21.1 %collective-permute-start.45 = (bf16[96,768]{1,0:T(8,128)(2,1)}, bf16[96,768]{1,0:T(8,128)(2,1)}, u32[]{:S(2)}, u32[]{:S(2)}) collective-permute-start(bf16[96,768]{1,0:T(8,128)(2,1)} %get-tuple-element.365), channel_id=1, source_target_pairs={{0,24},{4,28},{8,16},{12,20},{16,8},{20,12},{24,0},{28,4},{1,25},{... | collective-permute-start | bytes 442376 | tf_op jit(solution)/shard_map/ppermute | solution.py:83
  189.3 22.7 %collective-permute-start.42 = (bf16[2,96,768]{2,1,0:T(8,128)(2,1)}, bf16[2,96,768]{2,1,0:T(8,128)(2,1)}, u32[]{:S(2)}, u32[]{:S(2)}) collective-permute-start(bf16[2,96,768]{2,1,0:T(8,128)(2,1)} %add_convert_fusion.9), channel_id=1, source_target_pairs={{0,4},{4,0},{8,12},{12,8},{16,20},{20,16},{24,28},{28,24},{1,5},{5... | collective-permute-start | bytes 884744 | tf_op jit(solution)/shard_map/ppermute | solution.py:83
  191.4 20.8 %collective-permute-start.41 = (bf16[2,96,768]{2,1,0:T(8,128)(2,1)S(1)}, bf16[2,96,768]{2,1,0:T(8,128)(2,1)}, u32[]{:S(2)}, u32[]{:S(2)}) collective-permute-start(bf16[2,96,768]{2,1,0:T(8,128)(2,1)S(1)} %add_convert_fusion.10), channel_id=1, source_target_pairs={{0,2},{1,3},{2,0},{3,1},{4,6},{5,7},{6,4},{7,5},{8,10},{9,11},{10,... | collective-permute-start | bytes 884744 | tf_op jit(solution)/shard_map/ppermute | solution.py:83
  192.0 21.6 %collective-permute-start.38 = (bf16[2,96,768]{2,1,0:T(8,128)(2,1)}, bf16[2,96,768]{2,1,0:T(8,128)(2,1)}, u32[]{:S(2)}, u32[]{:S(2)}) collective-permute-start(bf16[2,96,768]{2,1,0:T(8,128)(2,1)} %get-tuple-element.176), channel_id=1, source_target_pairs={{0,4},{4,0},{8,12},{12,8},{16,20},{20,16},{24,28},{28,24},{1,5},{5... | collective-permute-start | bytes 884744 | tf_op jit(solution)/shard_map/ppermute | solution.py:83
  209.7 46.4 %collective-permute-start.31 = (bf16[416,768]{1,0:T(8,128)(2,1)S(1)}, bf16[416,768]{1,0:T(8,128)(2,1)S(1)}, u32[]{:S(2)}, u32[]{:S(2)}) collective-permute-start(bf16[416,768]{1,0:T(8,128)(2,1)S(1)} %multiply_convert_fusion.own_ref), channel_id=1, source_target_pairs={{0,1},{1,0},{2,3},{3,2},{4,5},{5,4},{6,7},{7,6},{8,9},{9,8},{10,11... | collective-permute-start | bytes 1916936 | tf_op jit(solution)/shard_map/ppermute | solution.py:83
  210.2 36.8 %collective-permute-start.36 = (bf16[416,768]{1,0:T(8,128)(2,1)S(1)}, bf16[416,768]{1,0:T(8,128)(2,1)S(1)}, u32[]{:S(2)}, u32[]{:S(2)}) collective-permute-start(bf16[416,768]{1,0:T(8,128)(2,1)S(1)} %multiply_convert_fusion.own_ref), channel_id=1, source_target_pairs={{0,2},{1,3},{2,0},{3,1},{4,6},{5,7},{6,4},{7,5},{8,10},{9,11},{10,... | collective-permute-start | bytes 1916936 | tf_op jit(solution)/shard_map/ppermute | solution.py:83
  211.9 28.3 %collective-permute-start.48 = (bf16[4,96,768]{2,1,0:T(8,128)(2,1)}, bf16[4,96,768]{2,1,0:T(8,128)(2,1)}, u32[]{:S(2)}, u32[]{:S(2)}) collective-permute-start(bf16[4,96,768]{2,1,0:T(8,128)(2,1)} %get-tuple-element.200), channel_id=1, source_target_pairs={{0,2},{1,3},{2,0},{3,1},{4,6},{5,7},{6,4},{7,5},{8,10},{9,11},{10,... | collective-permute-start | bytes 1769480 | tf_op jit(solution)/shard_map/ppermute | solution.py:83
  212.3 19.3 %collective-permute-start.49 = (bf16[2,96,768]{2,1,0:T(8,128)(2,1)}, bf16[2,96,768]{2,1,0:T(8,128)(2,1)}, u32[]{:S(2)}, u32[]{:S(2)}) collective-permute-start(bf16[2,96,768]{2,1,0:T(8,128)(2,1)} %get-tuple-element.201), channel_id=1, source_target_pairs={{0,4},{4,0},{8,12},{12,8},{16,20},{20,16},{24,28},{28,24},{1,5},{5... | collective-permute-start | bytes 884744 | tf_op jit(solution)/shard_map/ppermute | solution.py:83
  240.2 24.4 %collective-permute-start.51 = (bf16[96,768]{1,0:T(8,128)(2,1)}, bf16[96,768]{1,0:T(8,128)(2,1)}, u32[]{:S(2)}, u32[]{:S(2)}) collective-permute-start(bf16[96,768]{1,0:T(8,128)(2,1)} %slice_bitcast_fusion.5), channel_id=1, source_target_pairs={{0,16},{4,20},{8,24},{12,28},{16,0},{20,4},{24,8},{28,12},{1,17},{... | collective-permute-start | bytes 442376 | tf_op jit(solution)/shard_map/ppermute | solution.py:83
  260.3 19.9 %collective-permute-start.60 = (bf16[96,768]{1,0:T(8,128)(2,1)}, bf16[96,768]{1,0:T(8,128)(2,1)}, u32[]{:S(2)}, u32[]{:S(2)}) collective-permute-start(bf16[96,768]{1,0:T(8,128)(2,1)} %get-tuple-element.361), channel_id=1, source_target_pairs={{0,8},{4,12},{8,0},{12,4},{16,24},{20,28},{24,16},{28,20},{1,9},{5... | collective-permute-start | bytes 442376 | tf_op jit(solution)/shard_map/ppermute | solution.py:83
  282.5 16.7 %collective-permute-start.58 = (bf16[416,768]{1,0:T(8,128)(2,1)S(1)}, bf16[416,768]{1,0:T(8,128)(2,1)}, u32[]{:S(2)}, u32[]{:S(2)}) collective-permute-start(bf16[416,768]{1,0:T(8,128)(2,1)S(1)} %copy-done.19), channel_id=1, source_target_pairs={{0,2},{1,3},{2,0},{3,1},{4,6},{5,7},{6,4},{7,5},{8,10},{9,11},{10,... | collective-permute-start | bytes 1916936 | tf_op jit(solution)/shard_map/ppermute | solution.py:83
  (109 other events, 1091.7 us)

commit v4 on v3

--- a/solution.py
+++ b/solution.py
@@ -269,44 +269,40 @@
 def attend_body(images, patches, pad, spots, place_ref, normed_ref, bias_ref, *rest):
     n = len(spots)
     piece_refs = rest[:n]
-    branch_ref, full_ref = rest[n : n + 2]
-    per_block = rest[n + 2 : -4]
-    held, total, sems, out_sem = rest[-4:]
+    branch_ref, full_ref, qkv_ref, probs_ref, mixed_ref, held, total, sems, out_sem = rest[n:]
     columns = held.shape[2] // 4
     heads = columns // HEAD_DIM
     wait_all(load_pieces(place_ref, piece_refs, spots, held, sems))
     out = pltpu.make_async_copy(held, full_ref, out_sem)
     out.start()
     lanes = lax.broadcasted_iota(jnp.int32, (pad, pad), 1)
-
-    for b in range(held.shape[0]):
-        qkv_ref, probs_ref, mixed_ref = per_block[3 * b : 3 * b + 3]
+    total[...] = jnp.zeros_like(total)
+
+    def block(b, carry):
         qkv = dot(normed_ref[...], held[b, :, : 3 * columns]) + bias_ref[place_ref[1] ^ (2 * b)]
-        qkv_ref[...] = qkv.astype(HALF)
-
-        def one(i, carry, qkv_ref=qkv_ref, probs_ref=probs_ref, mixed_ref=mixed_ref):
+        qkv_ref[b] = qkv.astype(HALF)
+
+        def one(i, inner):
             rows = pl.ds(pl.multiple_of(i * pad, CHUNK), pad)
             for h in range(heads):
                 at = h * HEAD_DIM
-                query = qkv_ref[rows, at : at + HEAD_DIM]
-                keys = qkv_ref[rows, columns + at : columns + at + HEAD_DIM]
-                values = qkv_ref[rows, 2 * columns + at : 2 * columns + at + HEAD_DIM]
+                query = qkv_ref[b, rows, at : at + HEAD_DIM]
+                keys = qkv_ref[b, rows, columns + at : columns + at + HEAD_DIM]
+                values = qkv_ref[b, rows, 2 * columns + at : 2 * columns + at + HEAD_DIM]
                 scores = row_dot(query, keys) * HEAD_DIM ** (-0.5)
                 scores = jnp.where(lanes < patches, scores, -1e30)
                 risen = jnp.exp(scores - jnp.max(scores, -1, keepdims=True))
                 probs = (risen * (1.0 / jnp.sum(risen, -1, keepdims=True))).astype(HALF)
-                probs_ref[i * heads + h] = probs
-                mixed_ref[rows, at : at + HEAD_DIM] = dot(probs, values).astype(HALF)
-            return carry
+                probs_ref[b, i * heads + h] = probs
+                mixed_ref[b, rows, at : at + HEAD_DIM] = dot(probs, values).astype(HALF)
+            return inner
 
         lax.fori_loop(0, images, one, 0)
-        part = row_dot(mixed_ref[...], held[b, :, 3 * columns :])
-        if b == 0:
-            total[...] = part
-        elif b < held.shape[0] - 1:
-            total[...] += part
-        else:
-            branch_ref[...] = (total[...] + part).astype(HALF)
+        total[...] += row_dot(mixed_ref[b], held[b, :, 3 * columns :])
+        return carry
+
+    lax.fori_loop(0, held.shape[0], block, 0)
+    branch_ref[...] = total[...].astype(HALF)
     out.wait()
 
 
@@ -361,7 +357,9 @@
     wait_all(load_pieces(place_ref, piece_refs, spots, held, sems))
     out = pltpu.make_async_copy(held, reduce_ref, out_sem)
     out.start()
-    for b in range(held.shape[0]):
+    total[...] = jnp.zeros_like(total)
+
+    def block(b, carry):
         upper[...] = dot(low_ref[...], held[b])
 
         def bend(rows, sums):
@@ -370,13 +368,11 @@
             return sums + fold(grad.astype(SINGLE))
 
         sums_ref[b] = over_rows(tokens, bend, jnp.zeros((8, upper.shape[1]), SINGLE))
-        part = row_dot(grad_upper_ref[b], expand_ref[b])
-        if b == 0:
-            total[...] = part
-        elif b < held.shape[0] - 1:
-            total[...] += part
-        else:
-            normed_grad_ref[...] = (total[...] + part).astype(HALF)
+        total[...] += row_dot(grad_upper_ref[b], expand_ref[b])
+        return carry
+
+    lax.fori_loop(0, held.shape[0], block, 0)
+    normed_grad_ref[...] = total[...].astype(HALF)
     out.wait()
 
 
@@ -416,6 +412,7 @@
     grad_qkv_ref, sums_entry_ref = rest[:2]
     out_refs = rest[2 : 2 + m]
     grad_mixed, grads, full, full_sem, grad_sems = rest[2 + m :]
+    qkv_ref, probs_ref, mixed_ref = (ref.at[b] for ref in (qkv_ref, probs_ref, mixed_ref))
     tokens, columns = mixed_ref.shape
     heads = columns // HEAD_DIM
     scale = HEAD_DIM ** (-0.5)
@@ -468,9 +465,13 @@
 
 
 def output_body(place_ref, middle_ref, active_ref, reduce_ref, table_ref, keep_ref, send_ref, total):
-    total[...] = row_dot(active_ref[0], reduce_ref[0])
-    for b in range(1, active_ref.shape[0]):
+    total[...] = jnp.zeros_like(total)
+
+    def block(b, carry):
         total[...] += row_dot(active_ref[b], reduce_ref[b])
+        return carry
+
+    lax.fori_loop(0, active_ref.shape[0], block, 0)
     count = keep_ref.shape[0]
     core = place_ref[1] & 1
     rows = pl.ds(pl.multiple_of(core * count, count), count)
@@ -552,6 +553,29 @@
             out_ref[(place_ref[1] ^ flip) * images + i] = ref[i * pad : i * pad + patches, :]
 
 
+def exit_body(grad_ref, master_ref, moment_ref, second_ref, *out_refs):
+    outs = adamw(master_ref[...], moment_ref[...], second_ref[...], grad_ref[...].T, 0.05, 0.05)
+    for ref, out in zip(out_refs, outs):
+        ref[...] = out
+
+
+def tables_body(place_ref, pair_ref, other_ref, *rest):
+    place_refs, table_refs, place_outs, table_outs = rest[:3], rest[3:6], rest[6:10], rest[10:14]
+    four, spot = rest[14:]
+    for flip, ref in enumerate((pair_ref, other_ref)):
+        four[flip] = ref[0]
+        four[2 + flip] = ref[1]
+    for t in range(4):
+        spot[PLACE_ROWS * t : PLACE_ROWS * (t + 1), :] = four[place_ref[1] ^ t][:PLACE_ROWS]
+    rows, patches = place_refs[0].shape
+    grad = spot[...].T[:rows, :patches]
+    for ref, out in zip(place_outs, adamw(*[ref[...] for ref in place_refs], grad, 0.1, 0.0)):
+        ref[...] = out
+    grad = spot[200:208, :][:7, :rows]
+    for ref, out in zip(table_outs, adamw(*[ref[...] for ref in table_refs], grad, 0.3, 0.0)):
+        ref[...] = out
+
+
 def local(sizes, *arguments):
     (patches, cotangent, mask_rank, mask_count, image_count,
      entry_weight, entry_moment, entry_second, entry_bias, entry_bias_moment, entry_bias_second,
@@ -682,18 +706,16 @@
         expand_side = swap.gather_side(*after(expand_line, normed_one))
         expand_pieces = swap.gather_rest(*expand_side)
         reduce_side = swap.gather_side(*after(reduce_line, *expand_side))
-        reduce_pieces = swap.gather_rest(*reduce_side)
-        normed_one = after(normed_one, *expand_side, *reduce_line)
 
     per_block = [
-        (shape((tokens, 3 * columns), HALF), VMEM),
-        (shape((images * heads, pad, pad), HALF), VMEM),
-        (shape((tokens, columns), HALF), VMEM),
+        (shape((blocks, tokens, 3 * columns), HALF), VMEM),
+        (shape((blocks, images * heads, pad, pad), HALF), VMEM),
+        (shape((blocks, tokens, columns), HALF), VMEM),
     ]
     operands, spots = pieces_of(attn_pieces)
     branch, attn_full, *kept = kernel_call(
         functools.partial(attend_body, images, patch_count, pad, spots),
-        [whole_half, weight] + per_block * blocks,
+        [whole_half, weight] + per_block,
         at_in + [(normed_one, VMEM), (entry_shift, VMEM)] + operands,
         [held, wide, many, sem],
         16,
@@ -702,6 +724,7 @@
     if direct:
         flag = swap.along(corner(branch), "core")
         branch = after(branch, flag, *[piece for piece, _ in expand_pieces], *reduce_side)
+        reduce_pieces = swap.gather_rest(*after(reduce_side, flag))
     branch_came = swap.along(branch, "core")
     flat = [where for parts in layout for where in parts]
     by_flip = lambda outs: [outs[len(layout[0]) * b : len(layout[0]) * (b + 1)] for b in range(blocks)]
@@ -782,7 +805,7 @@
             + [(a, ANY) for a in outs_for(layout[b])],
             at_in
             + [(half, VMEM), (attn_full, ANY)]
-            + [(a, VMEM) for a in (*kept[3 * b : 3 * b + 2], normed_one, kept[3 * b + 2])],
+            + [(a, VMEM) for a in (*kept[:2], normed_one, kept[2])],
             [pltpu.VMEM((tokens, columns), HALF), pltpu.VMEM((1, width, width), HALF), pltpu.VMEM((width, width), HALF), sem, many],
             16,
             "back",
@@ -866,21 +889,37 @@
     if direct:
         reduced = sum_up(reduce_parts).T
         expanded = sum_up(expand_parts)
-        attn = sum_up(swap.reduce_line(*swap.reduce_ends(grad_attn[0], attn_early, attn_side)))
+        attn_parts = swap.reduce_line(*swap.reduce_ends(grad_attn[0], attn_early, attn_side))
         (small,) = small_grads
         small = add(small[:16], swap.along(small[16:], "core"))
         small = small.reshape(2, 2, 4, SMALL_ROWS, 128)
         small = add(small[:, 0], swap.along(small[:, 1], "y"))
+        attn = sum_up(after(attn_parts, small))
         small = sum_up([small[:, 0]] + [swap.along(small[:, k], f"z{k}") for k in (1, 2, 3)])
         small = after(small, grad_far)
         pair = small + swap.along(small[::-1], "x")
-        other = swap.along(pair, "core")
+        other = swap.along(after(pair, patch_grad), "core")
         small = pair[0]
-        four = jnp.stack([pair[0], other[0], pair[1], other[1]])
-        four = [lax.dynamic_index_in_dim(four, tensor ^ t, 0, keepdims=False) for t in range(n_tensor)]
-        spot = jnp.concatenate([part[:PLACE_ROWS, :rows] for part in four])
-        grad_place = spot[:patch_count]
-        grad_table = spot[200:207]
+        updated = lambda like: [(shape(like.shape, kind), VMEM) for kind in (SINGLE, SINGLE, SINGLE, HALF)]
+        exits = kernel_call(
+            exit_body,
+            updated(exit_weight),
+            [(a, VMEM) for a in (attn[:, 3 * columns :], exit_weight, exit_moment, exit_second)],
+            [],
+            2,
+            "exit",
+        )
+        tables = kernel_call(
+            tables_body,
+            updated(position.T) + updated(vectors),
+            at_in
+            + [(a, VMEM) for a in (pair, other, position.T, position_moment.T, position_second.T, vectors, vectors_moment, vectors_second)],
+            [pltpu.VMEM((4, SMALL_ROWS, 128), SINGLE), pltpu.VMEM((4 * PLACE_ROWS, 128), SINGLE)],
+            2,
+            "tables",
+        )
+        place_new = [a.T for a in tables[:4]]
+        table_new = tables[4:]
         grad_expand_shift = small[PLACE_ROWS : PLACE_ROWS + 1, :rows]
         grad_entry_shift = small[PLACE_ROWS + 1 : PLACE_ROWS + 3, : entry_bias.shape[2]][:, None, :]
     else:
@@ -906,18 +945,17 @@
         grad_expand_shift = deal(expand_part, 1)
         ends = [deal(entry_part[:, :, first : first + columns], 1) for first in (0, 2 * columns)]
         grad_entry_shift = jnp.stack(ends)
+        exits = adamw(exit_weight, exit_moment, exit_second, attn[:, 3 * columns :].T, 0.05, 0.05)
+        table_new = adamw(vectors, vectors_moment, vectors_second, grad_table, 0.3, 0.0)
+        place_new = adamw(position, position_moment, position_second, grad_place, 0.1, 0.0)
 
     grad_entry = jnp.stack([attn[:, j * columns : (j + 1) * columns] for j in range(3)])
-    grad_exit = attn[:, 3 * columns :].T
 
     entry = adamw(entry_weight, entry_moment, entry_second, grad_entry, 0.05, 0.05)
     entry_b = adamw(entry_bias, entry_bias_moment, entry_bias_second, grad_entry_shift, 0.3, 0.0)
-    exits = adamw(exit_weight, exit_moment, exit_second, grad_exit, 0.05, 0.05)
     expand = adamw(expand_weight, expand_moment, expand_second, expanded, 0.05, 0.05)
     expand_b = adamw(expand_bias, expand_bias_moment, expand_bias_second, grad_expand_shift, 0.3, 0.0)
     reduce_w = adamw(reduce_weight, reduce_moment, reduce_second, reduced, 0.05, 0.05)
-    table_new = adamw(vectors, vectors_moment, vectors_second, grad_table, 0.3, 0.0)
-    place_new = adamw(position, position_moment, position_second, grad_place, 0.1, 0.0)
     return (block_out, patch_grad, *entry, *entry_b, *exits, *expand, *expand_b, *reduce_w, *table_new, *place_new)
 
 

time: 326 us -> 323 us (level); the launches traced: 321 us -> 321 us
  local copies, waits for them, and re-layouts: 46 us -> 39.1 us
  Pallas kernels: 132 us -> 138 us
    unnamed x171 -> x140, local copies, waits for them, and re-layouts: 31 us -> 24.6 us
    pallas_call x13 -> x15, Pallas kernels: 132 us -> 138 us  [kernel_call(): pl.pallas_call(body, out_shape=[a for a, _ in outs], in_specs=[spec for _...]
    ppermute x70 -> x71, starting transfers between devices: 74 us -> 75.2 us  [flip(): return lax.ppermute(array, axis, [(i, i ^ bits) for i in range(count)])]
    ppermute x70 -> x71, waiting for transfers between devices: 24.5 us -> 25.5 us  [flip(): return lax.ppermute(array, axis, [(i, i ^ bits) for i in range(count)])]
    convert_element_type x8 -> x5, other arithmetic: 7.56 us -> 6.73 us  [adamw(): return (master, moment, second, master.astype(jnp.bfloat16))]
  transfers between devices with their start and end apart: 70 -> 71, of which waited for: 10 -> 11; matrix products, arithmetic and copies ran while one was open for 23% -> 20% of each run, Pallas kernels for 40% -> 39%
where the time goes in v4:
time: 323 us; the launch traced here: 321 us
  Pallas kernels  138 us (43%)
  starting transfers between devices  75.2 us (23%)
  other arithmetic  40.7 us (13%)
  local copies, waits for them, and re-layouts  39.1 us (12%)
  waiting for transfers between devices  25.5 us (8%)
    pallas_call x15, Pallas kernels, kernel_call(): pl.pallas_call(body, out_shape=[a for a, _ in outs], in_specs=[spec for _...  138 us
    ppermute x71, starting transfers between devices, flip(): return lax.ppermute(array, axis, [(i, i ^ bits) for i in range(count)])  75.2 us
    ppermute x71, waiting for transfers between devices, flip(): return lax.ppermute(array, axis, [(i, i ^ bits) for i in range(count)])  25.5 us
    unnamed x140, local copies, waits for them, and re-layouts  24.6 us
    convert_element_type x14, other arithmetic, add(): return total.astype(HALF)  15.1 us
    another operation x6, other arithmetic, gather_line(): return (jnp.stack([shard, far]), jnp.stack([near, last]))  7.87 us
    convert_element_type x5, other arithmetic, adamw(): return (master, moment, second, master.astype(jnp.bfloat16))  6.73 us
  transfers between devices with their start and end apart: 71, of which 11 were waited for; matrix products, arithmetic and copies ran while one was open for 20% of the time, Pallas kernels for 39%

profile of v4, /device:TPU:0, one launch (start us, length us, event | category | flops | bytes accessed | tf_op | source)
XLA Modules:
  0.0 321.1 jit_solution(2668157690056222031)
XLA Ops:
  7.0 3.1 collective-permute-start
  10.0 2.6 collective-permute-start.1
  13.5 2.9 collective-permute-start.10
  31.8 2.7 collective-permute-start.16
  36.1 1.9 copy.95.patch_ref
  38.4 2.0 copy.96.cot_ref
  45.5 2.4 collective-permute-done.14
  56.7 8.7 %start.1 = (f32[832,768]{1,0:T(8,128)}, bf16[832,768]{1,0:T(8,128)(2,1)}, bf16[832,768]{1,0:T(8,128)(2,1)}, f32[8,768]{1,0:T(8,128)}, f32[4,1,576]{2,1,0:T(1,128)}, /*index=5*/f32[4,1,768]{2,1,0:T(1,128)}) custom-call(s32[2]{0:T(128)} %pad_add_fusion.place_ref, bf16[8,196,768]{2,1,0:T(8,128)(2,1)} %copy.95.patch_ref, bf16[8,196,768]{2,1,0:T(8,128)(2,1)} %copy.96.cot_ref, ...), custom_call_target="tpu_custom_call" | custom-call | flops 10000000 | bytes 1024 | tf_op jit(solution)/shard_map/start/pallas_call | solution.py:48
  69.0 5.3 %collective-permute-done.19 = bf16[2,96,768]{2,1,0:T(8,128)(2,1)S(1)} collective-permute-done((bf16[2,96,768]{2,1,0:T(8,128)(2,1)S(1)}, bf16[2,96,768]{2,1,0:T(8,128)(2,1)S(1)}, u32[]{:S(2)}, u32[]{:S(2)}) %collective-permute-start.19) | collective-permute-done | bytes 294944 | tf_op jit(solution)/shard_map/ppermute | solution.py:83
  82.3 18.4 %attend.1 = (bf16[832,768]{1,0:T(8,128)(2,1)}, bf16[2,768,768]{2,1,0:T(8,128)(2,1)}, bf16[2,832,576]{2,1,0:T(8,128)(2,1)}, bf16[2,12,208,208]{3,2,1,0:T(8,128)(2,1)}, bf16[2,832,192]{2,1,0:T(8,128)(2,1)}) custom-call(s32[2]{0:T(128)} %pad_add_fusion.place_ref, bf16[832,768]{1,0:T(8,128)(2,1)} %get-tuple-element.151.normed_ref, ...), custom_call_target="tpu_custom_call" | custom-call | flops 16000000 | bytes 1024 | tf_op jit(solution)/shard_map/attend/pallas_call | solution.py:48
  108.1 20.0 %up.1 = (f32[832,768]{1,0:T(8,128)}, bf16[832,768]{1,0:T(8,128)(2,1)}, bf16[2,832,768]{2,1,0:T(8,128)(2,1)}, bf16[2,832,768]{2,1,0:T(8,128)(2,1)}, bf16[2,768,76...) custom-call(s32[2]{0:T(128)} %pad_add_fusion.place_ref, ...), custom_call_target="tpu_custom_call" | custom-call | flops 22000000 | bytes 1024 | tf_op jit(solution)/shard_map/up/pallas_call | solution.py:48
  131.9 14.0 %down.1 = (bf16[2,832,768]{2,1,0:T(8,128)(2,1)}, bf16[832,768]{1,0:T(8,128)(2,1)}, bf16[2,768,768]{2,1,0:T(8,128)(2,1)}, f32[2,8,768]{2,1,0:T(8,128)}) custom-call(s32[2]{0:T(128)} %pad_add_fusion.place_ref, bf16[832,768]{1,0:T(8,128)(2,1)} %get-tuple-element.161.low_ref, bf16[2,832,768]{2,1,0:T(8,128)(2,1)} %get-tuple-element.170.slope_ref, ...), custom_call_target="tpu_custom_call" | custom-call | flops 12000000 | bytes 1024 | tf_op jit(solution)/shard_map/down/pallas_call | solution.py:48
  151.7 6.5 %expand.1 = (bf16[4,96,768]{2,1,0:T(8,128)(2,1)}, bf16[2,96,768]{2,1,0:T(8,128)(2,1)}, bf16[2,96,768]{2,1,0:T(8,128)(2,1)}, bf16[4,96,768]{2,1,0:T(8,128)(2,1)},...) custom-call(s32[2]{0:T(128)} %pad_add_fusion.place_ref, bf16[832,768]{1,0:T(8,128)(2,1)} %get-tuple-element.169.normed_ref, ...), custom_call_target="tpu_custom_call" | custom-call | flops 5000000 | bytes 1024 | tf_op jit(solution)/shard_map/expand/pallas_call | solution.py:48
  158.2 7.4 %output.1 = (f32[416,768]{1,0:T(8,128)}, bf16[416,768]{1,0:T(8,128)(2,1)}) custom-call(s32[2]{0:T(128)} %pad_add_fusion.place_ref, f32[832,768]{1,0:T(8,128)} %get-tuple-element.164.middle_ref, bf16[2,832,768]{2,1,0:T(8,128)(2,1)} %get-tuple-element.176.active_ref, bf16[2,768,768]{2,1,0:T(8,128)(2,1)} %get-tuple-element.177.reduce_ref, ...), custom_call_target="tpu_custom_call" | custom-call | flops 6000000 | bytes 1024 | tf_op jit(solution)/shard_map/output/pallas_call | solution.py:48
  171.1 2.4 collective-permute-start.45
  176.1 8.8 %middle.1 = (f32[832,768]{1,0:T(8,128)}, bf16[832,768]{1,0:T(8,128)(2,1)}, f32[4,8,768]{2,1,0:T(8,128)}) custom-call(bf16[832,768]{1,0:T(8,128)(2,1)} %get-tuple-element.186.normed_grad_ref, bf16[832,768]{1,0:T(8,128)(2,1)} %copy-done.11, f32[832,768]{1,0:T(8,128)} %get-tuple-element.164.middle_ref, bf16[832,768]{1,0:T(8,128)(2,1)} %get-tuple-element.161.low_ref, ...), custom_call_target="tpu_custom_call" | custom-call | flops 8000000 | bytes 1024 | tf_op jit(solution)/shard_map/middle/pallas_call | solution.py:48
  184.9 14.5 %back.2 = (bf16[832,576]{1,0:T(8,128)(2,1)}, f32[8,576]{1,0:T(8,128)}, bf16[4,96,768]{2,1,0:T(8,128)(2,1)}, bf16[2,96,768]{2,1,0:T(8,128)(2,1)}, bf16[2,96,768]{2,1,0:T(8,128)(2,1)}) custom-call(s32[2]{0:T(128)} %pad_add_fusion.place_ref, bf16[832,768]{1,0:T(8,128)(2,1)} %get-tuple-element.208.half_ref, bf16[2,768,768]{2,1,0:T(8,128)(2,1)} %get-tuple-element.215.full_ref, ...), custom_call_target="tpu_custom_call" | custom-call | flops 16000000 | bytes 1024 | tf_op jit(solution)/shard_map/back/pallas_call | solution.py:48
  206.7 4.3 %collective-permute-done.44 = bf16[96,768]{1,0:T(8,128)(2,1)S(1)} collective-permute-done((bf16[96,768]{1,0:T(8,128)(2,1)S(1)}, bf16[96,768]{1,0:T(8,128)(2,1)S(1)}, u32[]{:S(2)}, u32[]{:S(2)}) %collective-permute-start.44) | collective-permute-done | bytes 147488 | tf_op jit(solution)/shard_map/ppermute | solution.py:83
  217.2 14.4 %back.3 = (bf16[832,576]{1,0:T(8,128)(2,1)}, f32[8,576]{1,0:T(8,128)}, bf16[4,96,768]{2,1,0:T(8,128)(2,1)}, bf16[2,96,768]{2,1,0:T(8,128)(2,1)}, bf16[2,96,768]{2,1,0:T(8,128)(2,1)}) custom-call(s32[2]{0:T(128)} %pad_add_fusion.place_ref, bf16[832,768]{1,0:T(8,128)(2,1)} %get-tuple-element.208.half_ref, bf16[2,768,768]{2,1,0:T(8,128)(2,1)} %get-tuple-element.215.full_ref, ...), custom_call_target="tpu_custom_call" | custom-call | flops 16000000 | bytes 1024 | tf_op jit(solution)/shard_map/back/pallas_call | solution.py:48
  239.7 2.6 collective-permute-start.53
  243.9 6.3 %normed.1 = (f32[416,768]{1,0:T(8,128)}, bf16[416,768]{1,0:T(8,128)(2,1)}) custom-call(s32[2]{0:T(128)} %pad_add_fusion.place_ref, bf16[2,768,768]{2,1,0:T(8,128)(2,1)} %get-tuple-element.215.full_ref, bf16[832,576]{1,0:T(8,128)(2,1)} %get-tuple-element.216.rest_0_, bf16[832,576]{1,0:T(8,128)(2,1)} %get-tuple-element.217.rest_1_), custom_call_target="tpu_custom_call" | custom-call | flops 5000000 | bytes 1024 | tf_op jit(solution)/shard_map/normed/pallas_call | solution.py:48
  254.5 2.4 fusion.22
  256.9 3.3 %collective-permute-done.54 = bf16[2,96,768]{2,1,0:T(8,128)(2,1)S(1)} collective-permute-done((bf16[2,96,768]{2,1,0:T(8,128)(2,1)}, bf16[2,96,768]{2,1,0:T(8,128)(2,1)S(1)}, u32[]{:S(2)}, u32[]{:S(2)}) %collective-permute-start.54) | collective-permute-done | bytes 294944 | tf_op jit(solution)/shard_map/ppermute | solution.py:83
  262.2 3.3 %spread.2 = bf16[8,196,768]{2,1,0:T(8,128)(2,1)} custom-call(s32[2]{0:T(128)} %pad_add_fusion.place_ref, bf16[416,768]{1,0:T(8,128)(2,1)} %copy-done.1, bf16[416,768]{1,0:T(8,128)(2,1)} %copy-done.22, bf16[416,768]{1,0:T(8,128)(2,1)} %copy-done.18, bf16[416,768]{1,0:T(8,128)(2,1)} %collective-permute-done.38.far_ref), custom_call_target="tpu_custom_call" | custom-call | flops 3000000 | bytes 1024 | tf_op jit(solution)/shard_map/spread/pallas_call | solution.py:48
  266.9 8.8 %end.1 = (bf16[416,768]{1,0:T(8,128)(2,1)}, bf16[32,80,128]{2,1,0:T(8,128)(2,1)}) custom-call(s32[2]{0:T(128)} %pad_add_fusion.place_ref, f32[416,768]{1,0:T(8,128)} %get-tuple-element.227.keep_ref, bf16[416,768]{1,0:T(8,128)(2,1)} %copy-done.21, f32[832,768]{1,0:T(8,128)} %get-tuple-element.150.start_ref, f32[832,768]{1,0:T(8,128)} %get-tuple-element.229.grad_middle_ref, ...), custom_call_target="tpu_custom_call" | custom-call | flops 8000000 | bytes 1024 | tf_op jit(solution)/shard_map/end/pallas_call | solution.py:48
  287.6 4.2 %collective-permute-start.67 = (bf16[2,80,128]{2,1,0:T(8,128)(2,1)S(1)}, bf16[2,80,128]{2,1,0:T(8,128)(2,1)S(1)}, u32[]{:S(2)}, u32[]{:S(2)}) collective-permute-start(bf16[2,80,128]{2,1,0:T(8,128)(2,1)S(1)} %get-tuple-element.393), channel_id=1, source_target_pairs={{0,16},{4,20},{8,24},{12,28},{16,0},{20,4},{24,8},{28,12},{1,17},{... | collective-permute-start | bytes 122888 | tf_op jit(solution)/shard_map/ppermute | solution.py:83
  291.9 3.0 collective-permute-done.62
  297.2 3.5 %collective-permute-done.68 = bf16[2,80,128]{2,1,0:T(8,128)(2,1)S(1)} collective-permute-done((bf16[2,80,128]{2,1,0:T(8,128)(2,1)S(1)}, bf16[2,80,128]{2,1,0:T(8,128)(2,1)S(1)}, u32[]{:S(2)}, u32[]{:S(2)}) %collective-permute-start.68) | collective-permute-done | bytes 40992 | tf_op jit(solution)/shard_map/ppermute | solution.py:83
  303.2 2.1 fusion.26
  310.4 3.3 %spread.3 = bf16[8,196,768]{2,1,0:T(8,128)(2,1)} custom-call(s32[2]{0:T(128)} %pad_add_fusion.place_ref, bf16[416,768]{1,0:T(8,128)(2,1)} %get-tuple-element.232.own_ref, bf16[416,768]{1,0:T(8,128)(2,1)} %copy-done.20, bf16[416,768]{1,0:T(8,128)(2,1)} %copy-done.19, bf16[416,768]{1,0:T(8,128)(2,1)} %copy-done.23), custom_call_target="tpu_custom_call" | custom-call | flops 3000000 | bytes 1024 | tf_op jit(solution)/shard_map/spread/pallas_call | solution.py:48
  314.8 3.6 %copy.106 = bf16[8,196,768]{2,0,1:T(8,128)(2,1)} copy(bf16[8,196,768]{2,1,0:T(8,128)(2,1)} %spread.3) | data formatting | bytes 4816896
  319.0 2.0 tables.1
  (344 shorter events, 128.1 us)
Async XLA Ops:
  12.6 15.8 %collective-permute-start.9 = (bf16[96,768]{1,0:T(8,128)(2,1)}, bf16[96,768]{1,0:T(8,128)(2,1)S(1)}, u32[]{:S(2)}, u32[]{:S(2)}) collective-permute-start(bf16[96,768]{1,0:T(8,128)(2,1)} %pad_maximum_fusion.9), channel_id=1, source_target_pairs={{0,8},{4,12},{8,0},{12,4},{16,24},{20,28},{24,16},{28,20},{1,9},{5... | collective-permute-start | bytes 442376 | tf_op jit(solution)/shard_map/ppermute | solution.py:83
  13.5 14.9 %collective-permute-start.10 = (bf16[96,768]{1,0:T(8,128)(2,1)}, bf16[96,768]{1,0:T(8,128)(2,1)}, u32[]{:S(2)}, u32[]{:S(2)}) collective-permute-start(bf16[96,768]{1,0:T(8,128)(2,1)} %pad_maximum_fusion.9), channel_id=1, source_target_pairs={{0,24},{4,28},{8,16},{12,20},{16,8},{20,12},{24,0},{28,4},{1,25},{... | collective-permute-start | bytes 442376 | tf_op jit(solution)/shard_map/ppermute | solution.py:83
  26.9 14.4 %collective-permute-start.4 = (bf16[8,80,128]{2,1,0:T(8,128)(2,1)}, bf16[8,80,128]{2,1,0:T(8,128)(2,1)}, u32[]{:S(2)}, u32[]{:S(2)}) collective-permute-start(bf16[8,80,128]{2,1,0:T(8,128)(2,1)} %get-tuple-element.398), channel_id=1, source_target_pairs={{0,2},{1,3},{2,0},{3,1},{4,6},{5,7},{6,4},{7,5},{8,10},{9,11},{10,... | collective-permute-start | bytes 491528 | tf_op jit(solution)/shard_map/ppermute | solution.py:83
  48.8 16.6 %collective-permute-start.22 = (bf16[96,768]{1,0:T(8,128)(2,1)}, bf16[96,768]{1,0:T(8,128)(2,1)}, u32[]{:S(2)}, u32[]{:S(2)}) collective-permute-start(bf16[96,768]{1,0:T(8,128)(2,1)} %convert_bitcast_fusion), channel_id=1, source_target_pairs={{0,8},{4,12},{8,0},{12,4},{16,24},{20,28},{24,16},{28,20},{1,9},{5... | collective-permute-start | bytes 442376 | tf_op jit(solution)/shard_map/ppermute | solution.py:83
  48.9 17.4 %collective-permute-start.23 = (bf16[96,768]{1,0:T(8,128)(2,1)}, bf16[96,768]{1,0:T(8,128)(2,1)}, u32[]{:S(2)}, u32[]{:S(2)}) collective-permute-start(bf16[96,768]{1,0:T(8,128)(2,1)} %convert_bitcast_fusion), channel_id=1, source_target_pairs={{0,24},{4,28},{8,16},{12,20},{16,8},{20,12},{24,0},{28,4},{1,25},{... | collective-permute-start | bytes 442376 | tf_op jit(solution)/shard_map/ppermute | solution.py:83
  50.8 25.9 %collective-permute-start.21 = (bf16[96,768]{1,0:T(8,128)(2,1)}, bf16[96,768]{1,0:T(8,128)(2,1)}, u32[]{:S(2)}, u32[]{:S(2)}) collective-permute-start(bf16[96,768]{1,0:T(8,128)(2,1)} %convert_bitcast_fusion), channel_id=1, source_target_pairs={{0,16},{4,20},{8,24},{12,28},{16,0},{20,4},{24,8},{28,12},{1,17},{... | collective-permute-start | bytes 442376 | tf_op jit(solution)/shard_map/ppermute | solution.py:83
  53.4 25.4 %collective-permute-start.12 = (bf16[4,96,768]{2,1,0:T(8,128)(2,1)S(1)}, bf16[4,96,768]{2,1,0:T(8,128)(2,1)}, u32[]{:S(2)}, u32[]{:S(2)}) collective-permute-start(bf16[4,96,768]{2,1,0:T(8,128)(2,1)S(1)} %pad_maximum_fusion.1.rest_2_), channel_id=1, source_target_pairs={{0,4},{4,0},{8,12},{12,8},{16,20},{20,16},{24,28},{28,24},{1,5},{5... | collective-permute-start | bytes 1769480 | tf_op jit(solution)/shard_map/ppermute | solution.py:83
  54.7 27.6 %collective-permute-start.8 = (bf16[4,96,768]{2,1,0:T(8,128)(2,1)S(1)}, bf16[4,96,768]{2,1,0:T(8,128)(2,1)}, u32[]{:S(2)}, u32[]{:S(2)}) collective-permute-start(bf16[4,96,768]{2,1,0:T(8,128)(2,1)S(1)} %pad_maximum_fusion.rest_0_), channel_id=1, source_target_pairs={{0,2},{1,3},{2,0},{3,1},{4,6},{5,7},{6,4},{7,5},{8,10},{9,11},{10,... | collective-permute-start | bytes 1769480 | tf_op jit(solution)/shard_map/ppermute | solution.py:83
  74.3 29.2 %collective-permute-start.20 = (bf16[4,96,768]{2,1,0:T(8,128)(2,1)S(1)}, bf16[4,96,768]{2,1,0:T(8,128)(2,1)}, u32[]{:S(2)}, u32[]{:S(2)}) collective-permute-start(bf16[4,96,768]{2,1,0:T(8,128)(2,1)S(1)} %constant_dynamic-update-slice_fusion.20.rest_2_), channel_id=1, source_target_pairs={{0,4},{4,0},{8,12},{12,8},{16,20},{20,16},{24,28},{28,24},{1,5},{5... | collective-permute-start | bytes 1769480 | tf_op jit(solution)/shard_map/ppermute | solution.py:83
  75.0 28.6 %collective-permute-start.18 = (bf16[4,96,768]{2,1,0:T(8,128)(2,1)S(1)}, bf16[4,96,768]{2,1,0:T(8,128)(2,1)}, u32[]{:S(2)}, u32[]{:S(2)}) collective-permute-start(bf16[4,96,768]{2,1,0:T(8,128)(2,1)S(1)} %constant_dynamic-update-slice_fusion.18.rest_0_), channel_id=1, source_target_pairs={{0,2},{1,3},{2,0},{3,1},{4,6},{5,7},{6,4},{7,5},{8,10},{9,11},{10,... | collective-permute-start | bytes 1769480 | tf_op jit(solution)/shard_map/ppermute | solution.py:83
  78.4 22.9 %collective-permute-start.25 = (bf16[2,96,768]{2,1,0:T(8,128)(2,1)}, bf16[2,96,768]{2,1,0:T(8,128)(2,1)}, u32[]{:S(2)}, u32[]{:S(2)}) collective-permute-start(bf16[2,96,768]{2,1,0:T(8,128)(2,1)} %pad_maximum_fusion.7), channel_id=1, source_target_pairs={{0,2},{1,3},{2,0},{3,1},{4,6},{5,7},{6,4},{7,5},{8,10},{9,11},{10,... | collective-permute-start | bytes 884744 | tf_op jit(solution)/shard_map/ppermute | solution.py:83
  78.8 23.5 %collective-permute-start.24 = (bf16[2,96,768]{2,1,0:T(8,128)(2,1)}, bf16[2,96,768]{2,1,0:T(8,128)(2,1)}, u32[]{:S(2)}, u32[]{:S(2)}) collective-permute-start(bf16[2,96,768]{2,1,0:T(8,128)(2,1)} %pad_maximum_fusion.6), channel_id=1, source_target_pairs={{0,4},{4,0},{8,12},{12,8},{16,20},{20,16},{24,28},{28,24},{1,5},{5... | collective-permute-start | bytes 884744 | tf_op jit(solution)/shard_map/ppermute | solution.py:83
  104.2 27.8 %collective-permute-start.29 = (bf16[4,96,768]{2,1,0:T(8,128)(2,1)S(1)}, bf16[4,96,768]{2,1,0:T(8,128)(2,1)}, u32[]{:S(2)}, u32[]{:S(2)}) collective-permute-start(bf16[4,96,768]{2,1,0:T(8,128)(2,1)S(1)} %constant_dynamic-update-slice_fusion.22.rest_0_), channel_id=1, source_target_pairs={{0,2},{1,3},{2,0},{3,1},{4,6},{5,7},{6,4},{7,5},{8,10},{9,11},{10,... | collective-permute-start | bytes 1769480 | tf_op jit(solution)/shard_map/ppermute | solution.py:83
  105.8 26.1 %collective-permute-start.30 = (bf16[4,96,768]{2,1,0:T(8,128)(2,1)S(1)}, bf16[4,96,768]{2,1,0:T(8,128)(2,1)}, u32[]{:S(2)}, u32[]{:S(2)}) collective-permute-start(bf16[4,96,768]{2,1,0:T(8,128)(2,1)S(1)} %constant_dynamic-update-slice_fusion.24.rest_2_), channel_id=1, source_target_pairs={{0,4},{4,0},{8,12},{12,8},{16,20},{20,16},{24,28},{28,24},{1,5},{5... | collective-permute-start | bytes 1769480 | tf_op jit(solution)/shard_map/ppermute | solution.py:83
  128.0 18.0 %collective-permute-start.27 = (bf16[4,96,768]{2,1,0:T(8,128)(2,1)}, bf16[4,96,768]{2,1,0:T(8,128)(2,1)S(1)}, u32[]{:S(2)}, u32[]{:S(2)}) collective-permute-start(bf16[4,96,768]{2,1,0:T(8,128)(2,1)} %get-tuple-element.167), channel_id=1, source_target_pairs={{0,2},{1,3},{2,0},{3,1},{4,6},{5,7},{6,4},{7,5},{8,10},{9,11},{10,... | collective-permute-start | bytes 1769480 | tf_op jit(solution)/shard_map/ppermute | solution.py:83
  129.8 16.2 %collective-permute-start.28 = (bf16[2,96,768]{2,1,0:T(8,128)(2,1)}, bf16[2,96,768]{2,1,0:T(8,128)(2,1)}, u32[]{:S(2)}, u32[]{:S(2)}) collective-permute-start(bf16[2,96,768]{2,1,0:T(8,128)(2,1)} %get-tuple-element.168), channel_id=1, source_target_pairs={{0,4},{4,0},{8,12},{12,8},{16,20},{20,16},{24,28},{28,24},{1,5},{5... | collective-permute-start | bytes 884744 | tf_op jit(solution)/shard_map/ppermute | solution.py:83
  130.4 35.3 %collective-permute-start.33 = (bf16[2,96,768]{2,1,0:T(8,128)(2,1)}, bf16[2,96,768]{2,1,0:T(8,128)(2,1)}, u32[]{:S(2)}, u32[]{:S(2)}) collective-permute-start(bf16[2,96,768]{2,1,0:T(8,128)(2,1)} %get-tuple-element.181), channel_id=1, source_target_pairs={{0,4},{4,0},{8,12},{12,8},{16,20},{20,16},{24,28},{28,24},{1,5},{5... | collective-permute-start | bytes 884744 | tf_op jit(solution)/shard_map/ppermute | solution.py:83
  145.9 29.1 %collective-permute-start.36 = (bf16[832,768]{1,0:T(8,128)(2,1)}, bf16[832,768]{1,0:T(8,128)(2,1)S(1)}, u32[]{:S(2)}, u32[]{:S(2)}) collective-permute-start(bf16[832,768]{1,0:T(8,128)(2,1)} %get-tuple-element.186.normed_grad_ref), channel_id=1, source_target_pairs={{0,1},{1,0},{2,3},{3,2},{4,5},{5,4},{6,7},{7,6},{8,9},{9,8},{10,11... | collective-permute-start | bytes 3833864 | tf_op jit(solution)/shard_map/ppermute | solution.py:83
  146.8 20.2 %collective-permute-start.35 = (bf16[2,96,768]{2,1,0:T(8,128)(2,1)}, bf16[2,96,768]{2,1,0:T(8,128)(2,1)}, u32[]{:S(2)}, u32[]{:S(2)}) collective-permute-start(bf16[2,96,768]{2,1,0:T(8,128)(2,1)} %add_convert_fusion.11), channel_id=1, source_target_pairs={{0,4},{4,0},{8,12},{12,8},{16,20},{20,16},{24,28},{28,24},{1,5},{5... | collective-permute-start | bytes 884744 | tf_op jit(solution)/shard_map/ppermute | solution.py:83
  149.1 19.5 %collective-permute-start.34 = (bf16[2,96,768]{2,1,0:T(8,128)(2,1)}, bf16[2,96,768]{2,1,0:T(8,128)(2,1)S(1)}, u32[]{:S(2)}, u32[]{:S(2)}) collective-permute-start(bf16[2,96,768]{2,1,0:T(8,128)(2,1)} %add_convert_fusion.12), channel_id=1, source_target_pairs={{0,2},{1,3},{2,0},{3,1},{4,6},{5,7},{6,4},{7,5},{8,10},{9,11},{10,... | collective-permute-start | bytes 884744 | tf_op jit(solution)/shard_map/ppermute | solution.py:83
  165.7 19.2 %collective-permute-start.40 = (bf16[4,96,768]{2,1,0:T(8,128)(2,1)}, bf16[4,96,768]{2,1,0:T(8,128)(2,1)}, u32[]{:S(2)}, u32[]{:S(2)}) collective-permute-start(bf16[4,96,768]{2,1,0:T(8,128)(2,1)} %get-tuple-element.194), channel_id=1, source_target_pairs={{0,2},{1,3},{2,0},{3,1},{4,6},{5,7},{6,4},{7,5},{8,10},{9,11},{10,... | collective-permute-start | bytes 1769480 | tf_op jit(solution)/shard_map/ppermute | solution.py:83
  167.0 17.8 %collective-permute-start.41 = (bf16[2,96,768]{2,1,0:T(8,128)(2,1)}, bf16[2,96,768]{2,1,0:T(8,128)(2,1)}, u32[]{:S(2)}, u32[]{:S(2)}) collective-permute-start(bf16[2,96,768]{2,1,0:T(8,128)(2,1)} %get-tuple-element.195), channel_id=1, source_target_pairs={{0,4},{4,0},{8,12},{12,8},{16,20},{20,16},{24,28},{28,24},{1,5},{5... | collective-permute-start | bytes 884744 | tf_op jit(solution)/shard_map/ppermute | solution.py:83
  171.1 33.6 %collective-permute-start.45 = (bf16[96,768]{1,0:T(8,128)(2,1)}, bf16[96,768]{1,0:T(8,128)(2,1)S(1)}, u32[]{:S(2)}, u32[]{:S(2)}) collective-permute-start(bf16[96,768]{1,0:T(8,128)(2,1)} %slice_bitcast_fusion.9), channel_id=1, source_target_pairs={{0,16},{4,20},{8,24},{12,28},{16,0},{20,4},{24,8},{28,12},{1,17},{... | collective-permute-start | bytes 442376 | tf_op jit(solution)/shard_map/ppermute | solution.py:83
  211.1 32.7 %collective-permute-start.37 = (bf16[416,768]{1,0:T(8,128)(2,1)S(1)}, bf16[416,768]{1,0:T(8,128)(2,1)S(1)}, u32[]{:S(2)}, u32[]{:S(2)}) collective-permute-start(bf16[416,768]{1,0:T(8,128)(2,1)S(1)} %multiply_convert_fusion.own_ref), channel_id=1, source_target_pairs={{0,2},{1,3},{2,0},{3,1},{4,6},{5,7},{6,4},{7,5},{8,10},{9,11},{10,... | collective-permute-start | bytes 1916936 | tf_op jit(solution)/shard_map/ppermute | solution.py:83
  213.4 28.9 %collective-permute-start.49 = (bf16[4,96,768]{2,1,0:T(8,128)(2,1)}, bf16[4,96,768]{2,1,0:T(8,128)(2,1)}, u32[]{:S(2)}, u32[]{:S(2)}) collective-permute-start(bf16[4,96,768]{2,1,0:T(8,128)(2,1)} %get-tuple-element.213), channel_id=1, source_target_pairs={{0,2},{1,3},{2,0},{3,1},{4,6},{5,7},{6,4},{7,5},{8,10},{9,11},{10,... | collective-permute-start | bytes 1769480 | tf_op jit(solution)/shard_map/ppermute | solution.py:83
  215.1 21.9 %collective-permute-start.50 = (bf16[2,96,768]{2,1,0:T(8,128)(2,1)}, bf16[2,96,768]{2,1,0:T(8,128)(2,1)}, u32[]{:S(2)}, u32[]{:S(2)}) collective-permute-start(bf16[2,96,768]{2,1,0:T(8,128)(2,1)} %get-tuple-element.214), channel_id=1, source_target_pairs={{0,4},{4,0},{8,12},{12,8},{16,20},{20,16},{24,28},{28,24},{1,5},{5... | collective-permute-start | bytes 884744 | tf_op jit(solution)/shard_map/ppermute | solution.py:83
  234.3 15.9 %collective-permute-start.52 = (bf16[96,768]{1,0:T(8,128)(2,1)}, bf16[96,768]{1,0:T(8,128)(2,1)}, u32[]{:S(2)}, u32[]{:S(2)}) collective-permute-start(bf16[96,768]{1,0:T(8,128)(2,1)} %slice_bitcast_fusion.5), channel_id=1, source_target_pairs={{0,16},{4,20},{8,24},{12,28},{16,0},{20,4},{24,8},{28,12},{1,17},{... | collective-permute-start | bytes 442376 | tf_op jit(solution)/shard_map/ppermute | solution.py:83
  237.0 14.1 %collective-permute-start.51 = (bf16[96,768]{1,0:T(8,128)(2,1)}, bf16[96,768]{1,0:T(8,128)(2,1)}, u32[]{:S(2)}, u32[]{:S(2)}) collective-permute-start(bf16[96,768]{1,0:T(8,128)(2,1)} %get-tuple-element.385), channel_id=1, source_target_pairs={{0,8},{4,12},{8,0},{12,4},{16,24},{20,28},{24,16},{28,20},{1,9},{5... | collective-permute-start | bytes 442376 | tf_op jit(solution)/shard_map/ppermute | solution.py:83
  243.8 17.5 %collective-permute-start.32 = (bf16[416,768]{1,0:T(8,128)(2,1)S(1)}, bf16[416,768]{1,0:T(8,128)(2,1)S(1)}, u32[]{:S(2)}, u32[]{:S(2)}) collective-permute-start(bf16[416,768]{1,0:T(8,128)(2,1)S(1)} %multiply_convert_fusion.own_ref), channel_id=1, source_target_pairs={{0,1},{1,0},{2,3},{3,2},{4,5},{5,4},{6,7},{7,6},{8,9},{9,8},{10,11... | collective-permute-start | bytes 1916936 | tf_op jit(solution)/shard_map/ppermute | solution.py:83
  251.1 14.9 %collective-permute-start.57 = (bf16[416,768]{1,0:T(8,128)(2,1)}, bf16[416,768]{1,0:T(8,128)(2,1)S(1)}, u32[]{:S(2)}, u32[]{:S(2)}) collective-permute-start(bf16[416,768]{1,0:T(8,128)(2,1)} %get-tuple-element.228), channel_id=1, source_target_pairs={{0,1},{1,0},{2,3},{3,2},{4,5},{5,4},{6,7},{7,6},{8,9},{9,8},{10,11... | collective-permute-start | bytes 1916936 | tf_op jit(solution)/shard_map/ppermute | solution.py:83
  284.9 15.8 %collective-permute-start.59 = (bf16[416,768]{1,0:T(8,128)(2,1)S(1)}, bf16[416,768]{1,0:T(8,128)(2,1)S(1)}, u32[]{:S(2)}, u32[]{:S(2)}) collective-permute-start(bf16[416,768]{1,0:T(8,128)(2,1)S(1)} %copy-done.17), channel_id=1, source_target_pairs={{0,2},{1,3},{2,0},{3,1},{4,6},{5,7},{6,4},{7,5},{8,10},{9,11},{10,... | collective-permute-start | bytes 1916936 | tf_op jit(solution)/shard_map/ppermute | solution.py:83
  286.3 22.4 %collective-permute-start.58 = (bf16[416,768]{1,0:T(8,128)(2,1)S(1)}, bf16[416,768]{1,0:T(8,128)(2,1)S(1)}, u32[]{:S(2)}, u32[]{:S(2)}) collective-permute-start(bf16[416,768]{1,0:T(8,128)(2,1)S(1)} %copy-done.17), channel_id=1, source_target_pairs={{0,1},{1,0},{2,3},{3,2},{4,5},{5,4},{6,7},{7,6},{8,9},{9,8},{10,11... | collective-permute-start | bytes 1916936 | tf_op jit(solution)/shard_map/ppermute | solution.py:83
  (101 other events, 984.7 us)
